TPU v7x, 32 devices: a whole 2x2x4 slice. The times are simulated.
32 devices in a mesh: members: 2 (over y), lon: 8 (over z, x), lev: 2 (over core).
Axes of the slice: x: 2, y: 2, z: 4, core: 2. Of those that a mesh axis runs over, the one named last changes fastest.
Arguments:
- velocity: bfloat16 [2, 4, 32, 1024], P(None, ('members', 'lev'), None, 'lon'), parts along dimension 1, may hold values from -3 to 3
- land_sea: int32 [4, 32, 1024], P(('members', 'lev'), None, 'lon'), parts along dimension 0, may hold values 0 or 1
- fold_pivot: int32 [2], replicated, may hold values from 1022 to 1024, as said below
- weight_one: bfloat16 [5, 5, 2, 128], replicated, may hold values from -1.25 to 1.25
- bias_one: float32 [128], replicated, may hold values from -2 to 2
- weight_two: bfloat16 [5, 5, 128, 64], replicated, may hold values from -0.15625 to 0.15625
- bias_two: float32 [64], replicated, may hold values from -2 to 2
- weight_three: bfloat16 [3, 3, 64, 32], replicated, may hold values from -0.375 to 0.375
- bias_three: float32 [32], replicated, may hold values from -2 to 2
- weight_four: bfloat16 [3, 3, 32, 2], replicated, may hold values from -1 to 1
- bias_four: float32 [2], replicated, may hold values from -2 to 2
Outputs:
- updated: bfloat16 [2, 4, 32, 1024], P(None, ('members', 'lev'), None, 'lon'), parts along dimension 1
There are 2 independent parts, one for each index of `members`. A program takes and returns all parts, laid end to end along the dimension named above; an argument that names none is the same for every part. Nothing has to cross between parts.
Inputs may be any that keep to these rules, and one draw needn't show every extreme that they name: `fold_pivot`: one entry is 1022 and the other 1024, in either order.
All inputs are finite; a program needn't handle non-finite values. No bound on the sum of `land_sea` on one device may be relied on, other than what follows from the above.
Results may differ from a plain program's by a relative error of at most 0.005.
The roundings to bfloat16 on the way count: a program that leaves them out, or rounds other values in their place, can miss the bound.
Values may be sent and summed in bfloat16 or wider, within the bound.
No kernel may reach another device: no remote copies, remote signals or barrier semaphores. Data moves between devices by JAX's collectives and lax.ppermute only.
A program may use at most 64 MiB of HBM per device.

v0:
```python
import jax
import jax.numpy as jnp
from jax import lax
from jax.sharding import PartitionSpec as P


def with_halo(x, sides, width):
    for axis, dim in sides:
        size, length = (lax.axis_size(axis), x.shape[dim])
        up = [(i, (i + 1) % size) for i in range(size)]
        down = [(j, i) for i, j in up]
        last = lax.slice_in_dim(x, length - width, length, axis=dim)
        leading = lax.slice_in_dim(x, 0, width, axis=dim)
        before = lax.ppermute(last, axis, up)
        after = lax.ppermute(leading, axis, down)
        x = jnp.concatenate([before, x, after], axis=dim)
    return x


def partner(x, axis, apart):
    return lax.ppermute(x, axis, [(i, i ^ 1 << apart) for i in range(lax.axis_size(axis))])


def convolve(field_data, weight, bias_term):
    kernel = weight.shape[0]
    in_channels = weight.shape[2]
    out_channels = weight.shape[3]
    out_rows = field_data.shape[2] - kernel + 1
    out_cols = field_data.shape[3] - kernel + 1
    if kernel * kernel * in_channels <= 64:
        stacked = jnp.concatenate(
            [
                field_data[:, :, row_shift : row_shift + out_rows, col_shift : col_shift + out_cols]
                for row_shift in range(kernel)
                for col_shift in range(kernel)
            ],
            axis=0,
        )
        flat_weight = weight.reshape(kernel * kernel * in_channels, out_channels)
        result = jnp.einsum(
            "ko,kvrl->ovrl", flat_weight, stacked, preferred_element_type=jnp.float32
        )
    else:
        result = jnp.zeros((out_channels, field_data.shape[1], out_rows, out_cols), jnp.float32)
        for row_shift in range(kernel):
            for col_shift in range(kernel):
                window = field_data[
                    :, :, row_shift : row_shift + out_rows, col_shift : col_shift + out_cols
                ]
                result = result + jnp.einsum(
                    "co,cvrl->ovrl",
                    weight[row_shift, col_shift],
                    window,
                    preferred_element_type=jnp.float32,
                )
    return result + bias_term[:, None, None, None]


def widen_cols(field_data, reach):
    return with_halo(field_data, (("lon", 3),), reach)


def shards(
    velocity,
    land_sea,
    fold_pivot,
    weight_one,
    bias_one,
    weight_two,
    bias_two,
    weight_three,
    bias_three,
    weight_four,
    bias_four,
):
    row_count = velocity.shape[2]
    lon_dev = velocity.shape[3]
    lon_count = lax.axis_size("lon")
    masked = velocity * land_sea.astype(jnp.bfloat16)[None]
    reaches = (2, 1, 1)
    halo_width = 2
    edge_cols = halo_width + 1
    widened = with_halo(masked, (("lon", 3),), edge_cols)
    span_cols = lon_dev + 2 * halo_width
    main_rows = widened[:, :, :, edge_cols - halo_width : edge_cols - halo_width + span_cols]
    offset = fold_pivot - (lon_count * lon_dev - 1)
    top_rows = widened[:, :, row_count - 7 : row_count - 1, :]
    for bit_index in range(lon_count.bit_length() - 1):
        top_rows = partner(top_rows, "lon", bit_index)
    turned = top_rows[:, :, ::-1, ::-1]
    fold_field = jnp.stack(
        [
            lax.dynamic_slice_in_dim(turned[component], 1 - offset[component], span_cols, 2)
            for component in range(2)
        ]
    )
    south_rows = jnp.zeros((2, masked.shape[1], 6, span_cols), jnp.bfloat16)
    extended = jnp.concatenate([south_rows, main_rows, -fold_field], axis=2)
    hidden = jnp.maximum(convolve(extended, weight_one, bias_one), 0.0).astype(jnp.bfloat16)
    hidden = widen_cols(hidden, reaches[0])
    hidden = jnp.maximum(convolve(hidden, weight_two, bias_two), 0.0).astype(jnp.bfloat16)
    hidden = widen_cols(hidden, reaches[1])
    hidden = jnp.maximum(convolve(hidden, weight_three, bias_three), 0.0).astype(jnp.bfloat16)
    hidden = widen_cols(hidden, reaches[2])
    tendency = convolve(hidden, weight_four, bias_four)
    result = land_sea.astype(jnp.float32)[None] * (velocity.astype(jnp.float32) + tendency)
    return result.astype(jnp.bfloat16)


def solution(mesh):
    in_specs = (
        P(None, ("members", "lev"), None, "lon"),
        P(("members", "lev"), None, "lon"),
        P(),
        P(),
        P(),
        P(),
        P(),
        P(),
        P(),
        P(),
        P(),
    )
    out_specs = P(None, ("members", "lev"), None, "lon")
    return jax.shard_map(shards, mesh=mesh, in_specs=in_specs, out_specs=out_specs, check_vma=False)
```

profile of v0, /device:TPU:0, one launch (start us, length us, event | category | flops | bytes accessed | tf_op | source)
XLA Modules:
  0.0 70.7 jit_solution(16445853666446446630)
XLA Ops:
  0.0 0.8 %convert_bitcast_fusion = (f32[32,128]{1,0:T(8,128)S(1)}, bf16[32,128]{1,0:T(8,128)(2,1)S(1)}) fusion(s32[1,32,128]{2,1,0:T(8,128)} %param.12), kind=kLoop, calls=%fused_computation.291 | loop fusion | flops 8192 | bytes 40960 | tf_op jit(solution)/shard_map/mul | solution.py:106
  0.8 0.7 %copy_multiply_fusion = bf16[2,1,32,128]{3,0,2,1:T(2,128)(2,1)S(1)} fusion(bf16[2,1,32,128]{3,2,1,0:T(8,128)(2,1)} %param.11, bf16[32,128]{1,0:T(8,128)(2,1)S(1)} %get-tuple-element.37), kind=kLoop, calls=%fused_computation.265 | loop fusion | flops 8192 | bytes 40960 | tf_op jit(solution)/shard_map/mul | solution.py:79
  1.6 3.0 %collective-permute-start = (bf16[2,1,32,3]{3,0,2,1:T(2,128)(2,1)S(1)}, bf16[2,1,32,3]{3,0,2,1:T(2,128)(2,1)S(1)}, u32[]{:S(2)}, u32[]{:S(2)}) collective-permute-start(bf16[2,1,32,3]{3,0,2,1:T(2,128)(2,1)S(1)} %get-tuple-element.38), channel_id=1, source_target_pairs={{0,2},{2,4},{4,6},{6,8},{8,10},{10,12},{12,14},{14,0},{1,3},{3,5},... | collective-permute-start | bytes 1160 | tf_op jit(solution)/shard_map/ppermute | solution.py:14
  4.7 3.1 %collective-permute-start.1 = (bf16[2,1,32,3]{3,0,2,1:T(2,128)(2,1)S(1)}, bf16[2,1,32,3]{3,0,2,1:T(2,128)(2,1)S(1)}, u32[]{:S(2)}, u32[]{:S(2)}) collective-permute-start(bf16[2,1,32,3]{3,0,2,1:T(2,128)(2,1)S(1)} %get-tuple-element.39), channel_id=1, source_target_pairs={{2,0},{4,2},{6,4},{8,6},{10,8},{12,10},{14,12},{0,14},{3,1},{5,3},... | collective-permute-start | bytes 1160 | tf_op jit(solution)/shard_map/ppermute | solution.py:15
  7.8 1.7 %collective-permute-done = bf16[2,1,32,3]{3,0,2,1:T(2,128)(2,1)S(1)} collective-permute-done((bf16[2,1,32,3]{3,0,2,1:T(2,128)(2,1)S(1)}, bf16[2,1,32,3]{3,0,2,1:T(2,128)(2,1)S(1)}, u32[]{:S(2)}, u32[]{:S(2)}) %collective-permute-start) | collective-permute-done | bytes 416 | tf_op jit(solution)/shard_map/ppermute | solution.py:14
  9.5 1.5 %collective-permute-start.2 = (bf16[2,1,6,134]{3,0,2,1:T(2,128)(2,1)S(1)}, bf16[2,1,6,134]{3,0,2,1:T(2,128)(2,1)S(1)}, u32[]{:S(2)}, u32[]{:S(2)}) collective-permute-start(bf16[2,1,6,134]{3,0,2,1:T(2,128)(2,1)S(1)} %pad_maximum_fusion.8), channel_id=1, source_target_pairs={{0,2},{2,0},{4,6},{6,4},{8,10},{10,8},{12,14},{14,12},{1,3},{3,1},... | collective-permute-start | bytes 9656 | tf_op jit(solution)/shard_map/ppermute | solution.py:21
  11.0 0.7 broadcast_add_fusion
  11.7 1.5 %collective-permute-done.2 = bf16[2,1,6,134]{3,0,2,1:T(2,128)(2,1)S(1)} collective-permute-done((bf16[2,1,6,134]{3,0,2,1:T(2,128)(2,1)S(1)}, bf16[2,1,6,134]{3,0,2,1:T(2,128)(2,1)S(1)}, u32[]{:S(2)}, u32[]{:S(2)}) %collective-permute-start.2) | collective-permute-done | bytes 3248 | tf_op jit(solution)/shard_map/ppermute | solution.py:21
  13.2 1.0 %collective-permute-start.3 = (bf16[2,1,6,134]{3,0,2,1:T(2,128)(2,1)S(1)}, bf16[2,1,6,134]{3,0,2,1:T(2,128)(2,1)S(1)}, u32[]{:S(2)}, u32[]{:S(2)}) collective-permute-start(bf16[2,1,6,134]{3,0,2,1:T(2,128)(2,1)S(1)} %collective-permute-done.2), channel_id=1, source_target_pairs={{0,4},{2,6},{4,0},{6,2},{8,12},{10,14},{12,8},{14,10},{1,5},{3,7},... | collective-permute-start | bytes 9656 | tf_op jit(solution)/shard_map/ppermute | solution.py:21
  14.2 0.7 fusion.314
  17.5 0.7 %reshape.332 = bf16[50,128,1]{1,0,2:T(8,128)(2,1)S(1)} reshape(bf16[5,5,2,128]{3,2,1,0:T(2,128)(2,1)} %param.14) | data formatting | bytes 25600 | tf_op jit(solution)/shard_map/reshape | solution.py:39
  18.3 3.0 %collective-permute-start.4 = (bf16[2,1,6,134]{3,0,2,1:T(2,128)(2,1)S(1)}, bf16[2,1,6,134]{3,0,2,1:T(2,128)(2,1)S(1)}, u32[]{:S(2)}, u32[]{:S(2)}) collective-permute-start(bf16[2,1,6,134]{3,0,2,1:T(2,128)(2,1)S(1)} %collective-permute-done.3), channel_id=1, source_target_pairs={{0,8},{2,10},{4,12},{6,14},{8,0},{10,2},{12,4},{14,6},{1,9},{3,11}... | collective-permute-start | bytes 9656 | tf_op jit(solution)/shard_map/ppermute | solution.py:21
  21.5 1.4 %collective-permute-done.4 = bf16[2,1,6,134]{3,0,2,1:T(2,128)(2,1)S(1)} collective-permute-done((bf16[2,1,6,134]{3,0,2,1:T(2,128)(2,1)S(1)}, bf16[2,1,6,134]{3,0,2,1:T(2,128)(2,1)S(1)}, u32[]{:S(2)}, u32[]{:S(2)}) %collective-permute-start.4) | collective-permute-done | bytes 3248 | tf_op jit(solution)/shard_map/ppermute | solution.py:21
  24.4 0.9 %concatenate.66 = bf16[50,1,40,128]{3,0,2,1:T(8,128)(2,1)S(1)} concatenate(bf16[2,1,40,128]{3,0,2,1:T(2,128)(2,1)S(1)} %get-tuple-element.35, bf16[2,1,40,128]{3,0,2,1:T(2,128)(2,1)S(1)} %get-tuple-element.34, bf16[2,1,40,128]{3,0,2,1:T(2,128)(2,1)S(1)} %get-tuple-element.33, bf16[2,1,40,128]{3,0,2,1:T(2,128)(2,1)S(1)} %get-tuple-element.32, ...), dimensions={0} | concatenate | bytes 1024000 | tf_op jit(solution)/shard_map/concatenate | solution.py:31
  25.3 0.6 fusion
  26.8 0.5 fusion.112
  27.9 2.1 %collective-permute-start.5 = (bf16[128,1,40,2]{0,3,2,1:T(2,128)(2,1)S(1)}, bf16[128,1,40,2]{0,3,2,1:T(2,128)(2,1)S(1)}, u32[]{:S(2)}, u32[]{:S(2)}) collective-permute-start(bf16[128,1,40,2]{0,3,2,1:T(2,128)(2,1)S(1)} %get-tuple-element.5), channel_id=1, source_target_pairs={{0,2},{2,4},{4,6},{6,8},{8,10},{10,12},{12,14},{14,0},{1,3},{3,5},... | collective-permute-start | bytes 61448 | tf_op jit(solution)/shard_map/ppermute | solution.py:14
  29.9 0.5 convolution_bitcast_fusion.2
  30.5 2.9 %collective-permute-start.6 = (bf16[128,1,40,2]{0,3,2,1:T(2,128)(2,1)S(1)}, bf16[128,1,40,2]{0,3,2,1:T(2,128)(2,1)S(1)}, u32[]{:S(2)}, u32[]{:S(2)}) collective-permute-start(bf16[128,1,40,2]{0,3,2,1:T(2,128)(2,1)S(1)} %get-tuple-element.6), channel_id=1, source_target_pairs={{2,0},{4,2},{6,4},{8,6},{10,8},{12,10},{14,12},{0,14},{3,1},{5,3},... | collective-permute-start | bytes 61448 | tf_op jit(solution)/shard_map/ppermute | solution.py:15
  33.4 1.0 %collective-permute-done.5 = bf16[128,1,40,2]{0,3,2,1:T(2,128)(2,1)S(1)} collective-permute-done((bf16[128,1,40,2]{0,3,2,1:T(2,128)(2,1)S(1)}, bf16[128,1,40,2]{0,3,2,1:T(2,128)(2,1)S(1)}, u32[]{:S(2)}, u32[]{:S(2)}) %collective-permute-start.5) | collective-permute-done | bytes 20512 | tf_op jit(solution)/shard_map/ppermute | solution.py:14
  34.4 0.5 fusion.67
  34.9 0.5 fusion.71
  35.5 0.6 fusion.75
  36.0 0.5 fusion.37
  36.6 0.5 fusion.44
  37.1 0.5 fusion.79
  37.7 0.6 fusion.83
  38.2 0.5 fusion.51
  38.8 0.5 fusion.87
  39.3 0.6 fusion.91
  39.9 0.6 fusion.23
  40.5 0.7 fusion.22
  41.2 0.7 fusion.18
  41.9 0.6 fusion.14
  42.5 0.5 fusion.1
  43.0 0.6 convolution_bitcast_fusion.3
  43.6 0.5 convolution_bitcast_fusion.4
  44.1 0.5 convolution_bitcast_fusion.5
  44.7 0.5 convolution_bitcast_fusion.1
  45.3 0.5 convolution_bitcast_fusion
  45.9 0.9 %fusion.25 = bf16[64,1,36,128]{3,0,2,1:T(8,128)(2,1)S(1)} fusion(f32[64,36,128]{2,0,1:T(8,128)S(1)} %convolution_bitcast_fusion, f32[64,36,128]{2,0,1:T(8,128)S(1)} %convolution_bitcast_fusion.1, f32[64,36,128]{2,0,1:T(8,128)S(1)} %convolution_bitcast_fusion.2, f32[64,36,128]{2,0,1:T(8,128)S(1)} %convolution_bitcast_fusion.3, ...), kind=kOutput, calls=%fused_computation.64 | convolution fusion | flops 80805888 | bytes 10195456 | tf_op jit(solution)/shard_map/co,cvrl->ovrl/dot_general | solution.py:50
  48.3 4.7 %collective-permute-start.8 = (bf16[64,1,36,1]{0,2,3,1:T(8,128)(2,1)S(1)}, bf16[64,1,36,1]{0,2,3,1:T(8,128)(2,1)S(1)}, u32[]{:S(2)}, u32[]{:S(2)}) collective-permute-start(bf16[64,1,36,1]{0,2,3,1:T(8,128)(2,1)S(1)} %copy.100), channel_id=1, source_target_pairs={{2,0},{4,2},{6,4},{8,6},{10,8},{12,10},{14,12},{0,14},{3,1},{5,3},... | collective-permute-start | bytes 13832 | tf_op jit(solution)/shard_map/ppermute | solution.py:15
  53.0 0.9 %collective-permute-done.7 = bf16[64,1,36,1]{0,2,3,1:T(8,128)(2,1)S(1)} collective-permute-done((bf16[64,1,36,1]{0,2,3,1:T(8,128)(2,1)S(1)}, bf16[64,1,36,1]{0,2,3,1:T(8,128)(2,1)S(1)}, u32[]{:S(2)}, u32[]{:S(2)}) %collective-permute-start.7) | collective-permute-done | bytes 4640 | tf_op jit(solution)/shard_map/ppermute | solution.py:14
  55.1 0.5 convolution_add_fusion.10
  57.9 0.6 fusion.120
  59.1 4.8 %collective-permute-start.10 = (bf16[32,1,34,1]{3,0,2,1:T(8,128)(2,1)S(1)}, bf16[32,1,34,1]{3,0,2,1:T(8,128)(2,1)S(1)}, u32[]{:S(2)}, u32[]{:S(2)}) collective-permute-start(bf16[32,1,34,1]{3,0,2,1:T(8,128)(2,1)S(1)} %get-tuple-element.10), channel_id=1, source_target_pairs={{2,0},{4,2},{6,4},{8,6},{10,8},{12,10},{14,12},{0,14},{3,1},{5,3},... | collective-permute-start | bytes 6536 | tf_op jit(solution)/shard_map/ppermute | solution.py:15
  63.9 4.4 %collective-permute-done.9 = bf16[32,1,34,1]{3,0,2,1:T(8,128)(2,1)S(1)} collective-permute-done((bf16[32,1,34,1]{3,0,2,1:T(8,128)(2,1)S(1)}, bf16[32,1,34,1]{3,0,2,1:T(8,128)(2,1)S(1)}, u32[]{:S(2)}, u32[]{:S(2)}) %collective-permute-start.9) | collective-permute-done | bytes 2208 | tf_op jit(solution)/shard_map/ppermute | solution.py:14
  70.1 0.7 fusion.187
  (64 shorter events, 10.6 us)
Async XLA Ops:
  1.6 7.8 %collective-permute-start = (bf16[2,1,32,3]{3,0,2,1:T(2,128)(2,1)S(1)}, bf16[2,1,32,3]{3,0,2,1:T(2,128)(2,1)S(1)}, u32[]{:S(2)}, u32[]{:S(2)}) collective-permute-start(bf16[2,1,32,3]{3,0,2,1:T(2,128)(2,1)S(1)} %get-tuple-element.38), channel_id=1, source_target_pairs={{0,2},{2,4},{4,6},{6,8},{8,10},{10,12},{12,14},{14,0},{1,3},{3,5},... | collective-permute-start | bytes 1160 | tf_op jit(solution)/shard_map/ppermute | solution.py:14
  4.7 4.8 %collective-permute-start.1 = (bf16[2,1,32,3]{3,0,2,1:T(2,128)(2,1)S(1)}, bf16[2,1,32,3]{3,0,2,1:T(2,128)(2,1)S(1)}, u32[]{:S(2)}, u32[]{:S(2)}) collective-permute-start(bf16[2,1,32,3]{3,0,2,1:T(2,128)(2,1)S(1)} %get-tuple-element.39), channel_id=1, source_target_pairs={{2,0},{4,2},{6,4},{8,6},{10,8},{12,10},{14,12},{0,14},{3,1},{5,3},... | collective-permute-start | bytes 1160 | tf_op jit(solution)/shard_map/ppermute | solution.py:15
  9.5 3.7 %collective-permute-start.2 = (bf16[2,1,6,134]{3,0,2,1:T(2,128)(2,1)S(1)}, bf16[2,1,6,134]{3,0,2,1:T(2,128)(2,1)S(1)}, u32[]{:S(2)}, u32[]{:S(2)}) collective-permute-start(bf16[2,1,6,134]{3,0,2,1:T(2,128)(2,1)S(1)} %pad_maximum_fusion.8), channel_id=1, source_target_pairs={{0,2},{2,0},{4,6},{6,4},{8,10},{10,8},{12,14},{14,12},{1,3},{3,1},... | collective-permute-start | bytes 9656 | tf_op jit(solution)/shard_map/ppermute | solution.py:21
  13.2 5.1 %collective-permute-start.3 = (bf16[2,1,6,134]{3,0,2,1:T(2,128)(2,1)S(1)}, bf16[2,1,6,134]{3,0,2,1:T(2,128)(2,1)S(1)}, u32[]{:S(2)}, u32[]{:S(2)}) collective-permute-start(bf16[2,1,6,134]{3,0,2,1:T(2,128)(2,1)S(1)} %collective-permute-done.2), channel_id=1, source_target_pairs={{0,4},{2,6},{4,0},{6,2},{8,12},{10,14},{12,8},{14,10},{1,5},{3,7},... | collective-permute-start | bytes 9656 | tf_op jit(solution)/shard_map/ppermute | solution.py:21
  18.3 4.6 %collective-permute-start.4 = (bf16[2,1,6,134]{3,0,2,1:T(2,128)(2,1)S(1)}, bf16[2,1,6,134]{3,0,2,1:T(2,128)(2,1)S(1)}, u32[]{:S(2)}, u32[]{:S(2)}) collective-permute-start(bf16[2,1,6,134]{3,0,2,1:T(2,128)(2,1)S(1)} %collective-permute-done.3), channel_id=1, source_target_pairs={{0,8},{2,10},{4,12},{6,14},{8,0},{10,2},{12,4},{14,6},{1,9},{3,11}... | collective-permute-start | bytes 9656 | tf_op jit(solution)/shard_map/ppermute | solution.py:21
  22.9 2.3 %copy-start.3 = (f32[128]{0:T(128)S(1)}, f32[128]{0:T(128)}, u32[]{:S(2)}) copy-start(f32[128]{0:T(128)} %param.15) | copy-start | bytes 1540
  25.3 1.0 %copy-start = (bf16[5,5,128,64]{2,3,1,0:T(8,128)(2,1)S(1)}, bf16[5,5,128,64]{2,3,1,0:T(8,128)(2,1)}, u32[]{:S(2)}) copy-start(bf16[5,5,128,64]{2,3,1,0:T(8,128)(2,1)} %param.16) | copy-start | bytes 1228804
  27.9 6.5 %collective-permute-start.5 = (bf16[128,1,40,2]{0,3,2,1:T(2,128)(2,1)S(1)}, bf16[128,1,40,2]{0,3,2,1:T(2,128)(2,1)S(1)}, u32[]{:S(2)}, u32[]{:S(2)}) collective-permute-start(bf16[128,1,40,2]{0,3,2,1:T(2,128)(2,1)S(1)} %get-tuple-element.5), channel_id=1, source_target_pairs={{0,2},{2,4},{4,6},{6,8},{8,10},{10,12},{12,14},{14,0},{1,3},{3,5},... | collective-permute-start | bytes 61448 | tf_op jit(solution)/shard_map/ppermute | solution.py:14
  30.5 5.6 %collective-permute-start.6 = (bf16[128,1,40,2]{0,3,2,1:T(2,128)(2,1)S(1)}, bf16[128,1,40,2]{0,3,2,1:T(2,128)(2,1)S(1)}, u32[]{:S(2)}, u32[]{:S(2)}) collective-permute-start(bf16[128,1,40,2]{0,3,2,1:T(2,128)(2,1)S(1)} %get-tuple-element.6), channel_id=1, source_target_pairs={{2,0},{4,2},{6,4},{8,6},{10,8},{12,10},{14,12},{0,14},{3,1},{5,3},... | collective-permute-start | bytes 61448 | tf_op jit(solution)/shard_map/ppermute | solution.py:15
  45.2 0.7 copy-start.4
  46.8 0.9 %copy-start.1 = (bf16[3,3,64,32]{2,3,1,0:T(8,128)(2,1)S(1)}, bf16[3,3,64,32]{2,3,1,0:T(8,128)(2,1)}, u32[]{:S(2)}) copy-start(bf16[3,3,64,32]{2,3,1,0:T(8,128)(2,1)} %param.18) | copy-start | bytes 110596
  47.5 6.4 %collective-permute-start.7 = (bf16[64,1,36,1]{0,2,3,1:T(8,128)(2,1)S(1)}, bf16[64,1,36,1]{0,2,3,1:T(8,128)(2,1)S(1)}, u32[]{:S(2)}, u32[]{:S(2)}) collective-permute-start(bf16[64,1,36,1]{0,2,3,1:T(8,128)(2,1)S(1)} %copy.98), channel_id=1, source_target_pairs={{0,2},{2,4},{4,6},{6,8},{8,10},{10,12},{12,14},{14,0},{1,3},{3,5},... | collective-permute-start | bytes 13832 | tf_op jit(solution)/shard_map/ppermute | solution.py:14
  48.3 6.4 %collective-permute-start.8 = (bf16[64,1,36,1]{0,2,3,1:T(8,128)(2,1)S(1)}, bf16[64,1,36,1]{0,2,3,1:T(8,128)(2,1)S(1)}, u32[]{:S(2)}, u32[]{:S(2)}) collective-permute-start(bf16[64,1,36,1]{0,2,3,1:T(8,128)(2,1)S(1)} %copy.100), channel_id=1, source_target_pairs={{2,0},{4,2},{6,4},{8,6},{10,8},{12,10},{14,12},{0,14},{3,1},{5,3},... | collective-permute-start | bytes 13832 | tf_op jit(solution)/shard_map/ppermute | solution.py:15
  57.2 0.7 copy-start.5
  57.9 0.7 copy-start.7
  58.9 9.4 %collective-permute-start.9 = (bf16[32,1,34,1]{3,0,2,1:T(8,128)(2,1)S(1)}, bf16[32,1,34,1]{3,0,2,1:T(8,128)(2,1)S(1)}, u32[]{:S(2)}, u32[]{:S(2)}) collective-permute-start(bf16[32,1,34,1]{3,0,2,1:T(8,128)(2,1)S(1)} %get-tuple-element.9), channel_id=1, source_target_pairs={{0,2},{2,4},{4,6},{6,8},{8,10},{10,12},{12,14},{14,0},{1,3},{3,5},... | collective-permute-start | bytes 6536 | tf_op jit(solution)/shard_map/ppermute | solution.py:14
  59.1 9.7 %collective-permute-start.10 = (bf16[32,1,34,1]{3,0,2,1:T(8,128)(2,1)S(1)}, bf16[32,1,34,1]{3,0,2,1:T(8,128)(2,1)S(1)}, u32[]{:S(2)}, u32[]{:S(2)}) collective-permute-start(bf16[32,1,34,1]{3,0,2,1:T(8,128)(2,1)S(1)} %get-tuple-element.10), channel_id=1, source_target_pairs={{2,0},{4,2},{6,4},{8,6},{10,8},{12,10},{14,12},{0,14},{3,1},{5,3},... | collective-permute-start | bytes 6536 | tf_op jit(solution)/shard_map/ppermute | solution.py:15
  68.8 1.3 %copy-start.2 = (bf16[2,1,32,128]{3,2,1,0:T(8,128)(2,1)S(1)}, bf16[2,1,32,128]{3,2,1,0:T(8,128)(2,1)}, u32[]{:S(2)}) copy-start(bf16[2,1,32,128]{3,2,1,0:T(8,128)(2,1)} %param.11) | copy-start | bytes 49156
  68.8 1.3 %copy-start.6 = (f32[2]{0:T(128)S(1)}, f32[2]{0:T(128)}, u32[]{:S(2)}) copy-start(f32[2]{0:T(128)} %param.21) | copy-start | bytes 28
where the time goes:
time: 71.3 us; the launch traced here: 70.7 us
  starting transfers between devices  26.1 us (37%)
  matrix products  20.7 us (29%)
  waiting for transfers between devices  10.9 us (15%)
  local copies, waits for them, and re-layouts  6.81 us (10%)
  other arithmetic  3.24 us (5%)
  between operations  3.01 us (4%)
    dot_general x43, matrix products, convolve(): jnp.einsum('co,cvrl->ovrl', weight[row_shift, col_shift], window, preferr...  20.1 us
    ppermute x4, starting transfers between devices, with_halo(): after = lax.ppermute(leading, axis, down)  15.5 us
    ppermute x4, waiting for transfers between devices, with_halo(): before = lax.ppermute(last, axis, up)  7.94 us
    ppermute x3, starting transfers between devices, partner(): lax.ppermute(x, axis, [(i, i ^ 1 << apart) for i in range(lax.axis_size(a...  5.44 us
    ppermute x4, starting transfers between devices, with_halo(): before = lax.ppermute(last, axis, up)  5.18 us
    ppermute x3, waiting for transfers between devices, partner(): lax.ppermute(x, axis, [(i, i ^ 1 << apart) for i in range(lax.axis_size(a...  2.93 us
    unnamed x20, local copies, waits for them, and re-layouts  1.76 us
  transfers between devices with their start and end apart: 11, of which 6 were waited for; matrix products, arithmetic and copies ran while one was open for 9% of the time, Pallas kernels for 0%

commit v1 on v0

v1 whole, which is shorter than its diff:
```python
import functools

import jax
import jax.numpy as jnp
from jax import lax
from jax.experimental import pallas as pl
from jax.experimental.pallas import tpu as pltpu
from jax.sharding import PartitionSpec as P

BF = jnp.bfloat16
F32 = jnp.float32
SLOT = 32
EDGE = 8


def dot(a, b):
    return jnp.dot(a, b, preferred_element_type=F32)


def dot_nt(a, b):
    return lax.dot_general(a, b, (((1,), (1,)), ((), ())), preferred_element_type=F32)


def iota(shape, dim):
    return lax.broadcasted_iota(jnp.int32, shape, dim)


def picks(pair, lanes, base, sign):
    want = lax.rem(base + sign * 2 * pair + 4 * lanes, lanes)
    return (iota(pair.shape, 1) == want).astype(BF)


def spread(patch_ref, first_row, rows, shifted):
    for tap in range(10):
        for component in range(2):
            start = first_row * SLOT + tap * 2 + component
            value = shifted(tap, component)
            for k in range(value.shape[1] // 128):
                patch_ref[k, pl.ds(start, rows, stride=SLOT), :] = value[:, 128 * k : 128 * k + 128]


def patches(patch_ref, lo, hi):
    parts = [patch_ref[k, lo:hi, :] for k in range(patch_ref.shape[0])]
    return jnp.concatenate(parts, axis=1).astype(BF)


def first_weights(w1_ref, row, half):
    lead = (w1_ref.shape[1] - 5 * SLOT) // 2
    start = lead - SLOT * row
    return jnp.concatenate(
        [w1_ref[2 * half + k, start : start + 8 * SLOT, :] for k in range(2)], axis=1
    )


def second_weights(w2_ref):
    tiles = []
    zero = jnp.zeros((256, 128), BF)
    for a in range(6):
        for half in range(3):
            part = [
                w2_ref[k, 256 * half : 256 * half + 256, :] if 0 <= k < 5 else zero
                for k in (a, a - 1)
            ]
            tiles.append(jnp.concatenate(part, axis=1))
    return jnp.concatenate(tiles, axis=0)


def body(
    pivot_ref,
    b4_ref,
    vel_ref,
    land_ref,
    own_ref,
    far_ref,
    near_a_ref,
    near_b_ref,
    w1_ref,
    b1_ref,
    w2_ref,
    b2_ref,
    w3_ref,
    b3_ref,
    w4_ref,
    out_ref,
    patch_i,
    patch_e,
    left_i,
    left_t,
    left_s,
    f_i,
    f_t,
    f_s,
    sec,
    third,
    turn,
    spill,
    tend,
    *,
    lon_count,
):
    rows = own_ref.shape[1]
    cols = own_ref.shape[2]
    bias1 = jnp.concatenate([b1_ref[...]] * 2, axis=1)
    bias2 = jnp.concatenate([b2_ref[...]] * 4, axis=1)
    bias3 = jnp.concatenate([b3_ref[...]] * 4, axis=1)
    ext_rows = rows + 12
    groups = (rows + 8) // 4
    pairs_in = (rows - 2) // 2
    groups_in = groups - 1

    own = own_ref[...].astype(F32)
    patch_i[...] = jnp.zeros_like(patch_i)
    rolled = [
        [pltpu.roll(own[c], (cols - t) % cols, axis=1) for c in range(2)] for t in range(10)
    ]
    spread(patch_i, 6, rows, lambda t, c: rolled[t][c])
    slot_pair = iota((64, cols), 0)
    pick = (iota((64, cols), 1) == 2 * slot_pair - 6).astype(BF)
    left_i[...] = dot_nt(pick, patches(patch_i, 0, ext_rows * SLOT)).astype(BF)
    stacked = jnp.concatenate(
        [left_i[:, 128 * g : 128 * g + 256] for g in range(groups_in)], axis=0
    )
    for row in range(4):
        for half in range(3):
            res = dot(stacked, first_weights(w1_ref, row, half))
            res = jnp.maximum(res + bias1, 0.0).astype(BF)
            for g in range(groups_in):
                f_i[row % 2, half, 2 * g + row // 2] = res[64 * g : 64 * g + 64]
    right2 = second_weights(w2_ref)
    step = 5
    for lo in range(0, pairs_in, step):
        left = jnp.concatenate(
            [
                f_i[a % 2, half, lo + a // 2 : lo + a // 2 + step].reshape(step * 64, 256)
                for a in range(6)
                for half in range(3)
            ],
            axis=1,
        )
        res = jnp.maximum(dot(left, right2) + bias2, 0.0)
        for k in range(step):
            sec[(lo + k) * 72 : (lo + k) * 72 + 64, :] = res[64 * k : 64 * k + 64]

    lon = lax.axis_index("lon")
    even = lax.rem(lon, 2) == 0
    own_tail = own_ref[:, rows - 8 :, :].astype(F32)
    far = far_ref[...].astype(F32)
    wrap = jnp.concatenate([far, own_tail], axis=1)
    near_a = near_a_ref[...].astype(F32)
    near_b = near_b_ref[...].astype(F32)
    west = jnp.where(lon == 0, wrap, jnp.where(even, near_b, near_a))
    east = jnp.where(lon == lon_count - 1, wrap, jnp.where(even, near_a, near_b))
    side = iota((rows, cols), 1) < cols // 2
    side8 = iota((8, cols), 1) < cols // 2
    wide = []
    fold = []
    for c in range(2):
        outer = jnp.where(side, east[c, :rows], west[c, :rows])
        wide.append(jnp.concatenate([own[c], outer], axis=1))
        outer = jnp.where(side8, west[c, rows:], east[c, rows:])
        turn[...] = jnp.concatenate([far[c, rows - 8 :], outer], axis=1)
        fold.append(
            -jnp.concatenate([turn[7 - k : 8 - k, :] for k in range(1, 7)] + [turn[0:2, :]], axis=0)
        )
    lanes = 2 * cols
    patch_e[...] = jnp.zeros_like(patch_e)
    spread(patch_e, 6, rows, lambda t, c: pltpu.roll(wide[c], (lanes - t) % lanes, axis=1))

    def folded(t, c):
        up = pivot_ref[c] - (lon_count * cols - 1) > 0
        value = jnp.where(
            up,
            pltpu.roll(fold[c], (t - 1 + lanes) % lanes, axis=1),
            pltpu.roll(fold[c], t + 1, axis=1),
        )
        return value[0:6]

    spread(patch_e, rows + 6, 6, folded)
    slot = iota((80, lanes), 0)
    strip = slot - 64
    pair = jnp.where(
        slot < 64,
        slot,
        jnp.where(strip < 3, strip, jnp.where(strip < 5, strip + 61, jnp.where(strip == 7, 63, 3))),
    )
    pick = picks(pair, lanes, -6, 1)
    pick_fold = picks(pair, lanes, cols + 5, -1)
    split = (rows + 6) * SLOT
    left = jnp.concatenate(
        [
            dot_nt(pick, patches(patch_e, 0, split)),
            dot_nt(pick_fold, patches(patch_e, split, ext_rows * SLOT)),
        ],
        axis=1,
    )
    left_t[...] = left[:64].astype(BF)
    left_s[...] = left[64:72]
    top = range(groups - 3, groups)
    stacked_t = [left_t[:, 128 * g : 128 * g + 256] for g in top]
    stacked_s = [left_s[:, 128 * g : 128 * g + 256] for g in range(groups)]
    stacked = jnp.concatenate(stacked_t + [jnp.concatenate(stacked_s, axis=0).astype(BF)], axis=0)
    for row in range(4):
        for half in range(3):
            res = dot(stacked, first_weights(w1_ref, row, half))
            res = jnp.maximum(res + bias1, 0.0)
            for g in range(3):
                f_t[row % 2, half, 2 * g + row // 2] = res[64 * g : 64 * g + 64].astype(BF)
            for g in range(groups):
                at = (2 * g + row // 2) * EDGE
                f_s[row % 2, half, at : at + EDGE, :] = res[192 + EDGE * g : 192 + EDGE * g + EDGE]
    pairs = (rows + 4) // 2
    left = jnp.concatenate(
        [
            jnp.concatenate(
                [
                    f_t[a % 2, half, 1 + a // 2 : 4 + a // 2].reshape(192, 256),
                    f_s[a % 2, half, (a // 2) * EDGE : (a // 2 + pairs) * EDGE, :].astype(BF),
                ],
                axis=0,
            )
            for a in range(6)
            for half in range(3)
        ],
        axis=1,
    )
    res = jnp.maximum(dot(left, right2) + bias2, 0.0)
    for k in range(3):
        at = (pairs - 3 + k) * 72
        sec[at : at + 64, :] = res[64 * k : 64 * k + 64]
    line = iota((EDGE, 256), 0)
    for k in range(pairs):
        new = res[192 + EDGE * k : 192 + EDGE * k + EDGE]
        at = k * 72
        sec[at : at + 8, :] = jnp.where(line < 3, new, sec[at : at + 8, :])
        sec[at + 56 : at + 64, :] = jnp.where(line == 7, new, sec[at + 56 : at + 64, :])
        sec[at + 64 : at + 72, :] = pltpu.roll(new, EDGE - 3, axis=0)

    pairs3 = pairs - 1
    size = pairs3 * 72
    left = jnp.concatenate(
        [sec[at : at + size, :].astype(BF) for at in (0, 1, 72, 73)], axis=1
    )
    third[0:size, :] = jnp.maximum(dot(left, w3_ref[...]) + bias3, 0.0)

    pairs4 = pairs - 2
    left = jnp.concatenate(
        [
            jnp.concatenate(
                [third[k * 72 + at : k * 72 + at + 64, :] for k in range(pairs4)], axis=0
            ).astype(BF)
            for at in (0, 1, 72, 73)
        ],
        axis=1,
    )
    res = dot_nt(w4_ref[...], left)
    parts = []
    for dc in range(2):
        stack = jnp.concatenate(
            [res[8 * dc : 8 * dc + 8, 128 * t : 128 * t + 128] for t in range(pairs4 // 2)], axis=0
        )
        high = stack.astype(BF)
        parts.append((high, (stack - high.astype(F32)).astype(BF)))
    left = jnp.concatenate([parts[0][0], parts[1][0], parts[0][1], parts[1][1]], axis=1)
    src = iota((512, 256), 0)
    dst = iota((512, 256), 1)
    half_src = lax.rem(src, 128)
    want = (half_src // 64) * 128 + 2 * lax.rem(half_src, 64) + lax.rem(src // 128, 2)
    res = dot(left, (dst == want).astype(BF))
    for k in range(2):
        spill[k] = res[:, 128 * k : 128 * k + 128]
    for c in range(2):
        for dr in range(2):
            for k in range(2):
                tend[c, pl.ds(2 * k + dr, pairs4 // 2, stride=4), :] = spill[
                    k, pl.ds(dr * 2 + c, pairs4 // 2, stride=8), :
                ]
    land = land_ref[...].astype(F32)
    for c in range(2):
        total = vel_ref[c].astype(F32) + (tend[c] + b4_ref[c])
        out_ref[c] = (land * total).astype(BF)


def pack_first(w):
    flat = w.reshape(5, 10, w.shape[3])
    lead = 3 * SLOT
    return jnp.stack(
        [
            jnp.pad(
                jnp.pad(flat, ((0, 0), (2 * b, SLOT - 10 - 2 * b), (0, 0))).reshape(5 * SLOT, -1),
                ((lead, lead), (0, 0)),
            )
            for b in range(6)
        ]
    )


def pack_second(w):
    ends = [jnp.pad(w, ((0, 0), (k, 1 - k), (0, 0), (0, 0))) for k in range(2)]
    both = jnp.concatenate(ends, axis=3)
    return both.reshape(5, 6 * w.shape[2], 2 * w.shape[3])


def blocks(w):
    parts = [
        jnp.pad(w, ((dr, 1 - dr), (dc, 1 - dc), (0, 0), (0, 0))) for dr in range(2) for dc in range(2)
    ]
    both = jnp.stack(parts, axis=3).reshape(2, 2, 2, 2, w.shape[2], 2, 2, w.shape[3])
    return both.transpose(0, 2, 1, 3, 4, 5, 6, 7)


def pack_third(w):
    return blocks(w).reshape(16 * w.shape[2], 4 * w.shape[3])


def pack_fourth(w):
    both = blocks(w).reshape(16 * w.shape[2], 2, 2, w.shape[3])
    both = both.transpose(2, 1, 3, 0).reshape(2, 2 * w.shape[3], -1)
    return jnp.pad(both, ((0, 0), (0, 8 - both.shape[1]), (0, 0))).reshape(16, -1)


def shards(velocity, land_sea, fold_pivot, w1, b1, w2, b2, w3, b3, w4, b4):
    rows = velocity.shape[2]
    cols = velocity.shape[3]
    n = lax.axis_size("lon")
    vel = velocity.reshape(2, rows, cols)
    land = land_sea.reshape(rows, cols)
    own = vel * land.astype(BF)[None]
    mirror = [(i, n - 1 - i) for i in range(n)]
    pairs_a = [(i, i ^ 1) for i in range(n)]
    pairs_b = [(0, 0), (n - 1, n - 1)]
    for k in range(1, n // 2):
        pairs_b += [(2 * k - 1, 2 * k), (2 * k, 2 * k - 1)]
    far = lax.ppermute(own, "lon", mirror)
    both = jnp.concatenate([own, far[:, rows - 8 :]], axis=1)
    near_a = lax.ppermute(both, "lon", pairs_a)
    near_b = lax.ppermute(both, "lon", pairs_b)
    vmem = pl.BlockSpec(memory_space=pltpu.VMEM)
    smem = pl.BlockSpec(memory_space=pltpu.SMEM)
    ext = rows + 12
    groups = (rows + 8) // 4
    pairs = (rows + 4) // 2
    return pl.pallas_call(
        functools.partial(body, lon_count=n),
        out_shape=jax.ShapeDtypeStruct((2, rows, cols), BF),
        in_specs=[smem, smem] + [vmem] * 13,
        out_specs=vmem,
        scratch_shapes=[
            pltpu.VMEM((1, ext * SLOT, cols), F32),
            pltpu.VMEM((2, ext * SLOT, cols), F32),
            pltpu.VMEM((64, ext * SLOT), BF),
            pltpu.VMEM((64, ext * SLOT), BF),
            pltpu.VMEM((EDGE, ext * SLOT), F32),
            pltpu.VMEM((2, 3, 2 * groups, 64, 256), BF),
            pltpu.VMEM((2, 3, 6, 64, 256), BF),
            pltpu.VMEM((2, 3, 2 * groups * EDGE, 256), F32),
            pltpu.VMEM((pairs * 72 + 8, 256), F32),
            pltpu.VMEM((pairs * 72 + 8, 128), F32),
            pltpu.VMEM((8, 2 * cols), F32),
            pltpu.VMEM((2, 64, 128), F32),
            pltpu.VMEM((2, rows, cols), F32),
        ],
        compiler_params=pltpu.CompilerParams(vmem_limit_bytes=40 << 20),
    )(
        fold_pivot,
        b4,
        vel,
        land,
        own,
        far,
        near_a,
        near_b,
        pack_first(w1),
        b1[None],
        pack_second(w2),
        b2[None],
        pack_third(w3),
        b3[None],
        pack_fourth(w4),
    ).reshape(velocity.shape)


def solution(mesh):
    in_specs = (
        P(None, ("members", "lev"), None, "lon"),
        P(("members", "lev"), None, "lon"),
    ) + (P(),) * 9
    out_specs = P(None, ("members", "lev"), None, "lon")
    return jax.shard_map(shards, mesh=mesh, in_specs=in_specs, out_specs=out_specs, check_vma=False)
```

time: 71.3 us -> 26.1 us (0.37)
  the two profiles are of different devices: /device:TPU:0 before, /device:TPU:2 now
where the time goes in v1:
time: 26.1 us; the launch traced here: 25.7 us
  Pallas kernels  9.57 us (37%)
  starting transfers between devices  7.04 us (27%)
  other arithmetic  3.09 us (12%)
  waiting for transfers between devices  2.96 us (11%)
  local copies, waits for them, and re-layouts  2.73 us (10%)
  between operations  0.28 us (1%)
    pallas_call x1, Pallas kernels, shards(): pl.pallas_call(functools.partial(body, lon_count=n), out_shape=jax.ShapeD...  9.57 us
    ppermute x1, starting transfers between devices, shards(): far = lax.ppermute(own, 'lon', mirror)  3.57 us
    ppermute x1, waiting for transfers between devices, shards(): near_b = lax.ppermute(both, 'lon', pairs_b)  2.94 us
    ppermute x1, starting transfers between devices, shards(): near_b = lax.ppermute(both, 'lon', pairs_b)  1.91 us
    ppermute x1, starting transfers between devices, shards(): near_a = lax.ppermute(both, 'lon', pairs_a)  1.56 us
    mul x2, other arithmetic, shards(): own = vel * land.astype(BF)[None]  1.47 us
    concatenate x1, other arithmetic, pack_second(): both = jnp.concatenate(ends, axis=3)  1.4 us
    reshape x1, local copies, waits for them, and re-layouts, pack_first(): flat = w.reshape(5, 10, w.shape[3])  0.73 us
  transfers between devices with their start and end apart: 3, of which 1 were waited for; matrix products, arithmetic and copies ran while one was open for 17% of the time, Pallas kernels for 0%

profile of v1, /device:TPU:2, one launch (start us, length us, event | category | flops | bytes accessed | tf_op | source)
XLA Modules:
  0.0 25.7 jit_solution(17963906783585969365)
XLA Ops:
  0.0 0.0 copy-start.7
  0.0 0.8 %convert_bitcast_fusion = bf16[32,128]{1,0:T(8,128)(2,1)S(1)} fusion(s32[1,32,128]{2,1,0:T(8,128)} %param.12), kind=kLoop, calls=%fused_computation.26 | loop fusion | flops 4096 | bytes 24576 | tf_op jit(solution)/shard_map/mul | solution.py:327
  0.8 0.7 %broadcast_multiply_fusion.own_ref = bf16[2,32,128]{2,1,0:T(8,128)(2,1)S(1)} fusion(bf16[32,128]{1,0:T(8,128)(2,1)S(1)} %convert_bitcast_fusion, bf16[2,1,32,128]{3,2,1,0:T(8,128)(2,1)} %param.11), kind=kLoop, calls=%fused_computation.25 | loop fusion | flops 8192 | bytes 40960 | tf_op jit(solution)/shard_map/mul | solution.py:327
  1.5 3.6 %collective-permute-start = (bf16[2,32,128]{2,1,0:T(8,128)(2,1)S(1)}, bf16[2,32,128]{2,1,0:T(8,128)(2,1)S(1)}, u32[]{:S(2)}, u32[]{:S(2)}) collective-permute-start(bf16[2,32,128]{2,1,0:T(8,128)(2,1)S(1)} %broadcast_multiply_fusion.own_ref), channel_id=1, source_target_pairs={{0,14},{2,12},{4,10},{6,8},{8,6},{10,4},{12,2},{14,0},{1,15},{3,13... | collective-permute-start | bytes 49160 | tf_op jit(solution)/shard_map/ppermute | solution.py:333
  5.1 0.7 %reshape.53 = bf16[5,10,128]{2,1,0:T(8,128)(2,1)S(1)} reshape(bf16[5,5,2,128]{3,2,1,0:T(2,128)(2,1)} %param.14) | data formatting | bytes 25600 | tf_op jit(solution)/shard_map/reshape | solution.py:284
  5.8 0.0 copy-start.8
  5.9 1.4 %fusion.2 = bf16[5,6,128,128]{2,3,1,0:T(8,128)(2,1)S(1)} fusion(bf16[5,5,128,64]{2,3,1,0:T(8,128)(2,1)} %param.16), kind=kLoop, calls=%fused_computation.4 | loop fusion | flops 3932160 | bytes 1392640 | tf_op jit(solution)/shard_map/concatenate | solution.py:299
  7.3 0.0 copy-done.7
  7.3 0.1 pad_bitcast_fusion.3
  7.4 0.0 copy-done.8
  7.5 0.1 pad_maximum_fusion
  7.7 0.1 pad_maximum_fusion.1
  7.8 0.1 reshape.64
  7.9 0.0 collective-permute-done.far_ref
  7.9 1.6 %collective-permute-start.1 = (bf16[2,40,128]{2,1,0:T(8,128)(2,1)S(1)}, bf16[2,40,128]{2,1,0:T(8,128)(2,1)S(1)}, u32[]{:S(2)}, u32[]{:S(2)}) collective-permute-start(bf16[2,40,128]{2,1,0:T(8,128)(2,1)S(1)} %pad_maximum_fusion.2), channel_id=1, source_target_pairs={{0,2},{2,0},{4,6},{6,4},{8,10},{10,8},{12,14},{14,12},{1,3},{3,1},... | collective-permute-start | bytes 61448 | tf_op jit(solution)/shard_map/ppermute | solution.py:335
  9.5 1.9 %collective-permute-start.2 = (bf16[2,40,128]{2,1,0:T(8,128)(2,1)S(1)}, bf16[2,40,128]{2,1,0:T(8,128)(2,1)S(1)}, u32[]{:S(2)}, u32[]{:S(2)}) collective-permute-start(bf16[2,40,128]{2,1,0:T(8,128)(2,1)S(1)} %pad_maximum_fusion.2), channel_id=1, source_target_pairs={{0,0},{14,14},{2,4},{4,2},{6,8},{8,6},{10,12},{12,10},{1,1},{15,15... | collective-permute-start | bytes 61448 | tf_op jit(solution)/shard_map/ppermute | solution.py:336
  11.4 0.7 %copy.20 = bf16[5,6,128,128]{3,2,1,0:T(8,128)(2,1)S(1)} copy(bf16[5,6,128,128]{2,3,1,0:T(8,128)(2,1)S(1)} %fusion.2) | data formatting | bytes 1966080 | tf_op jit(solution)/shard_map/concatenate | solution.py:299
  12.1 0.0 copy-start
  12.1 0.0 copy-start.1
  12.1 0.0 copy-start.2
  12.1 0.0 copy-start.3
  12.1 0.0 copy-start.4
  12.1 0.0 copy-start.5
  12.2 0.0 copy-start.6
  12.2 0.4 %copy.30 = bf16[2,2,2,2,64,2,2,32]{4,3,1,2,0,7,6,5:T(2,128)(2,1)S(1)} copy(bf16[2,2,2,2,64,2,2,32]{4,7,3,2,1,0,6,5:T(8,128)(2,1)S(1)} %bitcast.68) | data formatting | bytes 524288 | tf_op jit(solution)/shard_map/reshape | solution.py:307
  12.6 0.3 %reshape.62 = bf16[1024,128]{0,1:T(8,128)(2,1)S(1)} reshape(bf16[2,2,2,2,64,2,2,32]{4,3,2,1,0,7,6,5:T(2,128)(2,1)S(1)} %bitcast.69) | data formatting | bytes 524288 | tf_op jit(solution)/shard_map/reshape | solution.py:312
  12.9 0.2 copy.25.w3_ref
  13.1 0.0 collective-permute-done.1.near_a_ref
  13.1 2.9 %collective-permute-done.2.near_b_ref = bf16[2,40,128]{2,1,0:T(8,128)(2,1)S(1)} collective-permute-done((bf16[2,40,128]{2,1,0:T(8,128)(2,1)S(1)}, bf16[2,40,128]{2,1,0:T(8,128)(2,1)S(1)}, u32[]{:S(2)}, u32[]{:S(2)}) %collective-permute-start.2) | collective-permute-done | bytes 20512 | tf_op jit(solution)/shard_map/ppermute | solution.py:336
  16.0 0.0 copy-done
  16.1 0.0 copy-done.1
  16.1 0.0 copy-done.2
  16.1 0.0 copy-done.3
  16.1 0.0 copy-done.4
  16.1 0.0 copy-done.5
  16.1 0.0 copy-done.6
  16.1 9.6 %shard_map.109 = bf16[2,32,128]{2,1,0:T(8,128)(2,1)} custom-call(s32[2]{0:T(128)S(1)} %copy-done.2, f32[2]{0:T(128)S(1)} %copy-done.3, bf16[2,32,128]{2,1,0:T(8,128)(2,1)S(1)} %bitcast.63, s32[32,128]{1,0:T(8,128)S(1)} %bitcast.64, bf16[2,32,128]{2,1,0:T(8,128)(2,1)S(1)} %broadcast_multiply_fusion.own_ref, ...), custom_call_target="tpu_custom_call" | custom-call | tf_op jit(solution)/shard_map/pallas_call | solution.py:342
  (14 shorter events, 0.2 us)
Async XLA Ops:
  0.0 7.3 %copy-start.7 = (bf16[3,3,64,32]{2,3,1,0:T(8,128)(2,1)S(1)}, bf16[3,3,64,32]{2,3,1,0:T(8,128)(2,1)}, u32[]{:S(2)}) copy-start(bf16[3,3,64,32]{2,3,1,0:T(8,128)(2,1)} %param.18) | copy-start | bytes 110596
  1.5 6.4 %collective-permute-start = (bf16[2,32,128]{2,1,0:T(8,128)(2,1)S(1)}, bf16[2,32,128]{2,1,0:T(8,128)(2,1)S(1)}, u32[]{:S(2)}, u32[]{:S(2)}) collective-permute-start(bf16[2,32,128]{2,1,0:T(8,128)(2,1)S(1)} %broadcast_multiply_fusion.own_ref), channel_id=1, source_target_pairs={{0,14},{2,12},{4,10},{6,8},{8,6},{10,4},{12,2},{14,0},{1,15},{3,13... | collective-permute-start | bytes 49160 | tf_op jit(solution)/shard_map/ppermute | solution.py:333
  5.8 1.5 %copy-start.8 = (bf16[3,3,32,2]{2,3,1,0:T(2,128)(2,1)S(1)}, bf16[3,3,32,2]{2,3,1,0:T(2,128)(2,1)}, u32[]{:S(2)}) copy-start(bf16[3,3,32,2]{2,3,1,0:T(2,128)(2,1)} %param.20) | copy-start | bytes 3460
  7.9 5.2 %collective-permute-start.1 = (bf16[2,40,128]{2,1,0:T(8,128)(2,1)S(1)}, bf16[2,40,128]{2,1,0:T(8,128)(2,1)S(1)}, u32[]{:S(2)}, u32[]{:S(2)}) collective-permute-start(bf16[2,40,128]{2,1,0:T(8,128)(2,1)S(1)} %pad_maximum_fusion.2), channel_id=1, source_target_pairs={{0,2},{2,0},{4,6},{6,4},{8,10},{10,8},{12,14},{14,12},{1,3},{3,1},... | collective-permute-start | bytes 61448 | tf_op jit(solution)/shard_map/ppermute | solution.py:335
  9.5 6.6 %collective-permute-start.2 = (bf16[2,40,128]{2,1,0:T(8,128)(2,1)S(1)}, bf16[2,40,128]{2,1,0:T(8,128)(2,1)S(1)}, u32[]{:S(2)}, u32[]{:S(2)}) collective-permute-start(bf16[2,40,128]{2,1,0:T(8,128)(2,1)S(1)} %pad_maximum_fusion.2), channel_id=1, source_target_pairs={{0,0},{14,14},{2,4},{4,2},{6,8},{8,6},{10,12},{12,10},{1,1},{15,15... | collective-permute-start | bytes 61448 | tf_op jit(solution)/shard_map/ppermute | solution.py:336
  12.1 4.0 %copy-start = (bf16[2,1,32,128]{3,2,1,0:T(8,128)(2,1)S(1)}, bf16[2,1,32,128]{3,2,1,0:T(8,128)(2,1)}, u32[]{:S(2)}) copy-start(bf16[2,1,32,128]{3,2,1,0:T(8,128)(2,1)} %param.11) | copy-start | bytes 49156
  12.1 4.0 %copy-start.1 = (s32[1,32,128]{2,1,0:T(8,128)S(1)}, s32[1,32,128]{2,1,0:T(8,128)}, u32[]{:S(2)}) copy-start(s32[1,32,128]{2,1,0:T(8,128)} %param.12) | copy-start | bytes 49156
  12.1 4.0 %copy-start.2 = (s32[2]{0:T(128)S(1)}, s32[2]{0:T(128)}, u32[]{:S(2)}) copy-start(s32[2]{0:T(128)} %pivot_ref.1) | copy-start | bytes 28
  12.1 3.9 %copy-start.3 = (f32[2]{0:T(128)S(1)}, f32[2]{0:T(128)}, u32[]{:S(2)}) copy-start(f32[2]{0:T(128)} %b4_ref.1) | copy-start | bytes 28
  12.1 3.9 %copy-start.4 = (f32[128]{0:T(128)S(1)}, f32[128]{0:T(128)}, u32[]{:S(2)}) copy-start(f32[128]{0:T(128)} %param.15) | copy-start | bytes 1540
  12.1 3.9 %copy-start.5 = (f32[64]{0:T(128)S(1)}, f32[64]{0:T(128)}, u32[]{:S(2)}) copy-start(f32[64]{0:T(128)} %param.17) | copy-start | bytes 772
  12.2 3.9 %copy-start.6 = (f32[32]{0:T(128)S(1)}, f32[32]{0:T(128)}, u32[]{:S(2)}) copy-start(f32[32]{0:T(128)} %param.19) | copy-start | bytes 388

commit v2 on v0

v2 whole, which is shorter than its diff:
```python
import functools

import jax
import jax.numpy as jnp
from jax import lax
from jax.experimental import pallas as pl
from jax.experimental.pallas import tpu as pltpu
from jax.sharding import PartitionSpec as P

BF = jnp.bfloat16
F32 = jnp.float32
EDGE = 8
LINE = 72
SPLIT = 8


def dot(a, b):
    return jnp.dot(a, b, preferred_element_type=F32)


def dot_nt(a, b):
    return lax.dot_general(a, b, (((1,), (1,)), ((), ())), preferred_element_type=F32)


def iota(shape, dim):
    return lax.broadcasted_iota(jnp.int32, shape, dim)


def roll_lanes(x, shift):
    return pltpu.roll(x, shift % x.shape[1], axis=1)


def first_weights(w1_ref, row, half):
    zero = jnp.zeros(w1_ref.shape[2:], BF)
    sides = []
    for b in (2 * half, 2 * half + 1):
        tiles = [w1_ref[row, t - b] if 0 <= t - b < 5 else zero for t in range(10)]
        sides.append(jnp.concatenate(tiles, axis=0))
    return jnp.concatenate(sides, axis=1)


def load_field(field_ref, values):
    rows = values[0].shape[0]
    for c in range(2):
        field_ref[c, 0:8, :] = jnp.zeros((8, values[0].shape[1]), F32)
        field_ref[c, rows : rows + 16, :] = jnp.zeros((16, values[0].shape[1]), F32)
        field_ref[c, 6 : rows + 6, :] = values[c]


def load_fold(fold_ref, tails):
    for c in range(2):
        fold_ref[c] = jnp.zeros(fold_ref.shape[1:], F32)
        for k in range(1, 7):
            fold_ref[c, 5 + k : 6 + k, :] = -tails[c][7 - k : 8 - k]


def patches(ref, start, shifted):
    tiles = []
    windows = [ref[c, start : start + 8, :] for c in range(2)]
    for t in range(10):
        tiles.append(jnp.concatenate([shifted(windows[c], t, c) for c in range(2)], axis=0))
    return jnp.concatenate(tiles, axis=0).astype(BF)


def left_sides(field_ref, fold_ref, pivot_ref, wide, pick, pick_fold, groups, rows):
    out = []
    for g in groups:
        part = dot_nt(pick, patches(field_ref, 4 * g, lambda x, t, c: roll_lanes(x, -t)))
        if 4 * g + 8 > rows + 6:
            ups = [pivot_ref[c] - (wide - 1) > 0 for c in range(2)]

            def turned(x, t, c):
                return jnp.where(ups[c], roll_lanes(x, t - 1), roll_lanes(x, t + 1))

            part = part + dot_nt(pick_fold, patches(fold_ref, 4 * g - rows, turned))
        out.append(part)
    return out


def second_weights(w2_ref):
    zero = jnp.zeros(w2_ref.shape[2:], BF)
    rows = []
    for dr in range(2):
        for dc in range(2):
            rows.append(
                jnp.concatenate(
                    [
                        w2_ref[a - dr, b - dc] if 0 <= a - dr < 5 and 0 <= b - dc < 5 else zero
                        for a in range(6)
                        for b in range(6)
                    ],
                    axis=1,
                )
            )
    return jnp.concatenate(rows, axis=0)


def block_weights(w_ref):
    zero = jnp.zeros(w_ref.shape[2:], F32)
    rows = []
    for dr in range(2):
        for dc in range(2):
            cells = []
            for er in range(2):
                for ec in range(2):
                    for r in range(2):
                        for c in range(2):
                            a, b = 2 * er + r - dr, 2 * ec + c - dc
                            inside = 0 <= a < 3 and 0 <= b < 3
                            cells.append(w_ref[a, b].astype(F32) if inside else zero)
            rows.append(jnp.concatenate(cells, axis=1))
    return rows


def mask_body(vel_hbm, land_hbm, own_ref, vel_ref, land_ref, sems):
    copies = [
        pltpu.make_async_copy(vel_hbm, vel_ref, sems.at[0]),
        pltpu.make_async_copy(land_hbm, land_ref, sems.at[1]),
    ]
    for copy in copies:
        copy.start()
    for copy in copies:
        copy.wait()
    land = land_ref[...].astype(F32)
    for c in range(2):
        own_ref[c] = (vel_ref[c].astype(F32) * land).astype(BF)


def pack_first(w1_ref, wide_ref, w1_out):
    wide_ref[...] = jnp.zeros_like(wide_ref)
    for t in range(5):
        for a in range(5):
            value = w1_ref[a, t].astype(F32)
            for row in range(4):
                for c in range(2):
                    at = 8 * c + row + a
                    wide_ref[row, t, at : at + 1, :] = value[c : c + 1]
    w1_out[...] = wide_ref[...].astype(BF)


def first_layer(stacked, w1_ref, bias, put):
    for row in range(4):
        for half in range(3):
            res = dot(stacked, first_weights(w1_ref, row, half))
            put(row, half, jnp.maximum(res + bias, 0.0))


def second_layer(f_ref, right, bias, sec_ref, start, count, step):
    for lo in range(0, count, step):
        left = jnp.concatenate(
            [
                f_ref[a % 2, half, lo + a // 2 : lo + a // 2 + step].reshape(step * 64, 256)
                for a in range(6)
                for half in range(3)
            ],
            axis=1,
        )
        res = jnp.maximum(dot_nt(left, right) + bias, 0.0)
        for k in range(step):
            at = (start + lo + k) * LINE
            sec_ref[at : at + 64, :] = res[64 * k : 64 * k + 64]


def inner_first(lefts, f_ref, flat_ref, w1_ref, bias):
    stacked = jnp.concatenate(lefts, axis=0).astype(BF)
    size = stacked.shape[0]
    for row in range(4):
        res = dot(stacked, first_weights(w1_ref, row, 0))
        flat_ref[row, 0:size, :] = jnp.maximum(res + bias, 0.0)
        for half in range(3):
            for g in range(len(lefts)):
                at = 64 * g + half
                f_ref[row % 2, half, 2 * g + row // 2] = flat_ref[row, at : at + 64, :].astype(BF)


def inner_picks(cols):
    lane = iota((64, cols), 1)
    slot = iota((64, cols), 0)
    fold = lax.rem(2 * cols + 5 - 2 * slot, cols)
    return (lane == 2 * slot - 6).astype(BF), (lane == fold).astype(BF)


def south_body(
    own_ref, w1_hbm, b1_hbm, w2_hbm, b2_hbm, sec, w1_out, field, f, flat, wide, w1_ref, b1_ref,
    w2_ref, b2_ref, sems,
):
    moves = [(w1_hbm, w1_ref), (b1_hbm, b1_ref), (w2_hbm, w2_ref), (b2_hbm, b2_ref)]
    copies = [pltpu.make_async_copy(a, b, sems.at[k]) for k, (a, b) in enumerate(moves)]
    for copy in copies:
        copy.start()
    rows = own_ref.shape[1]
    cols = own_ref.shape[2]
    load_field(field, [own_ref[c].astype(F32) for c in range(2)])
    pick, _ = inner_picks(cols)
    lefts = left_sides(field, None, None, 0, pick, None, range(SPLIT // 2 + 1), rows)
    copies[0].wait()
    pack_first(w1_ref, wide, w1_out)
    copies[1].wait()
    inner_first(lefts, f, flat, w1_out, jnp.concatenate([b1_ref[...]] * 2, axis=1))
    copies[2].wait()
    copies[3].wait()
    bias2 = jnp.concatenate([b2_ref[...]] * 4, axis=1)
    second_layer(f, second_weights(w2_ref), bias2, sec, 0, SPLIT, SPLIT // 2)


def north_body(
    pivot_ref, own_ref, far_ref, w1_ref, b1_ref, w2_ref, b2_ref, w3_ref, w4_ref, sec_in,
    sec, w3_out, w4_out, sel_out, field, fold, f, flat, *, lon_count, step,
):
    bias1 = jnp.concatenate([b1_ref[...]] * 2, axis=1)
    bias2 = jnp.concatenate([b2_ref[...]] * 4, axis=1)
    rows = own_ref.shape[1]
    cols = own_ref.shape[2]
    w3_out[...] = jnp.concatenate(block_weights(w3_ref), axis=0).astype(BF)
    tiny = block_weights(w4_ref)
    blank = jnp.zeros((4, tiny[0].shape[1]), F32)
    order = [tiny[0], tiny[2], blank, tiny[1], tiny[3], blank]
    w4_out[...] = jnp.concatenate(order, axis=0).astype(BF)
    src = iota((256, 256), 0)
    want = 2 * (src & 127) + (src >> 7)
    sel_out[...] = (iota((256, 256), 1) == want).astype(BF)
    load_field(field, [own_ref[c].astype(F32) for c in range(2)])
    load_fold(fold, [far_ref[c, rows - 8 :].astype(F32) for c in range(2)])
    pick, pick_fold = inner_picks(cols)
    groups = range(SPLIT // 2, (rows + 8) // 4)
    lefts = left_sides(field, fold, pivot_ref, lon_count * cols, pick, pick_fold, groups, rows)
    inner_first(lefts, f, flat, w1_ref, bias1)
    count = (rows + 4) // 2 - SPLIT
    second_layer(f, second_weights(w2_ref), bias2, sec, SPLIT, count, step)


def last_body(
    pivot_ref, b4_ref, vel_ref, land_ref, own_ref, far_ref, near_a_ref, near_b_ref,
    w1_ref, b1_ref, w2_ref, b2_ref, w3_ref, b3_ref, w4_ref, sel_ref, sec_in,
    out_ref, sec, field, fold, f, third, spill, tend, *, lon_count,
):
    rows = own_ref.shape[1]
    cols = own_ref.shape[2]
    bias1 = jnp.concatenate([b1_ref[...]] * 2, axis=1)
    bias2 = jnp.concatenate([b2_ref[...]] * 4, axis=1)
    bias3 = jnp.concatenate([b3_ref[...]] * 4, axis=1)
    groups = (rows + 8) // 4
    pairs = (rows + 4) // 2

    lon = lax.axis_index("lon")
    even = lax.rem(lon, 2) == 0
    own = own_ref[...].astype(F32)
    far = far_ref[...].astype(F32)
    wrap = jnp.concatenate([far, own[:, rows - 8 :]], axis=1)
    near_a = near_a_ref[...].astype(F32)
    near_b = near_b_ref[...].astype(F32)
    west = jnp.where(lon == 0, wrap, jnp.where(even, near_b, near_a))
    east = jnp.where(lon == lon_count - 1, wrap, jnp.where(even, near_a, near_b))

    def around(mid, after, before):
        lane = iota(mid.shape, 1)
        half, quarter = cols // 2, cols // 4
        moved = jnp.where(lane < quarter, after, roll_lanes(mid, half))
        moved = jnp.where((lane >= quarter) & (lane < half), roll_lanes(before, half), moved)
        return jnp.where(lane >= half + quarter, mid, moved)

    load_field(field, [around(own[c], east[c, :rows], west[c, :rows]) for c in range(2)])
    load_fold(fold, [around(far[c, rows - 8 :], west[c, rows:], east[c, rows:]) for c in range(2)])
    slot = lax.rem(iota((16, cols), 0), EDGE)
    lane = iota((16, cols), 1)
    high = jnp.where(slot < 6, 60, 56)
    pair = jnp.where(slot < 4, slot, slot + high)
    start = jnp.where(slot < 4, 2 * pair - 6 + cols // 2, 2 * pair - 6)
    pick = (lane == lax.rem(start + cols, cols)).astype(BF)
    start = jnp.where(slot < 4, cols + 5 - 2 * pair, cols + 5 - 2 * pair + cols // 2)
    pick_fold = (lane == lax.rem(start + cols, cols)).astype(BF)
    lefts = left_sides(
        field, fold, pivot_ref, lon_count * cols, pick, pick_fold, range(groups), rows
    )
    stacked = jnp.concatenate([x[:EDGE] for x in lefts], axis=0).astype(BF)

    def put(row, half, res):
        for g in range(groups):
            at = (2 * g + row // 2) * EDGE
            f[row % 2, half, at : at + EDGE, :] = res[EDGE * g : EDGE * g + EDGE]

    first_layer(stacked, w1_ref, bias1, put)
    right = second_weights(w2_ref)
    sums = []
    for low in (0, 3):
        left = jnp.concatenate(
            [
                f[a % 2, half, (a // 2) * EDGE : (a // 2 + pairs) * EDGE, :].astype(BF)
                for a in range(low, low + 3)
                for half in range(3)
            ],
            axis=1,
        )
        sums.append(dot_nt(left, right[:, low * 768 : low * 768 + 2304]))
    res = jnp.maximum(sums[0] + sums[1] + bias2, 0.0)
    line = iota((EDGE, 256), 0)
    for k in range(pairs):
        new = res[EDGE * k : EDGE * k + EDGE]
        at = k * LINE
        sec[at : at + 8, :] = jnp.where(line < 4, new, sec_in[at : at + 8, :])
        sec[at + 56 : at + 64, :] = jnp.where(line >= 6, new, sec_in[at + 56 : at + 64, :])
        sec[at + 64 : at + 72, :] = pltpu.roll(new, 4, axis=0)

    pairs3 = pairs - 1
    right = w3_ref[...]
    middle = (pairs3 + 1) // 2
    for lo, hi in ((0, middle), (middle, pairs3)):
        base, size = lo * LINE, (hi - lo) * LINE
        left = jnp.concatenate(
            [
                sec[base + at : base + at + size, :].astype(BF)
                for at in (0, 1, LINE, LINE + 1)
            ],
            axis=1,
        )
        third[base : base + size, :] = jnp.maximum(dot_nt(left, right) + bias3, 0.0)

    pairs4 = pairs - 2
    right = w4_ref[...]
    tiles = []
    for lo in (0, pairs4 // 2):
        left = jnp.concatenate(
            [
                jnp.concatenate(
                    [
                        third[k * LINE + at : k * LINE + at + 64, :]
                        for k in range(lo, lo + pairs4 // 2)
                    ],
                    axis=0,
                ).astype(BF)
                for at in (0, 1, LINE, LINE + 1)
            ],
            axis=1,
        )
        res = dot_nt(right, left)
        tiles += [res[:, 128 * t : 128 * t + 128] for t in range(pairs4 // 4)]
    stack = jnp.concatenate(
        [jnp.concatenate([x[8 * dc : 8 * dc + 8] for x in tiles], axis=0) for dc in range(2)], axis=1
    )
    upper = stack.astype(BF)
    lower = (stack - upper.astype(F32)).astype(BF)
    res = dot(jnp.concatenate([upper, lower], axis=0), sel_ref[...])
    count = 8 * len(tiles)
    res = res[:count] + res[count:]
    for k in range(2):
        spill[k] = res[:, 128 * k : 128 * k + 128]
    for c in range(2):
        for dr in range(2):
            for k in range(2):
                tend[c, pl.ds(2 * k + dr, pairs4 // 2, stride=4), :] = spill[
                    k, pl.ds(dr * 2 + c, pairs4 // 2, stride=8), :
                ]
    land = land_ref[...].astype(F32)
    for c in range(2):
        total = vel_ref[c].astype(F32) + (tend[c] + b4_ref[c])
        out_ref[c] = (land * total).astype(BF)


def call(fn, ins, outs, scratch, scalars=0, flops=0, aliases=None, far_ins=()):
    vmem = pl.BlockSpec(memory_space=pltpu.VMEM)
    smem = pl.BlockSpec(memory_space=pltpu.SMEM)
    hbm = pl.BlockSpec(memory_space=pltpu.HBM)
    specs = [smem] * scalars + [vmem] * (len(ins) - scalars)
    ins = list(ins)
    for k in far_ins:
        specs[k] = hbm
        ins[k] = pltpu.with_memory_space_constraint(ins[k], pltpu.HBM)
    return pl.pallas_call(
        fn,
        out_shape=outs,
        in_specs=specs,
        out_specs=[vmem] * len(outs),
        scratch_shapes=scratch,
        input_output_aliases=aliases or {},
        cost_estimate=pl.CostEstimate(flops=flops, bytes_accessed=1 << 20, transcendentals=0),
        compiler_params=pltpu.CompilerParams(
            vmem_limit_bytes=32 << 20
        ),
    )(*ins)


def step(velocity, land_sea, fold_pivot, w1, b1, w2, b2, w3, b3, w4, b4):
    rows = velocity.shape[2]
    cols = velocity.shape[3]
    n = lax.axis_size("lon")
    vel = velocity.reshape(2, rows, cols)
    land = land_sea.reshape(rows, cols)
    w2, w3, w4 = (jnp.swapaxes(w, 2, 3) for w in (w2, w3, w4))
    b1, b2, b3 = b1[None], b2[None], b3[None]
    shape = jax.ShapeDtypeStruct
    scratch = pltpu.VMEM
    sems = pltpu.SemaphoreType.DMA
    (own,) = call(
        mask_body,
        [vel, land],
        [shape(vel.shape, BF)],
        [scratch(vel.shape, BF), scratch(land.shape, jnp.int32), sems((2,))],
        far_ins=(0, 1),
    )
    mirror = [(i, n - 1 - i) for i in range(n)]
    pairs_a = [(i, i ^ 1) for i in range(n)]
    pairs_b = [(0, 0), (n - 1, n - 1)]
    for k in range(1, n // 2):
        pairs_b += [(2 * k - 1, 2 * k), (2 * k, 2 * k - 1)]
    far = lax.ppermute(own, "lon", mirror)
    groups = (rows + 8) // 4
    pairs = (rows + 4) // 2
    sec_shape = shape((pairs * LINE + 8, 256), F32)
    south_groups = SPLIT // 2 + 1
    north_groups = groups - SPLIT // 2
    packed = (4, 5, 16, w1.shape[3])
    field = scratch((2, rows + 16, cols), F32)
    fold = scratch((2, 16, cols), F32)
    sec, w1_wide = call(
        south_body,
        [own, w1, b1, w2, b2],
        [sec_shape, shape(packed, BF)],
        [field, scratch((2, 3, 2 * south_groups, 64, 256), BF)]
        + [scratch((4, 64 * south_groups + 8, 256), F32), scratch(packed, F32)]
        + [scratch(x.shape, x.dtype) for x in (w1, b1, w2, b2)]
        + [sems((4,))],
        flops=2 * 64 * SPLIT * 256 * 4608,
        far_ins=(1, 2, 3, 4),
    )
    both = jnp.concatenate([own, far[:, rows - 8 :]], axis=1)
    near_a = lax.ppermute(both, "lon", pairs_a)
    near_b = lax.ppermute(both, "lon", pairs_b)
    sec, w3_wide, w4_wide, sel = call(
        functools.partial(north_body, lon_count=n, step=(pairs - SPLIT) // 2),
        [fold_pivot, own, far, w1_wide, b1, w2, b2, w3, w4, sec],
        [sec_shape, shape((128, 1024), BF), shape((16, 512), BF), shape((256, 256), BF)],
        [field, fold, scratch((2, 3, 2 * north_groups, 64, 256), BF)]
        + [scratch((4, 64 * north_groups + 8, 256), F32)],
        scalars=1,
        flops=2 * 64 * (pairs - SPLIT) * 256 * 4608,
        aliases={9: 0},
    )
    out, _ = call(
        functools.partial(last_body, lon_count=n),
        [fold_pivot, b4, vel, land, own, far, near_a, near_b]
        + [w1_wide, b1, w2, b2, w3_wide, b3, w4_wide, sel, sec],
        [shape((2, rows, cols), BF), sec_shape],
        [
            field,
            fold,
            scratch((2, 3, 2 * groups * EDGE, 256), F32),
            scratch((pairs * LINE + 8, 128), F32),
            scratch((2, 64, 128), F32),
            scratch((2, rows, cols), F32),
        ],
        scalars=2,
        flops=2 * 64 * pairs * 256 * 1024,
        aliases={16: 1},
    )
    return out.reshape(velocity.shape)


def solution(mesh):
    in_specs = (
        P(None, ("members", "lev"), None, "lon"),
        P(("members", "lev"), None, "lon"),
    ) + (P(),) * 9
    out_specs = P(None, ("members", "lev"), None, "lon")
    return jax.shard_map(step, mesh=mesh, in_specs=in_specs, out_specs=out_specs, check_vma=False)
```

time: 71.3 us -> 21.1 us (0.30)
  matrix products: 20.7 us -> 0 us
  starting transfers between devices: 26.1 us -> 9.06 us
  Pallas kernels: 0 us -> 11.5 us
  waiting for transfers between devices: 10.9 us -> 0.01 us
  local copies, waits for them, and re-layouts: 6.81 us -> 0.06 us
  other arithmetic: 3.24 us -> 0.01 us
  between operations: 3.01 us -> 0.18 us
    dot_general x44 -> x0, matrix products: 20.7 us -> none  [the longest x43 20.1 us: convolve(): jnp.einsum('co,cvrl->ovrl', weight[row_shift, col_shift], window, preferr...]
    ppermute x11 -> x3, starting transfers between devices: 26.1 us -> 9.06 us  [the longest x1 6.07 us: step(): far = lax.ppermute(own, 'lon', mirror)]
    pallas_call x0 -> x4, Pallas kernels: none -> 11.5 us  [call(): pl.pallas_call(fn, out_shape=outs, in_specs=specs, out_specs=[vmem] * len...]
    ppermute x11 -> x3, waiting for transfers between devices: 10.9 us -> 0.01 us  [the longest x1 0.01 us: step(): far = lax.ppermute(own, 'lon', mirror)]
    slice x11 -> x1, local copies, waits for them, and re-layouts: 2.54 us -> 0.01 us  [step(): both = jnp.concatenate([own, far[:, rows - 8:]], axis=1)]
    unnamed x20, local copies, waits for them, and re-layouts: 1.76 us -> 0.05 us
    mul x2 -> x0, other arithmetic: 1.54 us -> none  [the longest x1 0.8 us: shards(): land_sea.astype(jnp.float32)[None]]
    concatenate x2 -> x0, local copies, waits for them, and re-layouts: 0.89 us -> none  [the longest x1 0.89 us: convolve(): jnp.concatenate([field_data[:, :, row_shift:row_shift + out_rows, col_shi...]
  transfers between devices with their start and end apart: 11 -> 3, of which waited for: 6 -> 0; matrix products, arithmetic and copies ran while one was open for 9% -> 0% of each run, Pallas kernels for 0% -> 27%
where the time goes in v2:
time: 21.1 us; the launch traced here: 20.8 us
  Pallas kernels  11.5 us (55%)
  starting transfers between devices  9.06 us (43%)
    pallas_call x4, Pallas kernels, call(): pl.pallas_call(fn, out_shape=outs, in_specs=specs, out_specs=[vmem] * len...  11.5 us
    ppermute x1, starting transfers between devices, step(): far = lax.ppermute(own, 'lon', mirror)  6.07 us
    ppermute x1, starting transfers between devices, step(): near_a = lax.ppermute(both, 'lon', pairs_a)  2.33 us
    ppermute x1, starting transfers between devices, step(): near_b = lax.ppermute(both, 'lon', pairs_b)  0.66 us
  transfers between devices with their start and end apart: 3, of which 0 were waited for; matrix products, arithmetic and copies ran while one was open for 0% of the time, Pallas kernels for 27%

profile of v2, /device:TPU:0, one launch (start us, length us, event | category | flops | bytes accessed | tf_op | source)
XLA Modules:
  0.0 20.8 jit_solution(993195627089042988)
XLA Ops:
  0.0 0.8 %shard_map.109.own_ref = bf16[2,32,128]{2,1,0:T(8,128)(2,1)S(1)} custom-call(bf16[2,32,128]{2,1,0:T(8,128)(2,1)} %bitcast.14, s32[32,128]{1,0:T(8,128)} %bitcast.16), custom_call_target="tpu_custom_call" | custom-call | bytes 1048576 | tf_op jit(solution)/shard_map/pallas_call | solution.py:368
  0.8 6.1 %collective-permute-start = (bf16[2,32,128]{2,1,0:T(8,128)(2,1)S(1)}, bf16[2,32,128]{2,1,0:T(8,128)(2,1)S(1)}, u32[]{:S(2)}, u32[]{:S(2)}) collective-permute-start(bf16[2,32,128]{2,1,0:T(8,128)(2,1)S(1)} %shard_map.109.own_ref), channel_id=1, source_target_pairs={{0,14},{2,12},{4,10},{6,8},{8,6},{10,4},{12,2},{14,0},{1,15},{3,13... | collective-permute-start | bytes 49160 | tf_op jit(solution)/shard_map/ppermute | solution.py:405
  6.8 0.0 copy-start
  6.8 0.0 copy-start.3
  6.8 0.0 copy-start.5
  6.8 0.0 copy-start.6
  6.8 0.0 copy-start.8
  6.9 0.0 copy-start.9
  6.9 2.9 %shard_map.110 = (f32[1304,256]{1,0:T(8,128)S(1)}, bf16[4,5,16,128]{3,2,1,0:T(8,128)(2,1)S(1)}) custom-call(bf16[2,32,128]{2,1,0:T(8,128)(2,1)S(1)} %shard_map.109.own_ref, bf16[5,5,2,128]{3,2,1,0:T(2,128)(2,1)} %w1_hbm.1, f32[1,128]{1,0:T(1,128)} %bitcast.18, bf16[5,5,64,128]{3,2,1,0:T(8,128)(2,1)} %bitcast.11, f32[1,64]{1,0:T(1,128)} %bitcast.21), custom_call_target="tpu_custom_call" | custom-call | flops 1207959552 | bytes 1048576 | tf_op jit(solution)/shard_map/pallas_call | solution.py:368
  9.7 0.0 collective-permute-done.far_ref
  9.8 0.7 %collective-permute-start.2 = (bf16[2,40,128]{2,1,0:T(8,128)(2,1)S(1)}, bf16[2,40,128]{2,1,0:T(8,128)(2,1)S(1)}, u32[]{:S(2)}, u32[]{:S(2)}) collective-permute-start(bf16[2,40,128]{2,1,0:T(8,128)(2,1)S(1)} %pad_maximum_fusion), channel_id=1, source_target_pairs={{0,0},{14,14},{2,4},{4,2},{6,8},{8,6},{10,12},{12,10},{1,1},{15,15... | collective-permute-start | bytes 61448 | tf_op jit(solution)/shard_map/ppermute | solution.py:427
  10.5 2.3 %collective-permute-start.1 = (bf16[2,40,128]{2,1,0:T(8,128)(2,1)S(1)}, bf16[2,40,128]{2,1,0:T(8,128)(2,1)S(1)}, u32[]{:S(2)}, u32[]{:S(2)}) collective-permute-start(bf16[2,40,128]{2,1,0:T(8,128)(2,1)S(1)} %pad_maximum_fusion), channel_id=1, source_target_pairs={{0,2},{2,0},{4,6},{6,4},{8,10},{10,8},{12,14},{14,12},{1,3},{3,1},... | collective-permute-start | bytes 61448 | tf_op jit(solution)/shard_map/ppermute | solution.py:426
  12.8 0.0 copy-done
  12.8 0.0 copy-done.3
  12.8 0.0 copy-done.5
  12.8 0.0 copy-done.6
  12.8 0.0 copy-done.8
  12.8 0.0 copy-done.9
  12.8 0.0 copy-start.1
  12.8 0.0 copy-start.2
  12.8 0.0 copy-start.4
  12.9 0.0 copy-start.7
  12.9 2.8 %shard_map.111 = (f32[1304,256]{1,0:T(8,128)S(1)}, bf16[128,1024]{1,0:T(8,128)(2,1)S(1)}, bf16[16,512]{1,0:T(8,128)(2,1)S(1)}, bf16[256,256]{1,0:T(8,128)(2,1)S(1)}) custom-call(s32[2]{0:T(128)S(1)} %copy-done.3, bf16[2,32,128]{2,1,0:T(8,128)(2,1)S(1)} %shard_map.109.own_ref, ...), custom_call_target="tpu_custom_call", output_to_operand_aliasing={{0}: (9, {})} | custom-call | flops 1509949440 | bytes 1048576 | tf_op jit(solution)/shard_map/pallas_call | solution.py:368
  15.7 0.0 collective-permute-done.2.near_b_ref
  15.7 0.0 collective-permute-done.1.near_a_ref
  15.7 0.0 copy-done.1
  15.7 0.0 copy-done.2
  15.7 0.0 copy-done.4
  15.7 0.0 copy-done.7
  15.8 5.1 %shard_map.112 = (bf16[2,32,128]{2,1,0:T(8,128)(2,1)}, f32[1304,256]{1,0:T(8,128)S(1)}) custom-call(s32[2]{0:T(128)S(1)} %copy-done.3, f32[2]{0:T(128)S(1)} %copy-done.4, bf16[2,32,128]{2,1,0:T(8,128)(2,1)S(1)} %bitcast.15, s32[32,128]{1,0:T(8,128)S(1)} %bitcast.17, bf16[2,32,128]{2,1,0:T(8,128)(2,1)S(1)} %shard_map.109.own_ref, ...), custom_call_target="tpu_custom_call", output_to_operand_aliasing={{1}: (16, {})} | custom-call | flops 603979776 | bytes 1048576 | tf_op jit(solution)/shard_map/pallas_call | solution.py:368
  (2 shorter events, 0.0 us)
Async XLA Ops:
  0.8 9.0 %collective-permute-start = (bf16[2,32,128]{2,1,0:T(8,128)(2,1)S(1)}, bf16[2,32,128]{2,1,0:T(8,128)(2,1)S(1)}, u32[]{:S(2)}, u32[]{:S(2)}) collective-permute-start(bf16[2,32,128]{2,1,0:T(8,128)(2,1)S(1)} %shard_map.109.own_ref), channel_id=1, source_target_pairs={{0,14},{2,12},{4,10},{6,8},{8,6},{10,4},{12,2},{14,0},{1,15},{3,13... | collective-permute-start | bytes 49160 | tf_op jit(solution)/shard_map/ppermute | solution.py:405
  6.8 5.9 %copy-start = (bf16[5,5,128,64]{2,3,1,0:T(8,128)(2,1)S(1)}, bf16[5,5,128,64]{2,3,1,0:T(8,128)(2,1)}, u32[]{:S(2)}) copy-start(bf16[5,5,128,64]{2,3,1,0:T(8,128)(2,1)} %param.16) | copy-start | bytes 1228804
  6.8 5.9 %copy-start.3 = (s32[2]{0:T(128)S(1)}, s32[2]{0:T(128)}, u32[]{:S(2)}) copy-start(s32[2]{0:T(128)} %pivot_ref.3) | copy-start | bytes 28
  6.8 6.0 %copy-start.5 = (f32[128]{0:T(128)S(1)}, f32[128]{0:T(128)}, u32[]{:S(2)}) copy-start(f32[128]{0:T(128)} %param.15) | copy-start | bytes 1540
  6.8 6.0 %copy-start.6 = (f32[64]{0:T(128)S(1)}, f32[64]{0:T(128)}, u32[]{:S(2)}) copy-start(f32[64]{0:T(128)} %param.17) | copy-start | bytes 772
  6.8 6.0 %copy-start.8 = (bf16[3,3,64,32]{2,3,1,0:T(8,128)(2,1)S(1)}, bf16[3,3,64,32]{2,3,1,0:T(8,128)(2,1)}, u32[]{:S(2)}) copy-start(bf16[3,3,64,32]{2,3,1,0:T(8,128)(2,1)} %param.18) | copy-start | bytes 110596
  6.9 5.9 %copy-start.9 = (bf16[3,3,32,2]{2,3,1,0:T(2,128)(2,1)S(1)}, bf16[3,3,32,2]{2,3,1,0:T(2,128)(2,1)}, u32[]{:S(2)}) copy-start(bf16[3,3,32,2]{2,3,1,0:T(2,128)(2,1)} %param.20) | copy-start | bytes 3460
  9.8 5.9 %collective-permute-start.2 = (bf16[2,40,128]{2,1,0:T(8,128)(2,1)S(1)}, bf16[2,40,128]{2,1,0:T(8,128)(2,1)S(1)}, u32[]{:S(2)}, u32[]{:S(2)}) collective-permute-start(bf16[2,40,128]{2,1,0:T(8,128)(2,1)S(1)} %pad_maximum_fusion), channel_id=1, source_target_pairs={{0,0},{14,14},{2,4},{4,2},{6,8},{8,6},{10,12},{12,10},{1,1},{15,15... | collective-permute-start | bytes 61448 | tf_op jit(solution)/shard_map/ppermute | solution.py:427
  10.5 5.3 %collective-permute-start.1 = (bf16[2,40,128]{2,1,0:T(8,128)(2,1)S(1)}, bf16[2,40,128]{2,1,0:T(8,128)(2,1)S(1)}, u32[]{:S(2)}, u32[]{:S(2)}) collective-permute-start(bf16[2,40,128]{2,1,0:T(8,128)(2,1)S(1)} %pad_maximum_fusion), channel_id=1, source_target_pairs={{0,2},{2,0},{4,6},{6,4},{8,10},{10,8},{12,14},{14,12},{1,3},{3,1},... | collective-permute-start | bytes 61448 | tf_op jit(solution)/shard_map/ppermute | solution.py:426
  12.8 2.9 %copy-start.1 = (bf16[2,1,32,128]{3,2,1,0:T(8,128)(2,1)S(1)}, bf16[2,1,32,128]{3,2,1,0:T(8,128)(2,1)}, u32[]{:S(2)}) copy-start(bf16[2,1,32,128]{3,2,1,0:T(8,128)(2,1)} %param.11) | copy-start | bytes 49156
  12.8 2.9 %copy-start.2 = (s32[1,32,128]{2,1,0:T(8,128)S(1)}, s32[1,32,128]{2,1,0:T(8,128)}, u32[]{:S(2)}) copy-start(s32[1,32,128]{2,1,0:T(8,128)} %param.12) | copy-start | bytes 49156
  12.8 2.9 %copy-start.4 = (f32[2]{0:T(128)S(1)}, f32[2]{0:T(128)}, u32[]{:S(2)}) copy-start(f32[2]{0:T(128)} %b4_ref.1) | copy-start | bytes 28
  12.9 2.9 %copy-start.7 = (f32[32]{0:T(128)S(1)}, f32[32]{0:T(128)}, u32[]{:S(2)}) copy-start(f32[32]{0:T(128)} %param.19) | copy-start | bytes 388

commit v3 on v2

--- a/solution.py
+++ b/solution.py
@@ -30,11 +30,11 @@
     return pltpu.roll(x, shift % x.shape[1], axis=1)
 
 
-def first_weights(w1_ref, row, half):
+def first_weights(w1_ref, row):
     zero = jnp.zeros(w1_ref.shape[2:], BF)
     sides = []
-    for b in (2 * half, 2 * half + 1):
-        tiles = [w1_ref[row, t - b] if 0 <= t - b < 5 else zero for t in range(10)]
+    for b in range(2):
+        tiles = [w1_ref[row, t - b] if 0 <= t - b < 5 else zero for t in range(6)]
         sides.append(jnp.concatenate(tiles, axis=0))
     return jnp.concatenate(sides, axis=1)
 
@@ -57,7 +57,7 @@
 def patches(ref, start, shifted):
     tiles = []
     windows = [ref[c, start : start + 8, :] for c in range(2)]
-    for t in range(10):
+    for t in range(6):
         tiles.append(jnp.concatenate([shifted(windows[c], t, c) for c in range(2)], axis=0))
     return jnp.concatenate(tiles, axis=0).astype(BF)
 
@@ -80,29 +80,26 @@
 def second_weights(w2_ref):
     zero = jnp.zeros(w2_ref.shape[2:], BF)
     rows = []
-    for dr in range(2):
-        for dc in range(2):
-            rows.append(
-                jnp.concatenate(
-                    [
-                        w2_ref[a - dr, b - dc] if 0 <= a - dr < 5 and 0 <= b - dc < 5 else zero
-                        for a in range(6)
-                        for b in range(6)
-                    ],
-                    axis=1,
-                )
-            )
+    for shift in range(3):
+        for dr in range(2):
+            for dc in range(2):
+                cells = []
+                for a in range(6):
+                    for b in (2 * shift - dc, 2 * shift + 1 - dc):
+                        inside = 0 <= a - dr < 5 and 0 <= b < 5
+                        cells.append(w2_ref[a - dr, b] if inside else zero)
+                rows.append(jnp.concatenate(cells, axis=1))
     return jnp.concatenate(rows, axis=0)
 
 
-def block_weights(w_ref):
+def block_weights(w_ref, shifts):
     zero = jnp.zeros(w_ref.shape[2:], F32)
     rows = []
     for dr in range(2):
         for dc in range(2):
             cells = []
             for er in range(2):
-                for ec in range(2):
+                for ec in shifts:
                     for r in range(2):
                         for c in range(2):
                             a, b = 2 * er + r - dr, 2 * ec + c - dc
@@ -138,39 +135,46 @@
     w1_out[...] = wide_ref[...].astype(BF)
 
 
-def first_layer(stacked, w1_ref, bias, put):
+def first_layer(lefts, f_ref, w1_ref, bias):
+    stacked = jnp.concatenate(lefts, axis=0).astype(BF)
+    size = lefts[0].shape[0]
     for row in range(4):
-        for half in range(3):
-            res = dot(stacked, first_weights(w1_ref, row, half))
-            put(row, half, jnp.maximum(res + bias, 0.0))
-
-
-def second_layer(f_ref, right, bias, sec_ref, start, count, step):
-    for lo in range(0, count, step):
-        left = jnp.concatenate(
-            [
-                f_ref[a % 2, half, lo + a // 2 : lo + a // 2 + step].reshape(step * 64, 256)
-                for a in range(6)
-                for half in range(3)
-            ],
-            axis=1,
-        )
-        res = jnp.maximum(dot_nt(left, right) + bias, 0.0)
-        for k in range(step):
-            at = (start + lo + k) * LINE
-            sec_ref[at : at + 64, :] = res[64 * k : 64 * k + 64]
-
-
-def inner_first(lefts, f_ref, flat_ref, w1_ref, bias):
-    stacked = jnp.concatenate(lefts, axis=0).astype(BF)
-    size = stacked.shape[0]
-    for row in range(4):
-        res = dot(stacked, first_weights(w1_ref, row, 0))
-        flat_ref[row, 0:size, :] = jnp.maximum(res + bias, 0.0)
-        for half in range(3):
-            for g in range(len(lefts)):
-                at = 64 * g + half
-                f_ref[row % 2, half, 2 * g + row // 2] = flat_ref[row, at : at + 64, :].astype(BF)
+        res = dot(stacked, first_weights(w1_ref, row))
+        res = jnp.maximum(res + bias, 0.0).astype(BF)
+        for g in range(len(lefts)):
+            f_ref[row % 2, 2 * g + row // 2] = res[size * g : size * g + size]
+
+
+def second_layer(f_ref, right, acc_ref, lo, count):
+    size = f_ref.shape[2]
+    left = jnp.concatenate(
+        [
+            f_ref[a % 2, lo + a // 2 : lo + a // 2 + count].reshape(count * size, 256)
+            for a in range(6)
+        ],
+        axis=1,
+    )
+    res = dot_nt(left, right)
+    for shift in range(3):
+        acc_ref[shift, 0 : count * size, :] = res[:, 256 * shift : 256 * shift + 256]
+
+
+def shifted_sum(acc_ref, at, size, bias):
+    parts = [acc_ref[k, at + k : at + k + size, :] for k in range(acc_ref.shape[0])]
+    total = parts[0]
+    for part in parts[1:]:
+        total = total + part
+    return jnp.maximum(total + bias, 0.0)
+
+
+def inner_second(f_ref, right, bias, acc_ref, sec_ref, start, count):
+    chunks = acc_ref.shape[0]
+    step = count // chunks
+    for k in range(chunks):
+        second_layer(f_ref, right, acc_ref.at[k], k * step, step)
+        for p in range(step):
+            at = (start + k * step + p) * LINE
+            sec_ref[at : at + 64, :] = shifted_sum(acc_ref.at[k], 64 * p, 64, bias)
 
 
 def inner_picks(cols):
@@ -181,7 +185,7 @@
 
 
 def south_body(
-    own_ref, w1_hbm, b1_hbm, w2_hbm, b2_hbm, sec, w1_out, field, f, flat, wide, w1_ref, b1_ref,
+    own_ref, w1_hbm, b1_hbm, w2_hbm, b2_hbm, sec, w1_out, field, f, acc, wide, w1_ref, b1_ref,
     w2_ref, b2_ref, sems,
 ):
     moves = [(w1_hbm, w1_ref), (b1_hbm, b1_ref), (w2_hbm, w2_ref), (b2_hbm, b2_ref)]
@@ -196,23 +200,24 @@
     copies[0].wait()
     pack_first(w1_ref, wide, w1_out)
     copies[1].wait()
-    inner_first(lefts, f, flat, w1_out, jnp.concatenate([b1_ref[...]] * 2, axis=1))
+    first_layer(lefts, f, w1_out, jnp.concatenate([b1_ref[...]] * 2, axis=1))
     copies[2].wait()
     copies[3].wait()
     bias2 = jnp.concatenate([b2_ref[...]] * 4, axis=1)
-    second_layer(f, second_weights(w2_ref), bias2, sec, 0, SPLIT, SPLIT // 2)
+    inner_second(f, second_weights(w2_ref), bias2, acc, sec, 0, SPLIT)
 
 
 def north_body(
     pivot_ref, own_ref, far_ref, w1_ref, b1_ref, w2_ref, b2_ref, w3_ref, w4_ref, sec_in,
-    sec, w3_out, w4_out, sel_out, field, fold, f, flat, *, lon_count, step,
+    sec, w3_out, w4_out, sel_out, field, fold, f, acc, *, lon_count,
 ):
     bias1 = jnp.concatenate([b1_ref[...]] * 2, axis=1)
     bias2 = jnp.concatenate([b2_ref[...]] * 4, axis=1)
     rows = own_ref.shape[1]
     cols = own_ref.shape[2]
-    w3_out[...] = jnp.concatenate(block_weights(w3_ref), axis=0).astype(BF)
-    tiny = block_weights(w4_ref)
+    blocks = block_weights(w3_ref, (0,)) + block_weights(w3_ref, (1,))
+    w3_out[...] = jnp.concatenate(blocks, axis=0).astype(BF)
+    tiny = block_weights(w4_ref, (0, 1))
     blank = jnp.zeros((4, tiny[0].shape[1]), F32)
     order = [tiny[0], tiny[2], blank, tiny[1], tiny[3], blank]
     w4_out[...] = jnp.concatenate(order, axis=0).astype(BF)
@@ -224,15 +229,15 @@
     pick, pick_fold = inner_picks(cols)
     groups = range(SPLIT // 2, (rows + 8) // 4)
     lefts = left_sides(field, fold, pivot_ref, lon_count * cols, pick, pick_fold, groups, rows)
-    inner_first(lefts, f, flat, w1_ref, bias1)
+    first_layer(lefts, f, w1_ref, bias1)
     count = (rows + 4) // 2 - SPLIT
-    second_layer(f, second_weights(w2_ref), bias2, sec, SPLIT, count, step)
+    inner_second(f, second_weights(w2_ref), bias2, acc, sec, SPLIT, count)
 
 
 def last_body(
     pivot_ref, b4_ref, vel_ref, land_ref, own_ref, far_ref, near_a_ref, near_b_ref,
     w1_ref, b1_ref, w2_ref, b2_ref, w3_ref, b3_ref, w4_ref, sel_ref, sec_in,
-    out_ref, sec, field, fold, f, third, spill, tend, *, lon_count,
+    out_ref, sec, field, fold, f, acc, acc3, third, spill, tend, *, lon_count,
 ):
     rows = own_ref.shape[1]
     cols = own_ref.shape[2]
@@ -261,59 +266,38 @@
 
     load_field(field, [around(own[c], east[c, :rows], west[c, :rows]) for c in range(2)])
     load_fold(fold, [around(far[c, rows - 8 :], west[c, rows:], east[c, rows:]) for c in range(2)])
-    slot = lax.rem(iota((16, cols), 0), EDGE)
-    lane = iota((16, cols), 1)
-    high = jnp.where(slot < 6, 60, 56)
-    pair = jnp.where(slot < 4, slot, slot + high)
-    start = jnp.where(slot < 4, 2 * pair - 6 + cols // 2, 2 * pair - 6)
+    slot = iota((2 * EDGE, cols), 0)
+    lane = iota((2 * EDGE, cols), 1)
+    low = slot < EDGE
+    pair = jnp.where(low, slot, slot + (cols // 2 - 2 - EDGE))
+    start = 2 * pair - 6 + jnp.where(low, cols // 2, 0)
     pick = (lane == lax.rem(start + cols, cols)).astype(BF)
-    start = jnp.where(slot < 4, cols + 5 - 2 * pair, cols + 5 - 2 * pair + cols // 2)
+    start = cols + 5 - 2 * pair + jnp.where(low, 0, cols // 2)
     pick_fold = (lane == lax.rem(start + cols, cols)).astype(BF)
     lefts = left_sides(
         field, fold, pivot_ref, lon_count * cols, pick, pick_fold, range(groups), rows
     )
-    stacked = jnp.concatenate([x[:EDGE] for x in lefts], axis=0).astype(BF)
-
-    def put(row, half, res):
-        for g in range(groups):
-            at = (2 * g + row // 2) * EDGE
-            f[row % 2, half, at : at + EDGE, :] = res[EDGE * g : EDGE * g + EDGE]
-
-    first_layer(stacked, w1_ref, bias1, put)
-    right = second_weights(w2_ref)
-    sums = []
-    for low in (0, 3):
-        left = jnp.concatenate(
-            [
-                f[a % 2, half, (a // 2) * EDGE : (a // 2 + pairs) * EDGE, :].astype(BF)
-                for a in range(low, low + 3)
-                for half in range(3)
-            ],
-            axis=1,
-        )
-        sums.append(dot_nt(left, right[:, low * 768 : low * 768 + 2304]))
-    res = jnp.maximum(sums[0] + sums[1] + bias2, 0.0)
+    first_layer(lefts, f, w1_ref, bias1)
+    second_layer(f, second_weights(w2_ref), acc, 0, pairs)
     line = iota((EDGE, 256), 0)
     for k in range(pairs):
-        new = res[EDGE * k : EDGE * k + EDGE]
         at = k * LINE
+        new = shifted_sum(acc, 2 * EDGE * k, EDGE, bias2)
         sec[at : at + 8, :] = jnp.where(line < 4, new, sec_in[at : at + 8, :])
+        new = pltpu.roll(shifted_sum(acc, 2 * EDGE * k + EDGE, EDGE, bias2), 6, axis=0)
         sec[at + 56 : at + 64, :] = jnp.where(line >= 6, new, sec_in[at + 56 : at + 64, :])
-        sec[at + 64 : at + 72, :] = pltpu.roll(new, 4, axis=0)
+        sec[at + 64 : at + 72, :] = new
 
     pairs3 = pairs - 1
     right = w3_ref[...]
     middle = (pairs3 + 1) // 2
-    for lo, hi in ((0, middle), (middle, pairs3)):
+    for part, (lo, hi) in enumerate(((0, middle), (middle, pairs3))):
         base, size = lo * LINE, (hi - lo) * LINE
-        left = jnp.concatenate(
-            [
-                sec[base + at : base + at + size, :].astype(BF)
-                for at in (0, 1, LINE, LINE + 1)
-            ],
-            axis=1,
-        )
-        third[base : base + size, :] = jnp.maximum(dot_nt(left, right) + bias3, 0.0)
+        left = [sec[base + at : base + at + size, :].astype(BF) for at in (0, LINE)]
+        res = dot_nt(jnp.concatenate(left, axis=1), right)
+        for shift in range(2):
+            acc3[part, shift, 0:size, :] = res[:, 128 * shift : 128 * shift + 128]
+        third[base : base + size, :] = shifted_sum(acc3.at[part], 0, size, bias3)
 
     pairs4 = pairs - 2
     right = w4_ref[...]
@@ -415,8 +399,8 @@
         south_body,
         [own, w1, b1, w2, b2],
         [sec_shape, shape(packed, BF)],
-        [field, scratch((2, 3, 2 * south_groups, 64, 256), BF)]
-        + [scratch((4, 64 * south_groups + 8, 256), F32), scratch(packed, F32)]
+        [field, scratch((2, 2 * south_groups, 64, 256), BF)]
+        + [scratch((2, 3, 32 * SPLIT + 8, 256), F32), scratch(packed, F32)]
         + [scratch(x.shape, x.dtype) for x in (w1, b1, w2, b2)]
         + [sems((4,))],
         flops=2 * 64 * SPLIT * 256 * 4608,
@@ -426,11 +410,11 @@
     near_a = lax.ppermute(both, "lon", pairs_a)
     near_b = lax.ppermute(both, "lon", pairs_b)
     sec, w3_wide, w4_wide, sel = call(
-        functools.partial(north_body, lon_count=n, step=(pairs - SPLIT) // 2),
+        functools.partial(north_body, lon_count=n),
         [fold_pivot, own, far, w1_wide, b1, w2, b2, w3, w4, sec],
-        [sec_shape, shape((128, 1024), BF), shape((16, 512), BF), shape((256, 256), BF)],
-        [field, fold, scratch((2, 3, 2 * north_groups, 64, 256), BF)]
-        + [scratch((4, 64 * north_groups + 8, 256), F32)],
+        [sec_shape, shape((256, 512), BF), shape((16, 512), BF), shape((256, 256), BF)],
+        [field, fold, scratch((2, 2 * north_groups, 64, 256), BF)]
+        + [scratch((2, 3, 32 * (pairs - SPLIT) + 8, 256), F32)],
         scalars=1,
         flops=2 * 64 * (pairs - SPLIT) * 256 * 4608,
         aliases={9: 0},
@@ -443,7 +427,9 @@
         [
             field,
             fold,
-            scratch((2, 3, 2 * groups * EDGE, 256), F32),
+            scratch((2, 2 * groups, 2 * EDGE, 256), BF),
+            scratch((3, 2 * pairs * EDGE + 8, 256), F32),
+            scratch((2, 2, pairs // 2 * LINE + 8, 128), F32),
             scratch((pairs * LINE + 8, 128), F32),
             scratch((2, 64, 128), F32),
             scratch((2, rows, cols), F32),

time: 21.1 us -> 19.8 us (0.938)
  Pallas kernels: 11.5 us -> 10.2 us
    pallas_call x4, Pallas kernels: 11.5 us -> 10.2 us  [call(): pl.pallas_call(fn, out_shape=outs, in_specs=specs, out_specs=[vmem] * len...]
where the time goes in v3:
time: 19.8 us; the launch traced here: 19.5 us
  Pallas kernels  10.2 us (52%)
  starting transfers between devices  9.06 us (46%)
    pallas_call x4, Pallas kernels, call(): pl.pallas_call(fn, out_shape=outs, in_specs=specs, out_specs=[vmem] * len...  10.2 us
    ppermute x1, starting transfers between devices, step(): far = lax.ppermute(own, 'lon', mirror)  6.07 us
    ppermute x1, starting transfers between devices, step(): near_a = lax.ppermute(both, 'lon', pairs_a)  2.32 us
    ppermute x1, starting transfers between devices, step(): near_b = lax.ppermute(both, 'lon', pairs_b)  0.66 us
  transfers between devices with their start and end apart: 3, of which 0 were waited for; matrix products, arithmetic and copies ran while one was open for 0% of the time, Pallas kernels for 27%

profile of v3, /device:TPU:0, one launch (start us, length us, event | category | flops | bytes accessed | tf_op | source)
XLA Modules:
  0.0 19.5 jit_solution(9835306663708855005)
XLA Ops:
  0.0 0.8 %shard_map.109.own_ref = bf16[2,32,128]{2,1,0:T(8,128)(2,1)S(1)} custom-call(bf16[2,32,128]{2,1,0:T(8,128)(2,1)} %bitcast.14, s32[32,128]{1,0:T(8,128)} %bitcast.16), custom_call_target="tpu_custom_call" | custom-call | bytes 1048576 | tf_op jit(solution)/shard_map/pallas_call | solution.py:352
  0.8 6.1 %collective-permute-start = (bf16[2,32,128]{2,1,0:T(8,128)(2,1)S(1)}, bf16[2,32,128]{2,1,0:T(8,128)(2,1)S(1)}, u32[]{:S(2)}, u32[]{:S(2)}) collective-permute-start(bf16[2,32,128]{2,1,0:T(8,128)(2,1)S(1)} %shard_map.109.own_ref), channel_id=1, source_target_pairs={{0,14},{2,12},{4,10},{6,8},{8,6},{10,4},{12,2},{14,0},{1,15},{3,13... | collective-permute-start | bytes 49160 | tf_op jit(solution)/shard_map/ppermute | solution.py:389
  6.8 0.0 copy-start
  6.8 0.0 copy-start.3
  6.8 0.0 copy-start.5
  6.8 0.0 copy-start.6
  6.8 0.0 copy-start.8
  6.9 0.0 copy-start.9
  6.9 2.6 %shard_map.110 = (f32[1304,256]{1,0:T(8,128)S(1)}, bf16[4,5,16,128]{3,2,1,0:T(8,128)(2,1)S(1)}) custom-call(bf16[2,32,128]{2,1,0:T(8,128)(2,1)S(1)} %shard_map.109.own_ref, bf16[5,5,2,128]{3,2,1,0:T(2,128)(2,1)} %w1_hbm.1, f32[1,128]{1,0:T(1,128)} %bitcast.18, bf16[5,5,64,128]{3,2,1,0:T(8,128)(2,1)} %bitcast.11, f32[1,64]{1,0:T(1,128)} %bitcast.21), custom_call_target="tpu_custom_call" | custom-call | flops 1207959552 | bytes 1048576 | tf_op jit(solution)/shard_map/pallas_call | solution.py:352
  9.5 0.0 collective-permute-done.far_ref
  9.5 0.7 %collective-permute-start.2 = (bf16[2,40,128]{2,1,0:T(8,128)(2,1)S(1)}, bf16[2,40,128]{2,1,0:T(8,128)(2,1)S(1)}, u32[]{:S(2)}, u32[]{:S(2)}) collective-permute-start(bf16[2,40,128]{2,1,0:T(8,128)(2,1)S(1)} %pad_maximum_fusion), channel_id=1, source_target_pairs={{0,0},{14,14},{2,4},{4,2},{6,8},{8,6},{10,12},{12,10},{1,1},{15,15... | collective-permute-start | bytes 61448 | tf_op jit(solution)/shard_map/ppermute | solution.py:411
  10.2 2.3 %collective-permute-start.1 = (bf16[2,40,128]{2,1,0:T(8,128)(2,1)S(1)}, bf16[2,40,128]{2,1,0:T(8,128)(2,1)S(1)}, u32[]{:S(2)}, u32[]{:S(2)}) collective-permute-start(bf16[2,40,128]{2,1,0:T(8,128)(2,1)S(1)} %pad_maximum_fusion), channel_id=1, source_target_pairs={{0,2},{2,0},{4,6},{6,4},{8,10},{10,8},{12,14},{14,12},{1,3},{3,1},... | collective-permute-start | bytes 61448 | tf_op jit(solution)/shard_map/ppermute | solution.py:410
  12.5 0.0 copy-done
  12.5 0.0 copy-done.3
  12.5 0.0 copy-done.5
  12.5 0.0 copy-done.6
  12.5 0.0 copy-done.8
  12.6 0.0 copy-done.9
  12.6 0.0 copy-start.1
  12.6 0.0 copy-start.2
  12.6 0.0 copy-start.4
  12.6 0.0 copy-start.7
  12.6 2.7 %shard_map.111 = (f32[1304,256]{1,0:T(8,128)S(1)}, bf16[256,512]{1,0:T(8,128)(2,1)S(1)}, bf16[16,512]{1,0:T(8,128)(2,1)S(1)}, bf16[256,256]{1,0:T(8,128)(2,1)S(1)}) custom-call(s32[2]{0:T(128)S(1)} %copy-done.3, bf16[2,32,128]{2,1,0:T(8,128)(2,1)S(1)} %shard_map.109.own_ref, ...), custom_call_target="tpu_custom_call", output_to_operand_aliasing={{0}: (9, {})} | custom-call | flops 1509949440 | bytes 1048576 | tf_op jit(solution)/shard_map/pallas_call | solution.py:352
  15.3 0.0 collective-permute-done.2.near_b_ref
  15.3 0.0 collective-permute-done.1.near_a_ref
  15.3 0.0 copy-done.1
  15.3 0.0 copy-done.2
  15.3 0.0 copy-done.4
  15.3 0.0 copy-done.7
  15.4 4.1 %shard_map.112 = (bf16[2,32,128]{2,1,0:T(8,128)(2,1)}, f32[1304,256]{1,0:T(8,128)S(1)}) custom-call(s32[2]{0:T(128)S(1)} %copy-done.3, f32[2]{0:T(128)S(1)} %copy-done.4, bf16[2,32,128]{2,1,0:T(8,128)(2,1)S(1)} %bitcast.15, s32[32,128]{1,0:T(8,128)S(1)} %bitcast.17, bf16[2,32,128]{2,1,0:T(8,128)(2,1)S(1)} %shard_map.109.own_ref, ...), custom_call_target="tpu_custom_call", output_to_operand_aliasing={{1}: (16, {})} | custom-call | flops 603979776 | bytes 1048576 | tf_op jit(solution)/shard_map/pallas_call | solution.py:352
  (2 shorter events, 0.0 us)
Async XLA Ops:
  0.8 8.7 %collective-permute-start = (bf16[2,32,128]{2,1,0:T(8,128)(2,1)S(1)}, bf16[2,32,128]{2,1,0:T(8,128)(2,1)S(1)}, u32[]{:S(2)}, u32[]{:S(2)}) collective-permute-start(bf16[2,32,128]{2,1,0:T(8,128)(2,1)S(1)} %shard_map.109.own_ref), channel_id=1, source_target_pairs={{0,14},{2,12},{4,10},{6,8},{8,6},{10,4},{12,2},{14,0},{1,15},{3,13... | collective-permute-start | bytes 49160 | tf_op jit(solution)/shard_map/ppermute | solution.py:389
  6.8 5.7 %copy-start = (bf16[5,5,128,64]{2,3,1,0:T(8,128)(2,1)S(1)}, bf16[5,5,128,64]{2,3,1,0:T(8,128)(2,1)}, u32[]{:S(2)}) copy-start(bf16[5,5,128,64]{2,3,1,0:T(8,128)(2,1)} %param.16) | copy-start | bytes 1228804
  6.8 5.7 %copy-start.3 = (s32[2]{0:T(128)S(1)}, s32[2]{0:T(128)}, u32[]{:S(2)}) copy-start(s32[2]{0:T(128)} %pivot_ref.3) | copy-start | bytes 28
  6.8 5.7 %copy-start.5 = (f32[128]{0:T(128)S(1)}, f32[128]{0:T(128)}, u32[]{:S(2)}) copy-start(f32[128]{0:T(128)} %param.15) | copy-start | bytes 1540
  6.8 5.7 %copy-start.6 = (f32[64]{0:T(128)S(1)}, f32[64]{0:T(128)}, u32[]{:S(2)}) copy-start(f32[64]{0:T(128)} %param.17) | copy-start | bytes 772
  6.8 5.7 %copy-start.8 = (bf16[3,3,64,32]{2,3,1,0:T(8,128)(2,1)S(1)}, bf16[3,3,64,32]{2,3,1,0:T(8,128)(2,1)}, u32[]{:S(2)}) copy-start(bf16[3,3,64,32]{2,3,1,0:T(8,128)(2,1)} %param.18) | copy-start | bytes 110596
  6.9 5.7 %copy-start.9 = (bf16[3,3,32,2]{2,3,1,0:T(2,128)(2,1)S(1)}, bf16[3,3,32,2]{2,3,1,0:T(2,128)(2,1)}, u32[]{:S(2)}) copy-start(bf16[3,3,32,2]{2,3,1,0:T(2,128)(2,1)} %param.20) | copy-start | bytes 3460
  9.5 5.8 %collective-permute-start.2 = (bf16[2,40,128]{2,1,0:T(8,128)(2,1)S(1)}, bf16[2,40,128]{2,1,0:T(8,128)(2,1)S(1)}, u32[]{:S(2)}, u32[]{:S(2)}) collective-permute-start(bf16[2,40,128]{2,1,0:T(8,128)(2,1)S(1)} %pad_maximum_fusion), channel_id=1, source_target_pairs={{0,0},{14,14},{2,4},{4,2},{6,8},{8,6},{10,12},{12,10},{1,1},{15,15... | collective-permute-start | bytes 61448 | tf_op jit(solution)/shard_map/ppermute | solution.py:411
  10.2 5.1 %collective-permute-start.1 = (bf16[2,40,128]{2,1,0:T(8,128)(2,1)S(1)}, bf16[2,40,128]{2,1,0:T(8,128)(2,1)S(1)}, u32[]{:S(2)}, u32[]{:S(2)}) collective-permute-start(bf16[2,40,128]{2,1,0:T(8,128)(2,1)S(1)} %pad_maximum_fusion), channel_id=1, source_target_pairs={{0,2},{2,0},{4,6},{6,4},{8,10},{10,8},{12,14},{14,12},{1,3},{3,1},... | collective-permute-start | bytes 61448 | tf_op jit(solution)/shard_map/ppermute | solution.py:410
  12.6 2.8 %copy-start.1 = (bf16[2,1,32,128]{3,2,1,0:T(8,128)(2,1)S(1)}, bf16[2,1,32,128]{3,2,1,0:T(8,128)(2,1)}, u32[]{:S(2)}) copy-start(bf16[2,1,32,128]{3,2,1,0:T(8,128)(2,1)} %param.11) | copy-start | bytes 49156
  12.6 2.8 %copy-start.2 = (s32[1,32,128]{2,1,0:T(8,128)S(1)}, s32[1,32,128]{2,1,0:T(8,128)}, u32[]{:S(2)}) copy-start(s32[1,32,128]{2,1,0:T(8,128)} %param.12) | copy-start | bytes 49156
  12.6 2.7 %copy-start.4 = (f32[2]{0:T(128)S(1)}, f32[2]{0:T(128)}, u32[]{:S(2)}) copy-start(f32[2]{0:T(128)} %b4_ref.1) | copy-start | bytes 28
  12.6 2.7 %copy-start.7 = (f32[32]{0:T(128)S(1)}, f32[32]{0:T(128)}, u32[]{:S(2)}) copy-start(f32[32]{0:T(128)} %param.19) | copy-start | bytes 388

commit v4 on v3

--- a/solution.py
+++ b/solution.py
@@ -109,18 +109,44 @@
     return rows
 
 
-def mask_body(vel_hbm, land_hbm, own_ref, vel_ref, land_ref, sems):
-    copies = [
-        pltpu.make_async_copy(vel_hbm, vel_ref, sems.at[0]),
-        pltpu.make_async_copy(land_hbm, land_ref, sems.at[1]),
-    ]
+def edge_tile(values, blocks):
+    lane = iota(values[0].shape, 1) >> 4
+    tile = jnp.zeros(values[0].shape, F32)
+    for value, block in zip(values, blocks):
+        tile = jnp.where(lane == block, roll_lanes(value, 8 + 16 * block), tile)
+    return tile
+
+
+def mask_body(
+    vel_hbm, land_hbm, w1_hbm, b1_hbm, b2_hbm, own_ref, pay_ref, w1_ref, b1_ref, b2_ref,
+    vel_ref, land_ref, sems,
+):
+    moves = [(vel_hbm, vel_ref), (land_hbm, land_ref)]
+    moves += [(w1_hbm, w1_ref), (b1_hbm, b1_ref), (b2_hbm, b2_ref)]
+    copies = [pltpu.make_async_copy(a, b, sems.at[k]) for k, (a, b) in enumerate(moves)]
     for copy in copies:
         copy.start()
-    for copy in copies:
+    for copy in copies[:2]:
         copy.wait()
     land = land_ref[...].astype(F32)
-    for c in range(2):
-        own_ref[c] = (vel_ref[c].astype(F32) * land).astype(BF)
+    own = [vel_ref[c].astype(F32) * land for c in range(2)]
+    for c in range(2):
+        own_ref[c] = own[c].astype(BF)
+    rows = land.shape[0]
+    tiles = [own[c][rows - 8 :] for c in range(2)]
+    cuts = [own[c][k : k + 8] for c in range(2) for k in range(0, rows, 8)]
+    tiles.append(edge_tile(cuts, range(len(cuts))))
+    pay_ref[...] = jnp.concatenate(tiles, axis=0).astype(BF)
+    for copy in copies[2:]:
+        copy.wait()
+
+
+def pair_body(pay_ref, far_ref, both_ref):
+    far = far_ref[...].astype(F32)
+    half = far.shape[1] // 32
+    tile = edge_tile([far[0:8], far[8:16]], (half - 1, 2 * half - 1))
+    own = pay_ref[...].astype(F32)[16:24]
+    both_ref[...] = jnp.concatenate([own, tile], axis=0).astype(BF)
 
 
 def pack_first(w1_ref, wide_ref, w1_out):
@@ -185,24 +211,18 @@
 
 
 def south_body(
-    own_ref, w1_hbm, b1_hbm, w2_hbm, b2_hbm, sec, w1_out, field, f, acc, wide, w1_ref, b1_ref,
-    w2_ref, b2_ref, sems,
+    own_ref, w1_ref, b1_ref, w2_hbm, b2_ref, sec, w1_out, field, f, acc, wide, w2_ref, sem
 ):
-    moves = [(w1_hbm, w1_ref), (b1_hbm, b1_ref), (w2_hbm, w2_ref), (b2_hbm, b2_ref)]
-    copies = [pltpu.make_async_copy(a, b, sems.at[k]) for k, (a, b) in enumerate(moves)]
-    for copy in copies:
-        copy.start()
+    copy = pltpu.make_async_copy(w2_hbm, w2_ref, sem)
+    copy.start()
+    pack_first(w1_ref, wide, w1_out)
     rows = own_ref.shape[1]
     cols = own_ref.shape[2]
     load_field(field, [own_ref[c].astype(F32) for c in range(2)])
     pick, _ = inner_picks(cols)
     lefts = left_sides(field, None, None, 0, pick, None, range(SPLIT // 2 + 1), rows)
-    copies[0].wait()
-    pack_first(w1_ref, wide, w1_out)
-    copies[1].wait()
     first_layer(lefts, f, w1_out, jnp.concatenate([b1_ref[...]] * 2, axis=1))
-    copies[2].wait()
-    copies[3].wait()
+    copy.wait()
     bias2 = jnp.concatenate([b2_ref[...]] * 4, axis=1)
     inner_second(f, second_weights(w2_ref), bias2, acc, sec, 0, SPLIT)
 
@@ -225,7 +245,8 @@
     want = 2 * (src & 127) + (src >> 7)
     sel_out[...] = (iota((256, 256), 1) == want).astype(BF)
     load_field(field, [own_ref[c].astype(F32) for c in range(2)])
-    load_fold(fold, [far_ref[c, rows - 8 :].astype(F32) for c in range(2)])
+    far = far_ref[...].astype(F32)
+    load_fold(fold, [far[8 * c : 8 * c + 8] for c in range(2)])
     pick, pick_fold = inner_picks(cols)
     groups = range(SPLIT // 2, (rows + 8) // 4)
     lefts = left_sides(field, fold, pivot_ref, lon_count * cols, pick, pick_fold, groups, rows)
@@ -235,7 +256,7 @@
 
 
 def last_body(
-    pivot_ref, b4_ref, vel_ref, land_ref, own_ref, far_ref, near_a_ref, near_b_ref,
+    pivot_ref, b4_ref, vel_ref, land_ref, own_ref, pay_ref, far_ref, near_a_ref, near_b_ref,
     w1_ref, b1_ref, w2_ref, b2_ref, w3_ref, b3_ref, w4_ref, sel_ref, sec_in,
     out_ref, sec, field, fold, f, acc, acc3, third, spill, tend, *, lon_count,
 ):
@@ -251,21 +272,34 @@
     even = lax.rem(lon, 2) == 0
     own = own_ref[...].astype(F32)
     far = far_ref[...].astype(F32)
-    wrap = jnp.concatenate([far, own[:, rows - 8 :]], axis=1)
+    wrap = jnp.concatenate([far[16:24], pay_ref[...].astype(F32)[16:24]], axis=0)
     near_a = near_a_ref[...].astype(F32)
     near_b = near_b_ref[...].astype(F32)
     west = jnp.where(lon == 0, wrap, jnp.where(even, near_b, near_a))
     east = jnp.where(lon == lon_count - 1, wrap, jnp.where(even, near_a, near_b))
-
-    def around(mid, after, before):
-        lane = iota(mid.shape, 1)
-        half, quarter = cols // 2, cols // 4
-        moved = jnp.where(lane < quarter, after, roll_lanes(mid, half))
-        moved = jnp.where((lane >= quarter) & (lane < half), roll_lanes(before, half), moved)
-        return jnp.where(lane >= half + quarter, mid, moved)
-
-    load_field(field, [around(own[c], east[c, :rows], west[c, :rows]) for c in range(2)])
-    load_fold(fold, [around(far[c, rows - 8 :], west[c, rows:], east[c, rows:]) for c in range(2)])
+    lane = iota((8, cols), 1)
+    half = cols // 2
+
+    def around(mid, after, before, block):
+        outer = jnp.where(
+            lane < half // 2,
+            roll_lanes(after, -16 * block - 8),
+            roll_lanes(before, half - 8 - 16 * block),
+        )
+        inner = jnp.where(lane < half + half // 2, roll_lanes(mid, half), mid)
+        return jnp.where(lane < half, outer, inner)
+
+    wide = []
+    tails = []
+    for c in range(2):
+        parts = []
+        for k in range(rows // 8):
+            block = c * (rows // 8) + k
+            parts.append(around(own[c, 8 * k : 8 * k + 8], east[0:8], west[0:8], block))
+        wide.append(jnp.concatenate(parts, axis=0))
+        tails.append(around(far[8 * c : 8 * c + 8], west[8:16], east[8:16], block))
+    load_field(field, wide)
+    load_fold(fold, tails)
     slot = iota((2 * EDGE, cols), 0)
     lane = iota((2 * EDGE, cols), 1)
     low = slot < EDGE
@@ -374,19 +408,25 @@
     shape = jax.ShapeDtypeStruct
     scratch = pltpu.VMEM
     sems = pltpu.SemaphoreType.DMA
-    (own,) = call(
+    own, pay, w1, b1, b2 = call(
         mask_body,
-        [vel, land],
-        [shape(vel.shape, BF)],
-        [scratch(vel.shape, BF), scratch(land.shape, jnp.int32), sems((2,))],
-        far_ins=(0, 1),
+        [vel, land, w1, b1, b2],
+        [shape(vel.shape, BF), shape((24, cols), BF)]
+        + [shape(x.shape, x.dtype) for x in (w1, b1, b2)],
+        [scratch(vel.shape, BF), scratch(land.shape, jnp.int32), sems((5,))],
+        far_ins=(0, 1, 2, 3, 4),
     )
     mirror = [(i, n - 1 - i) for i in range(n)]
     pairs_a = [(i, i ^ 1) for i in range(n)]
-    pairs_b = [(0, 0), (n - 1, n - 1)]
-    for k in range(1, n // 2):
-        pairs_b += [(2 * k - 1, 2 * k), (2 * k, 2 * k - 1)]
-    far = lax.ppermute(own, "lon", mirror)
+    levels = lax.axis_size("lev")
+    pairs_b = []
+    for level in range(levels):
+        for k in range(1, n // 2):
+            low, high = (2 * k - 1) * levels + level, 2 * k * levels + level
+            pairs_b += [(low, high), (high, low)]
+        for end in (0, n - 1):
+            pairs_b.append((end * levels + level, end * levels + (level + 1) % levels))
+    far = lax.ppermute(pay, "lon", mirror)
     groups = (rows + 8) // 4
     pairs = (rows + 4) // 2
     sec_shape = shape((pairs * LINE + 8, 256), F32)
@@ -401,14 +441,13 @@
         [sec_shape, shape(packed, BF)],
         [field, scratch((2, 2 * south_groups, 64, 256), BF)]
         + [scratch((2, 3, 32 * SPLIT + 8, 256), F32), scratch(packed, F32)]
-        + [scratch(x.shape, x.dtype) for x in (w1, b1, w2, b2)]
-        + [sems((4,))],
+        + [scratch(w2.shape, BF), sems(())],
         flops=2 * 64 * SPLIT * 256 * 4608,
-        far_ins=(1, 2, 3, 4),
-    )
-    both = jnp.concatenate([own, far[:, rows - 8 :]], axis=1)
+        far_ins=(3,),
+    )
+    (both,) = call(pair_body, [pay, far], [shape((16, cols), BF)], [])
     near_a = lax.ppermute(both, "lon", pairs_a)
-    near_b = lax.ppermute(both, "lon", pairs_b)
+    near_b = lax.ppermute(both, ("lon", "lev"), pairs_b)
     sec, w3_wide, w4_wide, sel = call(
         functools.partial(north_body, lon_count=n),
         [fold_pivot, own, far, w1_wide, b1, w2, b2, w3, w4, sec],
@@ -421,7 +460,7 @@
     )
     out, _ = call(
         functools.partial(last_body, lon_count=n),
-        [fold_pivot, b4, vel, land, own, far, near_a, near_b]
+        [fold_pivot, b4, vel, land, own, pay, far, near_a, near_b]
         + [w1_wide, b1, w2, b2, w3_wide, b3, w4_wide, sel, sec],
         [shape((2, rows, cols), BF), sec_shape],
         [
@@ -436,7 +475,7 @@
         ],
         scalars=2,
         flops=2 * 64 * pairs * 256 * 1024,
-        aliases={16: 1},
+        aliases={17: 1},
     )
     return out.reshape(velocity.shape)
 

time: 19.8 us -> 18.1 us (0.914)
  starting transfers between devices: 9.06 us -> 7.08 us
  Pallas kernels: 10.2 us -> 10.6 us
    ppermute x1, starting transfers between devices: 2.32 us -> 1 us  [step(): near_a = lax.ppermute(both, 'lon', pairs_a)]
    ppermute x2, starting transfers between devices: 6.73 us -> 6.08 us  [the longest x1 6.07 us: step(): far = lax.ppermute(pay, 'lon', mirror)]
    pallas_call x4 -> x5, Pallas kernels: 10.2 us -> 10.6 us  [call(): pl.pallas_call(fn, out_shape=outs, in_specs=specs, out_specs=[vmem] * len...]
  transfers between devices with their start and end apart: 3 -> 3, of which waited for: 0 -> 0; matrix products, arithmetic and copies ran while one was open for 0% -> 0% of each run, Pallas kernels for 27% -> 31%
where the time goes in v4:
time: 18.1 us; the launch traced here: 17.8 us
  Pallas kernels  10.6 us (59%)
  starting transfers between devices  7.08 us (39%)
    pallas_call x5, Pallas kernels, call(): pl.pallas_call(fn, out_shape=outs, in_specs=specs, out_specs=[vmem] * len...  10.6 us
    ppermute x1, starting transfers between devices, step(): far = lax.ppermute(pay, 'lon', mirror)  6.07 us
    ppermute x1, starting transfers between devices, step(): near_a = lax.ppermute(both, 'lon', pairs_a)  1 us
  transfers between devices with their start and end apart: 3, of which 0 were waited for; matrix products, arithmetic and copies ran while one was open for 0% of the time, Pallas kernels for 31%

profile of v4, /device:TPU:0, one launch (start us, length us, event | category | flops | bytes accessed | tf_op | source)
XLA Modules:
  0.0 17.8 jit_solution(18216196619350583774)
XLA Ops:
  0.0 0.9 %shard_map.109 = (bf16[2,32,128]{2,1,0:T(8,128)(2,1)S(1)}, bf16[24,128]{1,0:T(8,128)(2,1)S(1)}, bf16[5,5,2,128]{3,2,1,0:T(2,128)(2,1)S(1)}, f32[1,128]{1,0:T(1,128)S(1)}, f32[1,64]{1,0:T(1,128)S(1)}) custom-call(bf16[2,32,128]{2,1,0:T(8,128)(2,1)} %bitcast.14, s32[32,128]{1,0:T(8,128)} %bitcast.16, bf16[5,5,2,128]{3,2,1,0:T(2,128)(2,1)} %w1_hbm.1, ...), custom_call_target="tpu_custom_call" | custom-call | bytes 1048576 | tf_op jit(solution)/shard_map/pallas_call | solution.py:386
  0.9 6.1 %collective-permute-start = (bf16[24,128]{1,0:T(8,128)(2,1)S(1)}, bf16[24,128]{1,0:T(8,128)(2,1)S(1)}, u32[]{:S(2)}, u32[]{:S(2)}) collective-permute-start(bf16[24,128]{1,0:T(8,128)(2,1)S(1)} %get-tuple-element.18.pay_ref), channel_id=1, source_target_pairs={{0,14},{2,12},{4,10},{6,8},{8,6},{10,4},{12,2},{14,0},{1,15},{3,13... | collective-permute-start | bytes 18440 | tf_op jit(solution)/shard_map/ppermute | solution.py:429
  6.9 0.0 copy-start
  6.9 0.0 copy-start.3
  6.9 0.0 copy-start.6
  6.9 0.0 copy-start.7
  7.0 2.9 %shard_map.111 = (f32[1304,256]{1,0:T(8,128)S(1)}, bf16[4,5,16,128]{3,2,1,0:T(8,128)(2,1)S(1)}) custom-call(bf16[2,32,128]{2,1,0:T(8,128)(2,1)S(1)} %get-tuple-element.17.own_ref, bf16[5,5,2,128]{3,2,1,0:T(2,128)(2,1)S(1)} %get-tuple-element.19.w1_ref, f32[1,128]{1,0:T(1,128)S(1)} %get-tuple-element.20.b1_ref, bf16[5,5,64,128]{3,2,1,0:T(8,128)(2,1)} %bitcast.11, ...), custom_call_target="tpu_custom_call" | custom-call | flops 1207959552 | bytes 1048576 | tf_op jit(solution)/shard_map/pallas_call | solution.py:386
  9.8 0.0 collective-permute-done.far_ref
  9.8 0.1 shard_map.110
  9.9 0.0 collective-permute-start.2
  9.9 1.0 %collective-permute-start.1 = (bf16[16,128]{1,0:T(8,128)(2,1)S(1)}, bf16[16,128]{1,0:T(8,128)(2,1)S(1)}, u32[]{:S(2)}, u32[]{:S(2)}) collective-permute-start(bf16[16,128]{1,0:T(8,128)(2,1)S(1)} %shard_map.110), channel_id=1, source_target_pairs={{0,2},{2,0},{4,6},{6,4},{8,10},{10,8},{12,14},{14,12},{1,3},{3,1},... | collective-permute-start | bytes 12296 | tf_op jit(solution)/shard_map/ppermute | solution.py:449
  10.9 0.0 copy-done
  10.9 0.0 copy-done.3
  10.9 0.0 copy-done.6
  10.9 0.0 copy-done.7
  10.9 0.0 copy-start.1
  11.0 0.0 copy-start.2
  11.0 0.0 copy-start.4
  11.0 0.0 copy-start.5
  11.0 2.7 %shard_map.112 = (f32[1304,256]{1,0:T(8,128)S(1)}, bf16[256,512]{1,0:T(8,128)(2,1)S(1)}, bf16[16,512]{1,0:T(8,128)(2,1)S(1)}, bf16[256,256]{1,0:T(8,128)(2,1)S(1)}) custom-call(s32[2]{0:T(128)S(1)} %copy-done.3, bf16[2,32,128]{2,1,0:T(8,128)(2,1)S(1)} %get-tuple-element.17.own_ref, ...), custom_call_target="tpu_custom_call", output_to_operand_aliasing={{0}: (9, {})} | custom-call | flops 1509949440 | bytes 1048576 | tf_op jit(solution)/shard_map/pallas_call | solution.py:386
  13.7 0.0 collective-permute-done.2.near_b_ref
  13.7 0.0 collective-permute-done.1.near_a_ref
  13.7 0.0 copy-done.1
  13.7 0.0 copy-done.2
  13.7 0.0 copy-done.4
  13.7 0.0 copy-done.5
  13.7 4.1 %shard_map.113 = (bf16[2,32,128]{2,1,0:T(8,128)(2,1)}, f32[1304,256]{1,0:T(8,128)S(1)}) custom-call(s32[2]{0:T(128)S(1)} %copy-done.3, f32[2]{0:T(128)S(1)} %copy-done.4, bf16[2,32,128]{2,1,0:T(8,128)(2,1)S(1)} %bitcast.15, s32[32,128]{1,0:T(8,128)S(1)} %bitcast.17, ...), custom_call_target="tpu_custom_call", output_to_operand_aliasing={{1}: (17, {})} | custom-call | flops 603979776 | bytes 1048576 | tf_op jit(solution)/shard_map/pallas_call | solution.py:386
Async XLA Ops:
  0.9 9.0 %collective-permute-start = (bf16[24,128]{1,0:T(8,128)(2,1)S(1)}, bf16[24,128]{1,0:T(8,128)(2,1)S(1)}, u32[]{:S(2)}, u32[]{:S(2)}) collective-permute-start(bf16[24,128]{1,0:T(8,128)(2,1)S(1)} %get-tuple-element.18.pay_ref), channel_id=1, source_target_pairs={{0,14},{2,12},{4,10},{6,8},{8,6},{10,4},{12,2},{14,0},{1,15},{3,13... | collective-permute-start | bytes 18440 | tf_op jit(solution)/shard_map/ppermute | solution.py:429
  6.9 4.0 %copy-start = (bf16[5,5,128,64]{2,3,1,0:T(8,128)(2,1)S(1)}, bf16[5,5,128,64]{2,3,1,0:T(8,128)(2,1)}, u32[]{:S(2)}) copy-start(bf16[5,5,128,64]{2,3,1,0:T(8,128)(2,1)} %param.16) | copy-start | bytes 1228804
  6.9 4.0 %copy-start.3 = (s32[2]{0:T(128)S(1)}, s32[2]{0:T(128)}, u32[]{:S(2)}) copy-start(s32[2]{0:T(128)} %pivot_ref.3) | copy-start | bytes 28
  6.9 4.0 %copy-start.6 = (bf16[3,3,64,32]{2,3,1,0:T(8,128)(2,1)S(1)}, bf16[3,3,64,32]{2,3,1,0:T(8,128)(2,1)}, u32[]{:S(2)}) copy-start(bf16[3,3,64,32]{2,3,1,0:T(8,128)(2,1)} %param.18) | copy-start | bytes 110596
  6.9 4.0 %copy-start.7 = (bf16[3,3,32,2]{2,3,1,0:T(2,128)(2,1)S(1)}, bf16[3,3,32,2]{2,3,1,0:T(2,128)(2,1)}, u32[]{:S(2)}) copy-start(bf16[3,3,32,2]{2,3,1,0:T(2,128)(2,1)} %param.20) | copy-start | bytes 3460
  9.9 3.8 %collective-permute-start.2 = (bf16[16,128]{1,0:T(8,128)(2,1)S(1)}, bf16[16,128]{1,0:T(8,128)(2,1)S(1)}, u32[]{:S(2)}, u32[]{:S(2)}) collective-permute-start(bf16[16,128]{1,0:T(8,128)(2,1)S(1)} %shard_map.110), channel_id=1, source_target_pairs={{2,4},{4,2},{6,8},{8,6},{10,12},{12,10},{0,1},{14,15},{3,5},{5,3},... | collective-permute-start | bytes 12296 | tf_op jit(solution)/shard_map/ppermute | solution.py:450
  9.9 3.8 %collective-permute-start.1 = (bf16[16,128]{1,0:T(8,128)(2,1)S(1)}, bf16[16,128]{1,0:T(8,128)(2,1)S(1)}, u32[]{:S(2)}, u32[]{:S(2)}) collective-permute-start(bf16[16,128]{1,0:T(8,128)(2,1)S(1)} %shard_map.110), channel_id=1, source_target_pairs={{0,2},{2,0},{4,6},{6,4},{8,10},{10,8},{12,14},{14,12},{1,3},{3,1},... | collective-permute-start | bytes 12296 | tf_op jit(solution)/shard_map/ppermute | solution.py:449
  10.9 2.8 %copy-start.1 = (bf16[2,1,32,128]{3,2,1,0:T(8,128)(2,1)S(1)}, bf16[2,1,32,128]{3,2,1,0:T(8,128)(2,1)}, u32[]{:S(2)}) copy-start(bf16[2,1,32,128]{3,2,1,0:T(8,128)(2,1)} %param.11) | copy-start | bytes 49156
  11.0 2.7 %copy-start.2 = (s32[1,32,128]{2,1,0:T(8,128)S(1)}, s32[1,32,128]{2,1,0:T(8,128)}, u32[]{:S(2)}) copy-start(s32[1,32,128]{2,1,0:T(8,128)} %param.12) | copy-start | bytes 49156
  11.0 2.7 %copy-start.4 = (f32[2]{0:T(128)S(1)}, f32[2]{0:T(128)}, u32[]{:S(2)}) copy-start(f32[2]{0:T(128)} %b4_ref.1) | copy-start | bytes 28
  11.0 2.7 %copy-start.5 = (f32[32]{0:T(128)S(1)}, f32[32]{0:T(128)}, u32[]{:S(2)}) copy-start(f32[32]{0:T(128)} %param.19) | copy-start | bytes 388

commit v5 on v4

--- a/solution.py
+++ b/solution.py
@@ -10,8 +10,8 @@
 BF = jnp.bfloat16
 F32 = jnp.float32
 EDGE = 8
-LINE = 72
-SPLIT = 8
+LINE = 80
+SPLIT = 6
 
 
 def dot(a, b):
@@ -67,7 +67,10 @@
     for g in groups:
         part = dot_nt(pick, patches(field_ref, 4 * g, lambda x, t, c: roll_lanes(x, -t)))
         if 4 * g + 8 > rows + 6:
-            ups = [pivot_ref[c] - (wide - 1) > 0 for c in range(2)]
+            ups = [
+                jnp.broadcast_to(pivot_ref[:, c : c + 1], (8, pick.shape[1])) > wide - 1
+                for c in range(2)
+            ]
 
             def turned(x, t, c):
                 return jnp.where(ups[c], roll_lanes(x, t - 1), roll_lanes(x, t + 1))
@@ -117,12 +120,12 @@
     return tile
 
 
-def mask_body(
-    vel_hbm, land_hbm, w1_hbm, b1_hbm, b2_hbm, own_ref, pay_ref, w1_ref, b1_ref, b2_ref,
-    vel_ref, land_ref, sems,
-):
+def mask_body(*refs, small):
+    vel_hbm, land_hbm = refs[:2]
+    own_ref, pay_ref = refs[2 + small : 4 + small]
+    vel_ref, land_ref, sems = refs[4 + 2 * small :]
     moves = [(vel_hbm, vel_ref), (land_hbm, land_ref)]
-    moves += [(w1_hbm, w1_ref), (b1_hbm, b1_ref), (b2_hbm, b2_ref)]
+    moves += list(zip(refs[2 : 2 + small], refs[4 + small : 4 + 2 * small]))
     copies = [pltpu.make_async_copy(a, b, sems.at[k]) for k, (a, b) in enumerate(moves)]
     for copy in copies:
         copy.start()
@@ -154,21 +157,23 @@
     for t in range(5):
         for a in range(5):
             value = w1_ref[a, t].astype(F32)
-            for row in range(4):
-                for c in range(2):
-                    at = 8 * c + row + a
-                    wide_ref[row, t, at : at + 1, :] = value[c : c + 1]
-    w1_out[...] = wide_ref[...].astype(BF)
-
-
-def first_layer(lefts, f_ref, w1_ref, bias):
+            for c in range(2):
+                wide_ref[t, c, a : a + 1, :] = value[c : c + 1]
+    for t in range(5):
+        base = [wide_ref[t, c] for c in range(2)]
+        for row in range(4):
+            both = [pltpu.roll(x, row, axis=0) if row else x for x in base]
+            w1_out[row, t] = jnp.concatenate(both, axis=0).astype(BF)
+
+
+def first_layer(lefts, f_ref, w1_ref, bias, start=0):
     stacked = jnp.concatenate(lefts, axis=0).astype(BF)
     size = lefts[0].shape[0]
     for row in range(4):
         res = dot(stacked, first_weights(w1_ref, row))
         res = jnp.maximum(res + bias, 0.0).astype(BF)
         for g in range(len(lefts)):
-            f_ref[row % 2, 2 * g + row // 2] = res[size * g : size * g + size]
+            f_ref[row % 2, 2 * (start + g) + row // 2] = res[size * g : size * g + size]
 
 
 def second_layer(f_ref, right, acc_ref, lo, count):
@@ -197,10 +202,10 @@
     chunks = acc_ref.shape[0]
     step = count // chunks
     for k in range(chunks):
-        second_layer(f_ref, right, acc_ref.at[k], k * step, step)
+        second_layer(f_ref, right, acc_ref.at[k], start + k * step, step)
         for p in range(step):
             at = (start + k * step + p) * LINE
-            sec_ref[at : at + 64, :] = shifted_sum(acc_ref.at[k], 64 * p, 64, bias)
+            sec_ref[at : at + 64, :] = shifted_sum(acc_ref.at[k], 64 * p, 64, bias).astype(BF)
 
 
 def inner_picks(cols):
@@ -211,7 +216,7 @@
 
 
 def south_body(
-    own_ref, w1_ref, b1_ref, w2_hbm, b2_ref, sec, w1_out, field, f, acc, wide, w2_ref, sem
+    own_ref, w1_ref, b1_ref, w2_hbm, b2_ref, sec, w1_out, f, field, acc, wide, w2_ref, sem
 ):
     copy = pltpu.make_async_copy(w2_hbm, w2_ref, sem)
     copy.start()
@@ -220,7 +225,7 @@
     cols = own_ref.shape[2]
     load_field(field, [own_ref[c].astype(F32) for c in range(2)])
     pick, _ = inner_picks(cols)
-    lefts = left_sides(field, None, None, 0, pick, None, range(SPLIT // 2 + 1), rows)
+    lefts = left_sides(field, None, None, 0, pick, None, range((rows - 2) // 4 + 1), rows)
     first_layer(lefts, f, w1_out, jnp.concatenate([b1_ref[...]] * 2, axis=1))
     copy.wait()
     bias2 = jnp.concatenate([b2_ref[...]] * 4, axis=1)
@@ -229,7 +234,7 @@
 
 def north_body(
     pivot_ref, own_ref, far_ref, w1_ref, b1_ref, w2_ref, b2_ref, w3_ref, w4_ref, sec_in,
-    sec, w3_out, w4_out, sel_out, field, fold, f, acc, *, lon_count,
+    f_in, sec, w3_out, w4_out, sel_out, f, field, fold, acc, *, lon_count,
 ):
     bias1 = jnp.concatenate([b1_ref[...]] * 2, axis=1)
     bias2 = jnp.concatenate([b2_ref[...]] * 4, axis=1)
@@ -248,15 +253,15 @@
     far = far_ref[...].astype(F32)
     load_fold(fold, [far[8 * c : 8 * c + 8] for c in range(2)])
     pick, pick_fold = inner_picks(cols)
-    groups = range(SPLIT // 2, (rows + 8) // 4)
+    groups = range((rows - 2) // 4 + 1, (rows + 8) // 4)
     lefts = left_sides(field, fold, pivot_ref, lon_count * cols, pick, pick_fold, groups, rows)
-    first_layer(lefts, f, w1_ref, bias1)
+    first_layer(lefts, f, w1_ref, bias1, groups[0])
     count = (rows + 4) // 2 - SPLIT
     inner_second(f, second_weights(w2_ref), bias2, acc, sec, SPLIT, count)
 
 
 def last_body(
-    pivot_ref, b4_ref, vel_ref, land_ref, own_ref, pay_ref, far_ref, near_a_ref, near_b_ref,
+    pivot_ref, lon_ref, b4_ref, vel_ref, land_ref, own_ref, pay_ref, far_ref, near_a_ref, near_b_ref,
     w1_ref, b1_ref, w2_ref, b2_ref, w3_ref, b3_ref, w4_ref, sel_ref, sec_in,
     out_ref, sec, field, fold, f, acc, acc3, third, spill, tend, *, lon_count,
 ):
@@ -268,8 +273,8 @@
     groups = (rows + 8) // 4
     pairs = (rows + 4) // 2
 
-    lon = lax.axis_index("lon")
-    even = lax.rem(lon, 2) == 0
+    lon = jnp.broadcast_to(lon_ref[...], (16, cols))
+    even = (lon & 1) == 0
     own = own_ref[...].astype(F32)
     far = far_ref[...].astype(F32)
     wrap = jnp.concatenate([far[16:24], pay_ref[...].astype(F32)[16:24]], axis=0)
@@ -313,25 +318,29 @@
     )
     first_layer(lefts, f, w1_ref, bias1)
     second_layer(f, second_weights(w2_ref), acc, 0, pairs)
-    line = iota((EDGE, 256), 0)
+    line = iota((2 * EDGE, 256), 0)
     for k in range(pairs):
         at = k * LINE
-        new = shifted_sum(acc, 2 * EDGE * k, EDGE, bias2)
-        sec[at : at + 8, :] = jnp.where(line < 4, new, sec_in[at : at + 8, :])
-        new = pltpu.roll(shifted_sum(acc, 2 * EDGE * k + EDGE, EDGE, bias2), 6, axis=0)
-        sec[at + 56 : at + 64, :] = jnp.where(line >= 6, new, sec_in[at + 56 : at + 64, :])
-        sec[at + 64 : at + 72, :] = new
+        new = shifted_sum(acc, 2 * EDGE * k, 2 * EDGE, bias2)
+        old = sec_in[at : at + 16, :].astype(F32)
+        sec[at : at + 16, :] = jnp.where(line < 4, new, old).astype(BF)
+        new = pltpu.roll(new, 6, axis=0)
+        old = sec_in[at + 48 : at + 64, :].astype(F32)
+        sec[at + 48 : at + 64, :] = jnp.where(line >= 14, new, old).astype(BF)
+        sec[at + 64 : at + 80, :] = new.astype(BF)
 
     pairs3 = pairs - 1
     right = w3_ref[...]
     middle = (pairs3 + 1) // 2
     for part, (lo, hi) in enumerate(((0, middle), (middle, pairs3))):
         base, size = lo * LINE, (hi - lo) * LINE
-        left = [sec[base + at : base + at + size, :].astype(BF) for at in (0, LINE)]
+        left = [sec[base + at : base + at + size, :] for at in (0, LINE)]
         res = dot_nt(jnp.concatenate(left, axis=1), right)
         for shift in range(2):
             acc3[part, shift, 0:size, :] = res[:, 128 * shift : 128 * shift + 128]
-        third[base : base + size, :] = shifted_sum(acc3.at[part], 0, size, bias3)
+        for shift in range(2):
+            value = shifted_sum(acc3.at[part], shift, size, bias3)
+            third[shift, base : base + size, :] = value.astype(BF)
 
     pairs4 = pairs - 2
     right = w4_ref[...]
@@ -341,12 +350,13 @@
             [
                 jnp.concatenate(
                     [
-                        third[k * LINE + at : k * LINE + at + 64, :]
-                        for k in range(lo, lo + pairs4 // 2)
+                        third[shift, k * LINE : k * LINE + 64, :]
+                        for k in range(lo + up, lo + up + pairs4 // 2)
                     ],
                     axis=0,
-                ).astype(BF)
-                for at in (0, 1, LINE, LINE + 1)
+                )
+                for up in range(2)
+                for shift in range(2)
             ],
             axis=1,
         )
@@ -370,15 +380,15 @@
                 ]
     land = land_ref[...].astype(F32)
     for c in range(2):
-        total = vel_ref[c].astype(F32) + (tend[c] + b4_ref[c])
+        bias4 = jnp.broadcast_to(b4_ref[:, c : c + 1], (1, cols))
+        total = vel_ref[c].astype(F32) + (tend[c] + bias4)
         out_ref[c] = (land * total).astype(BF)
 
 
-def call(fn, ins, outs, scratch, scalars=0, flops=0, aliases=None, far_ins=()):
+def call(fn, ins, outs, scratch, flops=0, aliases=None, far_ins=()):
     vmem = pl.BlockSpec(memory_space=pltpu.VMEM)
-    smem = pl.BlockSpec(memory_space=pltpu.SMEM)
     hbm = pl.BlockSpec(memory_space=pltpu.HBM)
-    specs = [smem] * scalars + [vmem] * (len(ins) - scalars)
+    specs = [vmem] * len(ins)
     ins = list(ins)
     for k in far_ins:
         specs[k] = hbm
@@ -401,20 +411,21 @@
     rows = velocity.shape[2]
     cols = velocity.shape[3]
     n = lax.axis_size("lon")
+    lon = jnp.full((1, 1), lax.axis_index("lon"), jnp.int32)
     vel = velocity.reshape(2, rows, cols)
     land = land_sea.reshape(rows, cols)
     w2, w3, w4 = (jnp.swapaxes(w, 2, 3) for w in (w2, w3, w4))
-    b1, b2, b3 = b1[None], b2[None], b3[None]
+    b1, b2, b3, b4, fold_pivot = (x[None] for x in (b1, b2, b3, b4, fold_pivot))
     shape = jax.ShapeDtypeStruct
     scratch = pltpu.VMEM
     sems = pltpu.SemaphoreType.DMA
-    own, pay, w1, b1, b2 = call(
-        mask_body,
-        [vel, land, w1, b1, b2],
-        [shape(vel.shape, BF), shape((24, cols), BF)]
-        + [shape(x.shape, x.dtype) for x in (w1, b1, b2)],
-        [scratch(vel.shape, BF), scratch(land.shape, jnp.int32), sems((5,))],
-        far_ins=(0, 1, 2, 3, 4),
+    near = [w1, b1, b2, b3, b4, fold_pivot]
+    own, pay, w1, b1, b2, b3, b4, fold_pivot = call(
+        functools.partial(mask_body, small=len(near)),
+        [vel, land] + near,
+        [shape(vel.shape, BF), shape((24, cols), BF)] + [shape(x.shape, x.dtype) for x in near],
+        [scratch(vel.shape, BF), scratch(land.shape, jnp.int32), sems((2 + len(near),))],
+        far_ins=range(2 + len(near)),
     )
     mirror = [(i, n - 1 - i) for i in range(n)]
     pairs_a = [(i, i ^ 1) for i in range(n)]
@@ -429,18 +440,17 @@
     far = lax.ppermute(pay, "lon", mirror)
     groups = (rows + 8) // 4
     pairs = (rows + 4) // 2
-    sec_shape = shape((pairs * LINE + 8, 256), F32)
-    south_groups = SPLIT // 2 + 1
-    north_groups = groups - SPLIT // 2
+    sec_shape = shape((pairs * LINE, 256), BF)
+    f_shape = shape((2, 2 * groups, 64, 256), BF)
     packed = (4, 5, 16, w1.shape[3])
     field = scratch((2, rows + 16, cols), F32)
     fold = scratch((2, 16, cols), F32)
-    sec, w1_wide = call(
+    sec, w1_wide, f = call(
         south_body,
         [own, w1, b1, w2, b2],
-        [sec_shape, shape(packed, BF)],
-        [field, scratch((2, 2 * south_groups, 64, 256), BF)]
-        + [scratch((2, 3, 32 * SPLIT + 8, 256), F32), scratch(packed, F32)]
+        [sec_shape, shape(packed, BF), f_shape],
+        [field, scratch((1, 3, 64 * SPLIT + 8, 256), F32)]
+        + [scratch((5, 2, 8, w1.shape[3]), F32)]
         + [scratch(w2.shape, BF), sems(())],
         flops=2 * 64 * SPLIT * 256 * 4608,
         far_ins=(3,),
@@ -448,19 +458,17 @@
     (both,) = call(pair_body, [pay, far], [shape((16, cols), BF)], [])
     near_a = lax.ppermute(both, "lon", pairs_a)
     near_b = lax.ppermute(both, ("lon", "lev"), pairs_b)
-    sec, w3_wide, w4_wide, sel = call(
+    sec, w3_wide, w4_wide, sel, _ = call(
         functools.partial(north_body, lon_count=n),
-        [fold_pivot, own, far, w1_wide, b1, w2, b2, w3, w4, sec],
-        [sec_shape, shape((256, 512), BF), shape((16, 512), BF), shape((256, 256), BF)],
-        [field, fold, scratch((2, 2 * north_groups, 64, 256), BF)]
-        + [scratch((2, 3, 32 * (pairs - SPLIT) + 8, 256), F32)],
-        scalars=1,
+        [fold_pivot, own, far, w1_wide, b1, w2, b2, w3, w4, sec, f],
+        [sec_shape, shape((256, 512), BF), shape((16, 512), BF), shape((256, 256), BF), f_shape],
+        [field, fold, scratch((1, 3, 64 * (pairs - SPLIT) + 8, 256), F32)],
         flops=2 * 64 * (pairs - SPLIT) * 256 * 4608,
-        aliases={9: 0},
+        aliases={9: 0, 10: 4},
     )
     out, _ = call(
         functools.partial(last_body, lon_count=n),
-        [fold_pivot, b4, vel, land, own, pay, far, near_a, near_b]
+        [fold_pivot, lon, b4, vel, land, own, pay, far, near_a, near_b]
         + [w1_wide, b1, w2, b2, w3_wide, b3, w4_wide, sel, sec],
         [shape((2, rows, cols), BF), sec_shape],
         [
@@ -468,14 +476,13 @@
             fold,
             scratch((2, 2 * groups, 2 * EDGE, 256), BF),
             scratch((3, 2 * pairs * EDGE + 8, 256), F32),
-            scratch((2, 2, pairs // 2 * LINE + 8, 128), F32),
-            scratch((pairs * LINE + 8, 128), F32),
+            scratch((2, 2, pairs // 2 * LINE + 16, 128), F32),
+            scratch((2, pairs * LINE, 128), BF),
             scratch((2, 64, 128), F32),
             scratch((2, rows, cols), F32),
         ],
-        scalars=2,
         flops=2 * 64 * pairs * 256 * 1024,
-        aliases={17: 1},
+        aliases={18: 1},
     )
     return out.reshape(velocity.shape)
 

time: 18.1 us -> 17.4 us (0.961)
  the two profiles are of different devices: /device:TPU:0 before, /device:TPU:24 now
where the time goes in v5:
time: 17.4 us; the launch traced here: 17.1 us
  Pallas kernels  9.61 us (55%)
  waiting for transfers between devices  4.72 us (27%)
  starting transfers between devices  2.71 us (16%)
    pallas_call x5, Pallas kernels, call(): pl.pallas_call(fn, out_shape=outs, in_specs=specs, out_specs=[vmem] * len...  9.61 us
    ppermute x1, waiting for transfers between devices, step(): far = lax.ppermute(pay, 'lon', mirror)  2.72 us
    ppermute x1, waiting for transfers between devices, step(): near_b = lax.ppermute(both, ('lon', 'lev'), pairs_b)  2 us
    ppermute x1, starting transfers between devices, step(): near_a = lax.ppermute(both, 'lon', pairs_a)  1.49 us
    ppermute x1, starting transfers between devices, step(): far = lax.ppermute(pay, 'lon', mirror)  1.21 us
  transfers between devices with their start and end apart: 3, of which 2 were waited for; matrix products, arithmetic and copies ran while one was open for 0% of the time, Pallas kernels for 29%

profile of v5, /device:TPU:24, one launch (start us, length us, event | category | flops | bytes accessed | tf_op | source)
XLA Modules:
  0.0 17.1 jit_solution(6319758217924356628)
XLA Ops:
  0.0 0.9 %shard_map.109 = (bf16[2,32,128]{2,1,0:T(8,128)(2,1)S(1)}, bf16[24,128]{1,0:T(8,128)(2,1)S(1)}, bf16[5,5,2,128]{3,2,1,0:T(2,128)(2,1)S(1)}, f32[1,128]{1,0:T(1,1...) custom-call(bf16[2,32,128]{2,1,0:T(8,128)(2,1)} %bitcast.14, ...), custom_call_target="tpu_custom_call" | custom-call | bytes 1048576 | tf_op jit(solution)/shard_map/pallas_call | solution.py:396
  0.9 1.2 %collective-permute-start = (bf16[24,128]{1,0:T(8,128)(2,1)S(1)}, bf16[24,128]{1,0:T(8,128)(2,1)S(1)}, u32[]{:S(2)}, u32[]{:S(2)}) collective-permute-start(bf16[24,128]{1,0:T(8,128)(2,1)S(1)} %get-tuple-element.24.pay_ref), channel_id=1, source_target_pairs={{0,14},{2,12},{4,10},{6,8},{8,6},{10,4},{12,2},{14,0},{1,15},{3,13... | collective-permute-start | bytes 18440 | tf_op jit(solution)/shard_map/ppermute | solution.py:440
  2.1 0.0 copy-start.2
  2.1 0.0 copy-start.3
  2.1 0.0 copy-start.4
  2.1 2.4 %shard_map.111 = (bf16[1440,256]{1,0:T(8,128)(2,1)S(1)}, bf16[4,5,16,128]{3,2,1,0:T(8,128)(2,1)S(1)}, bf16[2,20,64,256]{3,2,1,0:T(8,128)(2,1)S(1)}) custom-call(bf16[2,32,128]{2,1,0:T(8,128)(2,1)S(1)} %get-tuple-element.23.own_ref, bf16[5,5,2,128]{3,2,1,0:T(2,128)(2,1)S(1)} %get-tuple-element.25.w1_ref, f32[1,128]{1,0:T(1,128)S(1)} %get-tuple-element.26.b1_ref, ...), custom_call_target="tpu_custom_call" | custom-call | flops 905969664 | bytes 1048576 | tf_op jit(solution)/shard_map/pallas_call | solution.py:396
  4.6 2.7 %collective-permute-done.far_ref = bf16[24,128]{1,0:T(8,128)(2,1)S(1)} collective-permute-done((bf16[24,128]{1,0:T(8,128)(2,1)S(1)}, bf16[24,128]{1,0:T(8,128)(2,1)S(1)}, u32[]{:S(2)}, u32[]{:S(2)}) %collective-permute-start) | collective-permute-done | bytes 6176 | tf_op jit(solution)/shard_map/ppermute | solution.py:440
  7.3 0.1 shard_map.110
  7.4 1.5 %collective-permute-start.1 = (bf16[16,128]{1,0:T(8,128)(2,1)S(1)}, bf16[16,128]{1,0:T(8,128)(2,1)S(1)}, u32[]{:S(2)}, u32[]{:S(2)}) collective-permute-start(bf16[16,128]{1,0:T(8,128)(2,1)S(1)} %shard_map.110), channel_id=1, source_target_pairs={{0,2},{2,0},{4,6},{6,4},{8,10},{10,8},{12,14},{14,12},{1,3},{3,1},... | collective-permute-start | bytes 12296 | tf_op jit(solution)/shard_map/ppermute | solution.py:459
  8.9 0.0 collective-permute-start.2
  8.9 0.0 copy-done.2
  8.9 0.0 copy-done.3
  8.9 0.0 copy-done.4
  8.9 0.0 copy-start
  8.9 0.0 copy-start.1
  8.9 2.4 %shard_map.112 = (bf16[1440,256]{1,0:T(8,128)(2,1)S(1)}, bf16[256,512]{1,0:T(8,128)(2,1)S(1)}, bf16[16,512]{1,0:T(8,128)(2,1)S(1)}, bf16[256,256]{1,0:T(8,128)(2,1)S(1)}, bf16[2,20,64,256]{3,2,1,0:T(8,128)(2,1)S(1)}) custom-call(s32[1,2]{1,0:T(1,128)S(1)} %get-tuple-element.21.pivot_ref, ...), custom_call_target="tpu_custom_call", output_to_operand_aliasing={{0}: (9, {}), {4}: (10, {})} | custom-call | flops 1811939328 | bytes 1048576 | tf_op jit(solution)/shard_map/pallas_call | solution.py:396
  11.4 0.0 collective-permute-done.1.near_a_ref
  11.4 2.0 %collective-permute-done.2.near_b_ref = bf16[16,128]{1,0:T(8,128)(2,1)S(1)} collective-permute-done((bf16[16,128]{1,0:T(8,128)(2,1)S(1)}, bf16[16,128]{1,0:T(8,128)(2,1)S(1)}, u32[]{:S(2)}, u32[]{:S(2)}) %collective-permute-start.2) | collective-permute-done | bytes 4128 | tf_op jit(solution)/shard_map/ppermute | solution.py:460
  13.4 0.0 copy-done
  13.4 0.0 copy-done.1
  13.4 3.8 %shard_map.113 = (bf16[2,32,128]{2,1,0:T(8,128)(2,1)}, bf16[1440,256]{1,0:T(8,128)(2,1)S(1)}) custom-call(s32[1,2]{1,0:T(1,128)S(1)} %get-tuple-element.21.pivot_ref, s32[1,1]{1,0:T(1,128)} %bitcast.7.lon_ref, f32[1,2]{1,0:T(1,128)S(1)} %get-tuple-element.22.b4_ref, bf16[2,32,128]{2,1,0:T(8,128)(2,1)S(1)} %bitcast.15, ...), custom_call_target="tpu_custom_call", output_to_operand_aliasing={{1}: (18, {})} | custom-call | flops 603979776 | bytes 1048576 | tf_op jit(solution)/shard_map/pallas_call | solution.py:396
Async XLA Ops:
  0.9 6.4 %collective-permute-start = (bf16[24,128]{1,0:T(8,128)(2,1)S(1)}, bf16[24,128]{1,0:T(8,128)(2,1)S(1)}, u32[]{:S(2)}, u32[]{:S(2)}) collective-permute-start(bf16[24,128]{1,0:T(8,128)(2,1)S(1)} %get-tuple-element.24.pay_ref), channel_id=1, source_target_pairs={{0,14},{2,12},{4,10},{6,8},{8,6},{10,4},{12,2},{14,0},{1,15},{3,13... | collective-permute-start | bytes 18440 | tf_op jit(solution)/shard_map/ppermute | solution.py:440
  2.1 6.7 %copy-start.2 = (bf16[5,5,128,64]{2,3,1,0:T(8,128)(2,1)S(1)}, bf16[5,5,128,64]{2,3,1,0:T(8,128)(2,1)}, u32[]{:S(2)}) copy-start(bf16[5,5,128,64]{2,3,1,0:T(8,128)(2,1)} %param.16) | copy-start | bytes 1228804
  2.1 6.7 %copy-start.3 = (bf16[3,3,64,32]{2,3,1,0:T(8,128)(2,1)S(1)}, bf16[3,3,64,32]{2,3,1,0:T(8,128)(2,1)}, u32[]{:S(2)}) copy-start(bf16[3,3,64,32]{2,3,1,0:T(8,128)(2,1)} %param.18) | copy-start | bytes 110596
  2.1 6.8 %copy-start.4 = (bf16[3,3,32,2]{2,3,1,0:T(2,128)(2,1)S(1)}, bf16[3,3,32,2]{2,3,1,0:T(2,128)(2,1)}, u32[]{:S(2)}) copy-start(bf16[3,3,32,2]{2,3,1,0:T(2,128)(2,1)} %param.20) | copy-start | bytes 3460
  7.4 4.0 %collective-permute-start.1 = (bf16[16,128]{1,0:T(8,128)(2,1)S(1)}, bf16[16,128]{1,0:T(8,128)(2,1)S(1)}, u32[]{:S(2)}, u32[]{:S(2)}) collective-permute-start(bf16[16,128]{1,0:T(8,128)(2,1)S(1)} %shard_map.110), channel_id=1, source_target_pairs={{0,2},{2,0},{4,6},{6,4},{8,10},{10,8},{12,14},{14,12},{1,3},{3,1},... | collective-permute-start | bytes 12296 | tf_op jit(solution)/shard_map/ppermute | solution.py:459
  8.9 4.5 %collective-permute-start.2 = (bf16[16,128]{1,0:T(8,128)(2,1)S(1)}, bf16[16,128]{1,0:T(8,128)(2,1)S(1)}, u32[]{:S(2)}, u32[]{:S(2)}) collective-permute-start(bf16[16,128]{1,0:T(8,128)(2,1)S(1)} %shard_map.110), channel_id=1, source_target_pairs={{2,4},{4,2},{6,8},{8,6},{10,12},{12,10},{0,1},{14,15},{3,5},{5,3},... | collective-permute-start | bytes 12296 | tf_op jit(solution)/shard_map/ppermute | solution.py:460
  8.9 4.5 %copy-start = (bf16[2,1,32,128]{3,2,1,0:T(8,128)(2,1)S(1)}, bf16[2,1,32,128]{3,2,1,0:T(8,128)(2,1)}, u32[]{:S(2)}) copy-start(bf16[2,1,32,128]{3,2,1,0:T(8,128)(2,1)} %param.11) | copy-start | bytes 49156
  8.9 4.5 %copy-start.1 = (s32[1,32,128]{2,1,0:T(8,128)S(1)}, s32[1,32,128]{2,1,0:T(8,128)}, u32[]{:S(2)}) copy-start(s32[1,32,128]{2,1,0:T(8,128)} %param.12) | copy-start | bytes 49156

commit v6 on v5

--- a/solution.py
+++ b/solution.py
@@ -11,7 +11,7 @@
 F32 = jnp.float32
 EDGE = 8
 LINE = 80
-SPLIT = 6
+SPLIT = 10
 
 
 def dot(a, b):
@@ -215,10 +215,8 @@
     return (lane == 2 * slot - 6).astype(BF), (lane == fold).astype(BF)
 
 
-def south_body(
-    own_ref, w1_ref, b1_ref, w2_hbm, b2_ref, sec, w1_out, f, field, acc, wide, w2_ref, sem
-):
-    copy = pltpu.make_async_copy(w2_hbm, w2_ref, sem)
+def local_first(own_ref, w1_ref, b1_ref, w2_hbm, f, w1_out, w2_out, field, wide, sem):
+    copy = pltpu.make_async_copy(w2_hbm, w2_out, sem)
     copy.start()
     pack_first(w1_ref, wide, w1_out)
     rows = own_ref.shape[1]
@@ -228,8 +226,24 @@
     lefts = left_sides(field, None, None, 0, pick, None, range((rows - 2) // 4 + 1), rows)
     first_layer(lefts, f, w1_out, jnp.concatenate([b1_ref[...]] * 2, axis=1))
     copy.wait()
+
+
+def early_body(own_ref, w1_ref, b1_ref, w2_hbm, pay_in, pay, f, w1_out, w2_out, field, wide, sem):
+    @pl.when(lax.axis_index("lon") == 0)
+    def _():
+        local_first(own_ref, w1_ref, b1_ref, w2_hbm, f, w1_out, w2_out, field, wide, sem)
+
+
+def south_body(
+    own_ref, w1_ref, b1_ref, w2_hbm, b2_ref, f_in, w1_in, w2_in, sec, f, w1_out, w2_out,
+    field, acc, wide, sem,
+):
+    @pl.when(lax.axis_index("lon") != 0)
+    def _():
+        local_first(own_ref, w1_ref, b1_ref, w2_hbm, f, w1_out, w2_out, field, wide, sem)
+
     bias2 = jnp.concatenate([b2_ref[...]] * 4, axis=1)
-    inner_second(f, second_weights(w2_ref), bias2, acc, sec, 0, SPLIT)
+    inner_second(f, second_weights(w2_out), bias2, acc, sec, 0, SPLIT)
 
 
 def north_body(
@@ -437,7 +451,6 @@
             pairs_b += [(low, high), (high, low)]
         for end in (0, n - 1):
             pairs_b.append((end * levels + level, end * levels + (level + 1) % levels))
-    far = lax.ppermute(pay, "lon", mirror)
     groups = (rows + 8) // 4
     pairs = (rows + 4) // 2
     sec_shape = shape((pairs * LINE, 256), BF)
@@ -445,15 +458,25 @@
     packed = (4, 5, 16, w1.shape[3])
     field = scratch((2, rows + 16, cols), F32)
     fold = scratch((2, 16, cols), F32)
-    sec, w1_wide, f = call(
+    made = [f_shape, shape(packed, BF), shape(w2.shape, BF)]
+    wide = scratch((5, 2, 8, w1.shape[3]), F32)
+    pay, f, w1_wide, w2_near = call(
+        early_body,
+        [own, w1, b1, w2, pay],
+        [shape(pay.shape, BF)] + made,
+        [field, wide, sems(())],
+        far_ins=(3,),
+        aliases={4: 0},
+    )
+    far = lax.ppermute(pay, "lon", mirror)
+    sec, f, w1_wide, w2 = call(
         south_body,
-        [own, w1, b1, w2, b2],
-        [sec_shape, shape(packed, BF), f_shape],
-        [field, scratch((1, 3, 64 * SPLIT + 8, 256), F32)]
-        + [scratch((5, 2, 8, w1.shape[3]), F32)]
-        + [scratch(w2.shape, BF), sems(())],
+        [own, w1, b1, w2, b2, f, w1_wide, w2_near],
+        [sec_shape] + made,
+        [field, scratch((1, 3, 64 * SPLIT + 8, 256), F32), wide, sems(())],
         flops=2 * 64 * SPLIT * 256 * 4608,
         far_ins=(3,),
+        aliases={5: 1, 6: 2, 7: 3},
     )
     (both,) = call(pair_body, [pay, far], [shape((16, cols), BF)], [])
     near_a = lax.ppermute(both, "lon", pairs_a)

time: 17.4 us -> 17.5 us (level)
  the two profiles are of different devices: /device:TPU:24 before, /device:TPU:6 now
where the time goes in v6:
time: 17.5 us; the launch traced here: 17.2 us
  Pallas kernels  9.36 us (53%)
  starting transfers between devices  5.09 us (29%)
  waiting for transfers between devices  2.68 us (15%)
    pallas_call x6, Pallas kernels, call(): pl.pallas_call(fn, out_shape=outs, in_specs=specs, out_specs=[vmem] * len...  9.36 us
    ppermute x1, starting transfers between devices, step(): far = lax.ppermute(pay, 'lon', mirror)  3.64 us
    ppermute x1, waiting for transfers between devices, step(): near_b = lax.ppermute(both, ('lon', 'lev'), pairs_b)  2.34 us
    ppermute x1, starting transfers between devices, step(): near_a = lax.ppermute(both, 'lon', pairs_a)  1.45 us
  transfers between devices with their start and end apart: 3, of which 2 were waited for; matrix products, arithmetic and copies ran while one was open for 0% of the time, Pallas kernels for 27%

profile of v6, /device:TPU:6, one launch (start us, length us, event | category | flops | bytes accessed | tf_op | source)
XLA Modules:
  0.0 17.2 jit_solution(910842963830917347)
XLA Ops:
  0.0 0.9 %shard_map.109 = (bf16[2,32,128]{2,1,0:T(8,128)(2,1)S(1)}, bf16[24,128]{1,0:T(8,128)(2,1)S(1)}, bf16[5,5,2,128]{3,2,1,0:T(2,128)(2,1)S(1)}, f32[1,128]{1,0:T(1,1...) custom-call(bf16[2,32,128]{2,1,0:T(8,128)(2,1)} %bitcast.14, ...), custom_call_target="tpu_custom_call" | custom-call | bytes 1048576 | tf_op jit(solution)/shard_map/pallas_call | solution.py:410
  0.9 3.6 %collective-permute-start = (bf16[24,128]{1,0:T(8,128)(2,1)S(1)}, bf16[24,128]{1,0:T(8,128)(2,1)S(1)}, u32[]{:S(2)}, u32[]{:S(2)}) collective-permute-start(bf16[24,128]{1,0:T(8,128)(2,1)S(1)} %get-tuple-element.32.pay_ref), channel_id=1, source_target_pairs={{0,14},{2,12},{4,10},{6,8},{8,6},{10,4},{12,2},{14,0},{1,15},{3,13... | collective-permute-start | bytes 18440 | tf_op jit(solution)/shard_map/ppermute | solution.py:471
  4.6 0.0 copy-start.2
  4.6 0.0 copy-start.3
  4.6 2.8 %shard_map.112 = (bf16[1440,256]{1,0:T(8,128)(2,1)S(1)}, bf16[2,20,64,256]{3,2,1,0:T(8,128)(2,1)S(1)}, bf16[4,5,16,128]{3,2,1,0:T(8,128)(2,1)S(1)}, bf16[5,5,64,128]{3,2,1,0:T(8,128)(2,1)S(1)}) custom-call(bf16[2,32,128]{2,1,0:T(8,128)(2,1)S(1)} %get-tuple-element.28.own_ref, ...), custom_call_target="tpu_custom_call", output_to_operand_aliasing={{1}: (5, {}), {2}: (6, {}), {3}: (7, {})} | custom-call | flops 1509949440 | bytes 1048576 | tf_op jit(solution)/shard_map/pallas_call | solution.py:410
  7.4 0.0 collective-permute-done.far_ref
  7.4 0.1 shard_map.111
  7.5 1.5 %collective-permute-start.1 = (bf16[16,128]{1,0:T(8,128)(2,1)S(1)}, bf16[16,128]{1,0:T(8,128)(2,1)S(1)}, u32[]{:S(2)}, u32[]{:S(2)}) collective-permute-start(bf16[16,128]{1,0:T(8,128)(2,1)S(1)} %shard_map.111), channel_id=1, source_target_pairs={{0,2},{2,0},{4,6},{6,4},{8,10},{10,8},{12,14},{14,12},{1,3},{3,1},... | collective-permute-start | bytes 12296 | tf_op jit(solution)/shard_map/ppermute | solution.py:482
  8.9 0.0 collective-permute-start.2
  8.9 0.0 copy-done.2
  8.9 0.0 copy-done.3
  8.9 0.0 copy-start
  9.0 0.0 copy-start.1
  9.0 1.8 %shard_map.113 = (bf16[1440,256]{1,0:T(8,128)(2,1)S(1)}, bf16[256,512]{1,0:T(8,128)(2,1)S(1)}, bf16[16,512]{1,0:T(8,128)(2,1)S(1)}, bf16[256,256]{1,0:T(8,128)(2,1)S(1)}, bf16[2,20,64,256]{3,2,1,0:T(8,128)(2,1)S(1)}) custom-call(s32[1,2]{1,0:T(1,128)S(1)} %get-tuple-element.26.pivot_ref, ...), custom_call_target="tpu_custom_call", output_to_operand_aliasing={{0}: (9, {}), {4}: (10, {})} | custom-call | flops 1207959552 | bytes 1048576 | tf_op jit(solution)/shard_map/pallas_call | solution.py:410
  10.8 0.3 %collective-permute-done.1.near_a_ref = bf16[16,128]{1,0:T(8,128)(2,1)S(1)} collective-permute-done((bf16[16,128]{1,0:T(8,128)(2,1)S(1)}, bf16[16,128]{1,0:T(8,128)(2,1)S(1)}, u32[]{:S(2)}, u32[]{:S(2)}) %collective-permute-start.1) | collective-permute-done | bytes 4128 | tf_op jit(solution)/shard_map/ppermute | solution.py:482
  11.1 2.3 %collective-permute-done.2.near_b_ref = bf16[16,128]{1,0:T(8,128)(2,1)S(1)} collective-permute-done((bf16[16,128]{1,0:T(8,128)(2,1)S(1)}, bf16[16,128]{1,0:T(8,128)(2,1)S(1)}, u32[]{:S(2)}, u32[]{:S(2)}) %collective-permute-start.2) | collective-permute-done | bytes 4128 | tf_op jit(solution)/shard_map/ppermute | solution.py:483
  13.4 0.0 copy-done
  13.4 0.0 copy-done.1
  13.4 3.8 %shard_map.114 = (bf16[2,32,128]{2,1,0:T(8,128)(2,1)}, bf16[1440,256]{1,0:T(8,128)(2,1)S(1)}) custom-call(s32[1,2]{1,0:T(1,128)S(1)} %get-tuple-element.26.pivot_ref, s32[1,1]{1,0:T(1,128)} %bitcast.7.lon_ref, f32[1,2]{1,0:T(1,128)S(1)} %get-tuple-element.27.b4_ref, bf16[2,32,128]{2,1,0:T(8,128)(2,1)S(1)} %bitcast.15, ...), custom_call_target="tpu_custom_call", output_to_operand_aliasing={{1}: (18, {})} | custom-call | flops 603979776 | bytes 1048576 | tf_op jit(solution)/shard_map/pallas_call | solution.py:410
  (1 shorter events, 0.0 us)
Async XLA Ops:
  0.9 6.5 %collective-permute-start = (bf16[24,128]{1,0:T(8,128)(2,1)S(1)}, bf16[24,128]{1,0:T(8,128)(2,1)S(1)}, u32[]{:S(2)}, u32[]{:S(2)}) collective-permute-start(bf16[24,128]{1,0:T(8,128)(2,1)S(1)} %get-tuple-element.32.pay_ref), channel_id=1, source_target_pairs={{0,14},{2,12},{4,10},{6,8},{8,6},{10,4},{12,2},{14,0},{1,15},{3,13... | collective-permute-start | bytes 18440 | tf_op jit(solution)/shard_map/ppermute | solution.py:471
  4.6 4.4 %copy-start.2 = (bf16[3,3,64,32]{2,3,1,0:T(8,128)(2,1)S(1)}, bf16[3,3,64,32]{2,3,1,0:T(8,128)(2,1)}, u32[]{:S(2)}) copy-start(bf16[3,3,64,32]{2,3,1,0:T(8,128)(2,1)} %param.18) | copy-start | bytes 110596
  4.6 4.4 %copy-start.3 = (bf16[3,3,32,2]{2,3,1,0:T(2,128)(2,1)S(1)}, bf16[3,3,32,2]{2,3,1,0:T(2,128)(2,1)}, u32[]{:S(2)}) copy-start(bf16[3,3,32,2]{2,3,1,0:T(2,128)(2,1)} %param.20) | copy-start | bytes 3460
  7.5 3.6 %collective-permute-start.1 = (bf16[16,128]{1,0:T(8,128)(2,1)S(1)}, bf16[16,128]{1,0:T(8,128)(2,1)S(1)}, u32[]{:S(2)}, u32[]{:S(2)}) collective-permute-start(bf16[16,128]{1,0:T(8,128)(2,1)S(1)} %shard_map.111), channel_id=1, source_target_pairs={{0,2},{2,0},{4,6},{6,4},{8,10},{10,8},{12,14},{14,12},{1,3},{3,1},... | collective-permute-start | bytes 12296 | tf_op jit(solution)/shard_map/ppermute | solution.py:482
  8.9 4.5 %collective-permute-start.2 = (bf16[16,128]{1,0:T(8,128)(2,1)S(1)}, bf16[16,128]{1,0:T(8,128)(2,1)S(1)}, u32[]{:S(2)}, u32[]{:S(2)}) collective-permute-start(bf16[16,128]{1,0:T(8,128)(2,1)S(1)} %shard_map.111), channel_id=1, source_target_pairs={{2,4},{4,2},{6,8},{8,6},{10,12},{12,10},{0,1},{14,15},{3,5},{5,3},... | collective-permute-start | bytes 12296 | tf_op jit(solution)/shard_map/ppermute | solution.py:483
  8.9 4.5 %copy-start = (bf16[2,1,32,128]{3,2,1,0:T(8,128)(2,1)S(1)}, bf16[2,1,32,128]{3,2,1,0:T(8,128)(2,1)}, u32[]{:S(2)}) copy-start(bf16[2,1,32,128]{3,2,1,0:T(8,128)(2,1)} %param.11) | copy-start | bytes 49156
  9.0 4.5 %copy-start.1 = (s32[1,32,128]{2,1,0:T(8,128)S(1)}, s32[1,32,128]{2,1,0:T(8,128)}, u32[]{:S(2)}) copy-start(s32[1,32,128]{2,1,0:T(8,128)} %param.12) | copy-start | bytes 49156

commit v7 on v6

--- a/solution.py
+++ b/solution.py
@@ -277,7 +277,7 @@
 def last_body(
     pivot_ref, lon_ref, b4_ref, vel_ref, land_ref, own_ref, pay_ref, far_ref, near_a_ref, near_b_ref,
     w1_ref, b1_ref, w2_ref, b2_ref, w3_ref, b3_ref, w4_ref, sel_ref, sec_in,
-    out_ref, sec, field, fold, f, acc, acc3, third, spill, tend, *, lon_count,
+    out_ref, field, fold, f, acc, strip, accs, acc3, third, spill, tend, *, lon_count,
 ):
     rows = own_ref.shape[1]
     cols = own_ref.shape[2]
@@ -322,7 +322,7 @@
     slot = iota((2 * EDGE, cols), 0)
     lane = iota((2 * EDGE, cols), 1)
     low = slot < EDGE
-    pair = jnp.where(low, slot, slot + (cols // 2 - 2 - EDGE))
+    pair = jnp.where(low, slot, slot + (cols // 2 - 4 - EDGE))
     start = 2 * pair - 6 + jnp.where(low, cols // 2, 0)
     pick = (lane == lax.rem(start + cols, cols)).astype(BF)
     start = cols + 5 - 2 * pair + jnp.where(low, 0, cols // 2)
@@ -332,29 +332,36 @@
     )
     first_layer(lefts, f, w1_ref, bias1)
     second_layer(f, second_weights(w2_ref), acc, 0, pairs)
-    line = iota((2 * EDGE, 256), 0)
-    for k in range(pairs):
-        at = k * LINE
-        new = shifted_sum(acc, 2 * EDGE * k, 2 * EDGE, bias2)
-        old = sec_in[at : at + 16, :].astype(F32)
-        sec[at : at + 16, :] = jnp.where(line < 4, new, old).astype(BF)
-        new = pltpu.roll(new, 6, axis=0)
-        old = sec_in[at + 48 : at + 64, :].astype(F32)
-        sec[at + 48 : at + 64, :] = jnp.where(line >= 14, new, old).astype(BF)
-        sec[at + 64 : at + 80, :] = new.astype(BF)
-
     pairs3 = pairs - 1
     right = w3_ref[...]
     middle = (pairs3 + 1) // 2
     for part, (lo, hi) in enumerate(((0, middle), (middle, pairs3))):
         base, size = lo * LINE, (hi - lo) * LINE
-        left = [sec[base + at : base + at + size, :] for at in (0, LINE)]
+        left = [sec_in[base + at : base + at + size, :] for at in (0, LINE)]
         res = dot_nt(jnp.concatenate(left, axis=1), right)
         for shift in range(2):
             acc3[part, shift, 0:size, :] = res[:, 128 * shift : 128 * shift + 128]
         for shift in range(2):
             value = shifted_sum(acc3.at[part], shift, size, bias3)
             third[shift, base : base + size, :] = value.astype(BF)
+
+    strip[...] = shifted_sum(acc, 0, 2 * EDGE * pairs, bias2).astype(BF)
+    size = 2 * EDGE * pairs3
+    res = dot_nt(jnp.concatenate([strip[0:size], strip[2 * EDGE :]], axis=1), w3_ref[...])
+    for shift in range(2):
+        accs[shift, 0:size, :] = res[:, 128 * shift : 128 * shift + 128]
+    line = iota((2 * EDGE, 128), 0)
+    for shift in range(2):
+        edge = shifted_sum(accs, shift, size, bias3)
+        for k in range(pairs3):
+            new = edge[2 * EDGE * k : 2 * EDGE * k + 2 * EDGE]
+            at = k * LINE
+            old = third[shift, at : at + 16, :].astype(F32)
+            third[shift, at : at + 16, :] = jnp.where(line < 4, new, old).astype(BF)
+            at += 48
+            new = pltpu.roll(new, 4, axis=0)
+            old = third[shift, at : at + 16, :].astype(F32)
+            third[shift, at : at + 16, :] = jnp.where(line >= 12, new, old).astype(BF)
 
     pairs4 = pairs - 2
     right = w4_ref[...]
@@ -489,23 +496,24 @@
         flops=2 * 64 * (pairs - SPLIT) * 256 * 4608,
         aliases={9: 0, 10: 4},
     )
-    out, _ = call(
+    (out,) = call(
         functools.partial(last_body, lon_count=n),
         [fold_pivot, lon, b4, vel, land, own, pay, far, near_a, near_b]
         + [w1_wide, b1, w2, b2, w3_wide, b3, w4_wide, sel, sec],
-        [shape((2, rows, cols), BF), sec_shape],
+        [shape((2, rows, cols), BF)],
         [
             field,
             fold,
             scratch((2, 2 * groups, 2 * EDGE, 256), BF),
             scratch((3, 2 * pairs * EDGE + 8, 256), F32),
+            scratch((2 * pairs * EDGE, 256), BF),
+            scratch((2, 2 * pairs * EDGE + 8, 128), F32),
             scratch((2, 2, pairs // 2 * LINE + 16, 128), F32),
             scratch((2, pairs * LINE, 128), BF),
             scratch((2, 64, 128), F32),
             scratch((2, rows, cols), F32),
         ],
         flops=2 * 64 * pairs * 256 * 1024,
-        aliases={18: 1},
     )
     return out.reshape(velocity.shape)
 

time: 17.5 us -> 16.9 us (0.966)
  Pallas kernels: 9.36 us -> 8.84 us
    pallas_call x6, Pallas kernels: 9.36 us -> 8.84 us  [call(): pl.pallas_call(fn, out_shape=outs, in_specs=specs, out_specs=[vmem] * len...]
where the time goes in v7:
time: 16.9 us; the launch traced here: 16.7 us
  Pallas kernels  8.84 us (52%)
  starting transfers between devices  5.09 us (30%)
  waiting for transfers between devices  2.68 us (16%)
    pallas_call x6, Pallas kernels, call(): pl.pallas_call(fn, out_shape=outs, in_specs=specs, out_specs=[vmem] * len...  8.84 us
    ppermute x1, starting transfers between devices, step(): far = lax.ppermute(pay, 'lon', mirror)  3.64 us
    ppermute x1, waiting for transfers between devices, step(): near_b = lax.ppermute(both, ('lon', 'lev'), pairs_b)  2.34 us
    ppermute x1, starting transfers between devices, step(): near_a = lax.ppermute(both, 'lon', pairs_a)  1.45 us
  transfers between devices with their start and end apart: 3, of which 2 were waited for; matrix products, arithmetic and copies ran while one was open for 0% of the time, Pallas kernels for 27%

profile of v7, /device:TPU:6, one launch (start us, length us, event | category | flops | bytes accessed | tf_op | source)
XLA Modules:
  0.0 16.7 jit_solution(489736057032336628)
XLA Ops:
  0.0 0.9 %shard_map.109 = (bf16[2,32,128]{2,1,0:T(8,128)(2,1)S(1)}, bf16[24,128]{1,0:T(8,128)(2,1)S(1)}, bf16[5,5,2,128]{3,2,1,0:T(2,128)(2,1)S(1)}, f32[1,128]{1,0:T(1,1...) custom-call(bf16[2,32,128]{2,1,0:T(8,128)(2,1)} %bitcast.14, ...), custom_call_target="tpu_custom_call" | custom-call | bytes 1048576 | tf_op jit(solution)/shard_map/pallas_call | solution.py:417
  0.9 3.6 %collective-permute-start = (bf16[24,128]{1,0:T(8,128)(2,1)S(1)}, bf16[24,128]{1,0:T(8,128)(2,1)S(1)}, u32[]{:S(2)}, u32[]{:S(2)}) collective-permute-start(bf16[24,128]{1,0:T(8,128)(2,1)S(1)} %get-tuple-element.31.pay_ref), channel_id=1, source_target_pairs={{0,14},{2,12},{4,10},{6,8},{8,6},{10,4},{12,2},{14,0},{1,15},{3,13... | collective-permute-start | bytes 18440 | tf_op jit(solution)/shard_map/ppermute | solution.py:478
  4.6 0.0 copy-start.2
  4.6 0.0 copy-start.3
  4.6 2.8 %shard_map.112 = (bf16[1440,256]{1,0:T(8,128)(2,1)S(1)}, bf16[2,20,64,256]{3,2,1,0:T(8,128)(2,1)S(1)}, bf16[4,5,16,128]{3,2,1,0:T(8,128)(2,1)S(1)}, bf16[5,5,64,128]{3,2,1,0:T(8,128)(2,1)S(1)}) custom-call(bf16[2,32,128]{2,1,0:T(8,128)(2,1)S(1)} %get-tuple-element.27.own_ref, ...), custom_call_target="tpu_custom_call", output_to_operand_aliasing={{1}: (5, {}), {2}: (6, {}), {3}: (7, {})} | custom-call | flops 1509949440 | bytes 1048576 | tf_op jit(solution)/shard_map/pallas_call | solution.py:417
  7.4 0.0 collective-permute-done.far_ref
  7.4 0.1 shard_map.111
  7.5 1.5 %collective-permute-start.1 = (bf16[16,128]{1,0:T(8,128)(2,1)S(1)}, bf16[16,128]{1,0:T(8,128)(2,1)S(1)}, u32[]{:S(2)}, u32[]{:S(2)}) collective-permute-start(bf16[16,128]{1,0:T(8,128)(2,1)S(1)} %shard_map.111), channel_id=1, source_target_pairs={{0,2},{2,0},{4,6},{6,4},{8,10},{10,8},{12,14},{14,12},{1,3},{3,1},... | collective-permute-start | bytes 12296 | tf_op jit(solution)/shard_map/ppermute | solution.py:489
  8.9 0.0 collective-permute-start.2
  8.9 0.0 copy-done.2
  8.9 0.0 copy-done.3
  8.9 0.0 copy-start
  9.0 0.0 copy-start.1
  9.0 1.8 %shard_map.113 = (bf16[1440,256]{1,0:T(8,128)(2,1)S(1)}, bf16[256,512]{1,0:T(8,128)(2,1)S(1)}, bf16[16,512]{1,0:T(8,128)(2,1)S(1)}, bf16[256,256]{1,0:T(8,128)(2,1)S(1)}, bf16[2,20,64,256]{3,2,1,0:T(8,128)(2,1)S(1)}) custom-call(s32[1,2]{1,0:T(1,128)S(1)} %get-tuple-element.25.pivot_ref, ...), custom_call_target="tpu_custom_call", output_to_operand_aliasing={{0}: (9, {}), {4}: (10, {})} | custom-call | flops 1207959552 | bytes 1048576 | tf_op jit(solution)/shard_map/pallas_call | solution.py:417
  10.8 0.3 %collective-permute-done.1.near_a_ref = bf16[16,128]{1,0:T(8,128)(2,1)S(1)} collective-permute-done((bf16[16,128]{1,0:T(8,128)(2,1)S(1)}, bf16[16,128]{1,0:T(8,128)(2,1)S(1)}, u32[]{:S(2)}, u32[]{:S(2)}) %collective-permute-start.1) | collective-permute-done | bytes 4128 | tf_op jit(solution)/shard_map/ppermute | solution.py:489
  11.1 2.3 %collective-permute-done.2.near_b_ref = bf16[16,128]{1,0:T(8,128)(2,1)S(1)} collective-permute-done((bf16[16,128]{1,0:T(8,128)(2,1)S(1)}, bf16[16,128]{1,0:T(8,128)(2,1)S(1)}, u32[]{:S(2)}, u32[]{:S(2)}) %collective-permute-start.2) | collective-permute-done | bytes 4128 | tf_op jit(solution)/shard_map/ppermute | solution.py:490
  13.4 0.0 copy-done
  13.4 0.0 copy-done.1
  13.4 3.3 %shard_map.114 = bf16[2,32,128]{2,1,0:T(8,128)(2,1)} custom-call(s32[1,2]{1,0:T(1,128)S(1)} %get-tuple-element.25.pivot_ref, s32[1,1]{1,0:T(1,128)} %bitcast.7.lon_ref, f32[1,2]{1,0:T(1,128)S(1)} %get-tuple-element.26.b4_ref, bf16[2,32,128]{2,1,0:T(8,128)(2,1)S(1)} %bitcast.15, s32[32,128]{1,0:T(8,128)S(1)} %bitcast.17, ...), custom_call_target="tpu_custom_call" | custom-call | flops 603979776 | bytes 1048576 | tf_op jit(solution)/shard_map/pallas_call | solution.py:417
  (1 shorter events, 0.0 us)
Async XLA Ops:
  0.9 6.5 %collective-permute-start = (bf16[24,128]{1,0:T(8,128)(2,1)S(1)}, bf16[24,128]{1,0:T(8,128)(2,1)S(1)}, u32[]{:S(2)}, u32[]{:S(2)}) collective-permute-start(bf16[24,128]{1,0:T(8,128)(2,1)S(1)} %get-tuple-element.31.pay_ref), channel_id=1, source_target_pairs={{0,14},{2,12},{4,10},{6,8},{8,6},{10,4},{12,2},{14,0},{1,15},{3,13... | collective-permute-start | bytes 18440 | tf_op jit(solution)/shard_map/ppermute | solution.py:478
  4.6 4.4 %copy-start.2 = (bf16[3,3,64,32]{2,3,1,0:T(8,128)(2,1)S(1)}, bf16[3,3,64,32]{2,3,1,0:T(8,128)(2,1)}, u32[]{:S(2)}) copy-start(bf16[3,3,64,32]{2,3,1,0:T(8,128)(2,1)} %param.18) | copy-start | bytes 110596
  4.6 4.4 %copy-start.3 = (bf16[3,3,32,2]{2,3,1,0:T(2,128)(2,1)S(1)}, bf16[3,3,32,2]{2,3,1,0:T(2,128)(2,1)}, u32[]{:S(2)}) copy-start(bf16[3,3,32,2]{2,3,1,0:T(2,128)(2,1)} %param.20) | copy-start | bytes 3460
  7.5 3.6 %collective-permute-start.1 = (bf16[16,128]{1,0:T(8,128)(2,1)S(1)}, bf16[16,128]{1,0:T(8,128)(2,1)S(1)}, u32[]{:S(2)}, u32[]{:S(2)}) collective-permute-start(bf16[16,128]{1,0:T(8,128)(2,1)S(1)} %shard_map.111), channel_id=1, source_target_pairs={{0,2},{2,0},{4,6},{6,4},{8,10},{10,8},{12,14},{14,12},{1,3},{3,1},... | collective-permute-start | bytes 12296 | tf_op jit(solution)/shard_map/ppermute | solution.py:489
  8.9 4.5 %collective-permute-start.2 = (bf16[16,128]{1,0:T(8,128)(2,1)S(1)}, bf16[16,128]{1,0:T(8,128)(2,1)S(1)}, u32[]{:S(2)}, u32[]{:S(2)}) collective-permute-start(bf16[16,128]{1,0:T(8,128)(2,1)S(1)} %shard_map.111), channel_id=1, source_target_pairs={{2,4},{4,2},{6,8},{8,6},{10,12},{12,10},{0,1},{14,15},{3,5},{5,3},... | collective-permute-start | bytes 12296 | tf_op jit(solution)/shard_map/ppermute | solution.py:490
  8.9 4.5 %copy-start = (bf16[2,1,32,128]{3,2,1,0:T(8,128)(2,1)S(1)}, bf16[2,1,32,128]{3,2,1,0:T(8,128)(2,1)}, u32[]{:S(2)}) copy-start(bf16[2,1,32,128]{3,2,1,0:T(8,128)(2,1)} %param.11) | copy-start | bytes 49156
  9.0 4.5 %copy-start.1 = (s32[1,32,128]{2,1,0:T(8,128)S(1)}, s32[1,32,128]{2,1,0:T(8,128)}, u32[]{:S(2)}) copy-start(s32[1,32,128]{2,1,0:T(8,128)} %param.12) | copy-start | bytes 49156

commit v8 on v7

--- a/solution.py
+++ b/solution.py
@@ -82,17 +82,24 @@
 
 def second_weights(w2_ref):
     zero = jnp.zeros(w2_ref.shape[2:], BF)
-    rows = []
-    for shift in range(3):
-        for dr in range(2):
+
+    def part(places, taps):
+        rows = []
+        for dr, shift in places:
             for dc in range(2):
                 cells = []
-                for a in range(6):
+                for a in taps:
                     for b in (2 * shift - dc, 2 * shift + 1 - dc):
                         inside = 0 <= a - dr < 5 and 0 <= b < 5
                         cells.append(w2_ref[a - dr, b] if inside else zero)
                 rows.append(jnp.concatenate(cells, axis=1))
-    return jnp.concatenate(rows, axis=0)
+        return jnp.concatenate(rows, axis=0)
+
+    return (
+        part(((0, 0), (0, 1)), range(5)),
+        part(((1, 0), (1, 1)), range(1, 6)),
+        part(((0, 2), (1, 2)), range(6)),
+    )
 
 
 def block_weights(w_ref, shifts):
@@ -185,9 +192,13 @@
         ],
         axis=1,
     )
-    res = dot_nt(left, right)
-    for shift in range(3):
-        acc_ref[shift, 0 : count * size, :] = res[:, 256 * shift : 256 * shift + 256]
+    rows = count * size
+    for dr, cut in enumerate((left[:, : 5 * 256], left[:, 256:])):
+        res = dot_nt(cut, right[dr])
+        lanes = slice(128 * dr, 128 * dr + 128)
+        for shift in range(2):
+            acc_ref[shift, 0:rows, lanes] = res[:, 128 * shift : 128 * shift + 128]
+    acc_ref[2, 0:rows, :] = dot_nt(left, right[2])
 
 
 def shifted_sum(acc_ref, at, size, bias):
@@ -334,8 +345,7 @@
     second_layer(f, second_weights(w2_ref), acc, 0, pairs)
     pairs3 = pairs - 1
     right = w3_ref[...]
-    middle = (pairs3 + 1) // 2
-    for part, (lo, hi) in enumerate(((0, middle), (middle, pairs3))):
+    for part, (lo, hi) in enumerate(((0, pairs3),)):
         base, size = lo * LINE, (hi - lo) * LINE
         left = [sec_in[base + at : base + at + size, :] for at in (0, LINE)]
         res = dot_nt(jnp.concatenate(left, axis=1), right)
@@ -350,18 +360,14 @@
     res = dot_nt(jnp.concatenate([strip[0:size], strip[2 * EDGE :]], axis=1), w3_ref[...])
     for shift in range(2):
         accs[shift, 0:size, :] = res[:, 128 * shift : 128 * shift + 128]
-    line = iota((2 * EDGE, 128), 0)
     for shift in range(2):
         edge = shifted_sum(accs, shift, size, bias3)
+        first = edge.astype(BF)
+        last = pltpu.roll(edge, 4, axis=0).astype(BF)
         for k in range(pairs3):
-            new = edge[2 * EDGE * k : 2 * EDGE * k + 2 * EDGE]
             at = k * LINE
-            old = third[shift, at : at + 16, :].astype(F32)
-            third[shift, at : at + 16, :] = jnp.where(line < 4, new, old).astype(BF)
-            at += 48
-            new = pltpu.roll(new, 4, axis=0)
-            old = third[shift, at : at + 16, :].astype(F32)
-            third[shift, at : at + 16, :] = jnp.where(line >= 12, new, old).astype(BF)
+            third[shift, at : at + 4, :] = first[2 * EDGE * k : 2 * EDGE * k + 4]
+            third[shift, at + 60 : at + 64, :] = last[2 * EDGE * k + 12 : 2 * EDGE * k + 16]
 
     pairs4 = pairs - 2
     right = w4_ref[...]
@@ -508,7 +514,7 @@
             scratch((3, 2 * pairs * EDGE + 8, 256), F32),
             scratch((2 * pairs * EDGE, 256), BF),
             scratch((2, 2 * pairs * EDGE + 8, 128), F32),
-            scratch((2, 2, pairs // 2 * LINE + 16, 128), F32),
+            scratch((1, 2, pairs * LINE + 16, 128), F32),
             scratch((2, pairs * LINE, 128), BF),
             scratch((2, 64, 128), F32),
             scratch((2, rows, cols), F32),

time: 16.9 us -> 16.8 us (level)
  Pallas kernels: 8.84 us -> 8.43 us
  waiting for transfers between devices: 2.68 us -> 2.91 us
    pallas_call x6, Pallas kernels: 8.84 us -> 8.43 us  [call(): pl.pallas_call(fn, out_shape=outs, in_specs=specs, out_specs=[vmem] * len...]
  transfers between devices with their start and end apart: 3 -> 3, of which waited for: 2 -> 3; matrix products, arithmetic and copies ran while one was open for 0% -> 0% of each run, Pallas kernels for 27% -> 26%
where the time goes in v8:
time: 16.8 us; the launch traced here: 16.6 us
  Pallas kernels  8.43 us (50%)
  starting transfers between devices  5.18 us (31%)
  waiting for transfers between devices  2.91 us (17%)
    pallas_call x6, Pallas kernels, call(): pl.pallas_call(fn, out_shape=outs, in_specs=specs, out_specs=[vmem] * len...  8.43 us
    ppermute x1, starting transfers between devices, step(): far = lax.ppermute(pay, 'lon', mirror)  3.64 us
    ppermute x1, waiting for transfers between devices, step(): near_b = lax.ppermute(both, ('lon', 'lev'), pairs_b)  2.43 us
    ppermute x1, starting transfers between devices, step(): near_a = lax.ppermute(both, 'lon', pairs_a)  1.53 us
    ppermute x1, waiting for transfers between devices, step(): near_a = lax.ppermute(both, 'lon', pairs_a)  0.37 us
  transfers between devices with their start and end apart: 3, of which 3 were waited for; matrix products, arithmetic and copies ran while one was open for 0% of the time, Pallas kernels for 26%

profile of v8, /device:TPU:6, one launch (start us, length us, event | category | flops | bytes accessed | tf_op | source)
XLA Modules:
  0.0 16.6 jit_solution(14559345444421698556)
XLA Ops:
  0.0 0.9 %shard_map.109 = (bf16[2,32,128]{2,1,0:T(8,128)(2,1)S(1)}, bf16[24,128]{1,0:T(8,128)(2,1)S(1)}, bf16[5,5,2,128]{3,2,1,0:T(2,128)(2,1)S(1)}, f32[1,128]{1,0:T(1,1...) custom-call(bf16[2,32,128]{2,1,0:T(8,128)(2,1)} %bitcast.14, ...), custom_call_target="tpu_custom_call" | custom-call | bytes 1048576 | tf_op jit(solution)/shard_map/pallas_call | solution.py:423
  0.9 3.6 %collective-permute-start = (bf16[24,128]{1,0:T(8,128)(2,1)S(1)}, bf16[24,128]{1,0:T(8,128)(2,1)S(1)}, u32[]{:S(2)}, u32[]{:S(2)}) collective-permute-start(bf16[24,128]{1,0:T(8,128)(2,1)S(1)} %get-tuple-element.31.pay_ref), channel_id=1, source_target_pairs={{0,14},{2,12},{4,10},{6,8},{8,6},{10,4},{12,2},{14,0},{1,15},{3,13... | collective-permute-start | bytes 18440 | tf_op jit(solution)/shard_map/ppermute | solution.py:484
  4.6 0.0 copy-start.2
  4.6 0.0 copy-start.3
  4.6 2.6 %shard_map.112 = (bf16[1440,256]{1,0:T(8,128)(2,1)S(1)}, bf16[2,20,64,256]{3,2,1,0:T(8,128)(2,1)S(1)}, bf16[4,5,16,128]{3,2,1,0:T(8,128)(2,1)S(1)}, bf16[5,5,64,128]{3,2,1,0:T(8,128)(2,1)S(1)}) custom-call(bf16[2,32,128]{2,1,0:T(8,128)(2,1)S(1)} %get-tuple-element.27.own_ref, ...), custom_call_target="tpu_custom_call", output_to_operand_aliasing={{1}: (5, {}), {2}: (6, {}), {3}: (7, {})} | custom-call | flops 1509949440 | bytes 1048576 | tf_op jit(solution)/shard_map/pallas_call | solution.py:423
  7.2 0.1 collective-permute-done.far_ref
  7.3 0.1 shard_map.111
  7.4 1.5 %collective-permute-start.1 = (bf16[16,128]{1,0:T(8,128)(2,1)S(1)}, bf16[16,128]{1,0:T(8,128)(2,1)S(1)}, u32[]{:S(2)}, u32[]{:S(2)}) collective-permute-start(bf16[16,128]{1,0:T(8,128)(2,1)S(1)} %shard_map.111), channel_id=1, source_target_pairs={{0,2},{2,0},{4,6},{6,4},{8,10},{10,8},{12,14},{14,12},{1,3},{3,1},... | collective-permute-start | bytes 12296 | tf_op jit(solution)/shard_map/ppermute | solution.py:495
  8.9 0.0 collective-permute-start.2
  8.9 0.0 copy-done.2
  8.9 0.0 copy-done.3
  8.9 0.0 copy-start
  9.0 0.0 copy-start.1
  9.0 1.7 %shard_map.113 = (bf16[1440,256]{1,0:T(8,128)(2,1)S(1)}, bf16[256,512]{1,0:T(8,128)(2,1)S(1)}, bf16[16,512]{1,0:T(8,128)(2,1)S(1)}, bf16[256,256]{1,0:T(8,128)(2,1)S(1)}, bf16[2,20,64,256]{3,2,1,0:T(8,128)(2,1)S(1)}) custom-call(s32[1,2]{1,0:T(1,128)S(1)} %get-tuple-element.25.pivot_ref, ...), custom_call_target="tpu_custom_call", output_to_operand_aliasing={{0}: (9, {}), {4}: (10, {})} | custom-call | flops 1207959552 | bytes 1048576 | tf_op jit(solution)/shard_map/pallas_call | solution.py:423
  10.6 0.4 %collective-permute-done.1.near_a_ref = bf16[16,128]{1,0:T(8,128)(2,1)S(1)} collective-permute-done((bf16[16,128]{1,0:T(8,128)(2,1)S(1)}, bf16[16,128]{1,0:T(8,128)(2,1)S(1)}, u32[]{:S(2)}, u32[]{:S(2)}) %collective-permute-start.1) | collective-permute-done | bytes 4128 | tf_op jit(solution)/shard_map/ppermute | solution.py:495
  11.0 2.4 %collective-permute-done.2.near_b_ref = bf16[16,128]{1,0:T(8,128)(2,1)S(1)} collective-permute-done((bf16[16,128]{1,0:T(8,128)(2,1)S(1)}, bf16[16,128]{1,0:T(8,128)(2,1)S(1)}, u32[]{:S(2)}, u32[]{:S(2)}) %collective-permute-start.2) | collective-permute-done | bytes 4128 | tf_op jit(solution)/shard_map/ppermute | solution.py:496
  13.4 0.0 copy-done
  13.4 0.0 copy-done.1
  13.4 3.1 %shard_map.114 = bf16[2,32,128]{2,1,0:T(8,128)(2,1)} custom-call(s32[1,2]{1,0:T(1,128)S(1)} %get-tuple-element.25.pivot_ref, s32[1,1]{1,0:T(1,128)} %bitcast.7.lon_ref, f32[1,2]{1,0:T(1,128)S(1)} %get-tuple-element.26.b4_ref, bf16[2,32,128]{2,1,0:T(8,128)(2,1)S(1)} %bitcast.15, s32[32,128]{1,0:T(8,128)S(1)} %bitcast.17, ...), custom_call_target="tpu_custom_call" | custom-call | flops 603979776 | bytes 1048576 | tf_op jit(solution)/shard_map/pallas_call | solution.py:423
  (1 shorter events, 0.0 us)
Async XLA Ops:
  0.9 6.4 %collective-permute-start = (bf16[24,128]{1,0:T(8,128)(2,1)S(1)}, bf16[24,128]{1,0:T(8,128)(2,1)S(1)}, u32[]{:S(2)}, u32[]{:S(2)}) collective-permute-start(bf16[24,128]{1,0:T(8,128)(2,1)S(1)} %get-tuple-element.31.pay_ref), channel_id=1, source_target_pairs={{0,14},{2,12},{4,10},{6,8},{8,6},{10,4},{12,2},{14,0},{1,15},{3,13... | collective-permute-start | bytes 18440 | tf_op jit(solution)/shard_map/ppermute | solution.py:484
  4.6 4.4 %copy-start.2 = (bf16[3,3,64,32]{2,3,1,0:T(8,128)(2,1)S(1)}, bf16[3,3,64,32]{2,3,1,0:T(8,128)(2,1)}, u32[]{:S(2)}) copy-start(bf16[3,3,64,32]{2,3,1,0:T(8,128)(2,1)} %param.18) | copy-start | bytes 110596
  4.6 4.4 %copy-start.3 = (bf16[3,3,32,2]{2,3,1,0:T(2,128)(2,1)S(1)}, bf16[3,3,32,2]{2,3,1,0:T(2,128)(2,1)}, u32[]{:S(2)}) copy-start(bf16[3,3,32,2]{2,3,1,0:T(2,128)(2,1)} %param.20) | copy-start | bytes 3460
  7.4 3.6 %collective-permute-start.1 = (bf16[16,128]{1,0:T(8,128)(2,1)S(1)}, bf16[16,128]{1,0:T(8,128)(2,1)S(1)}, u32[]{:S(2)}, u32[]{:S(2)}) collective-permute-start(bf16[16,128]{1,0:T(8,128)(2,1)S(1)} %shard_map.111), channel_id=1, source_target_pairs={{0,2},{2,0},{4,6},{6,4},{8,10},{10,8},{12,14},{14,12},{1,3},{3,1},... | collective-permute-start | bytes 12296 | tf_op jit(solution)/shard_map/ppermute | solution.py:495
  8.9 4.5 %collective-permute-start.2 = (bf16[16,128]{1,0:T(8,128)(2,1)S(1)}, bf16[16,128]{1,0:T(8,128)(2,1)S(1)}, u32[]{:S(2)}, u32[]{:S(2)}) collective-permute-start(bf16[16,128]{1,0:T(8,128)(2,1)S(1)} %shard_map.111), channel_id=1, source_target_pairs={{2,4},{4,2},{6,8},{8,6},{10,12},{12,10},{0,1},{14,15},{3,5},{5,3},... | collective-permute-start | bytes 12296 | tf_op jit(solution)/shard_map/ppermute | solution.py:496
  8.9 4.5 %copy-start = (bf16[2,1,32,128]{3,2,1,0:T(8,128)(2,1)S(1)}, bf16[2,1,32,128]{3,2,1,0:T(8,128)(2,1)}, u32[]{:S(2)}) copy-start(bf16[2,1,32,128]{3,2,1,0:T(8,128)(2,1)} %param.11) | copy-start | bytes 49156
  9.0 4.5 %copy-start.1 = (s32[1,32,128]{2,1,0:T(8,128)S(1)}, s32[1,32,128]{2,1,0:T(8,128)}, u32[]{:S(2)}) copy-start(s32[1,32,128]{2,1,0:T(8,128)} %param.12) | copy-start | bytes 49156
